TPU v7x, 32 devices: a whole 2x2x4 slice. The times are simulated.
32 devices in a mesh: dp: 16 (over z, x, core), tensor: 2 (over y).
Axes of the slice: x: 2, y: 2, z: 4, core: 2. Of those that a mesh axis runs over, the one named last changes fastest.
Arguments:
- tokens: bfloat16 [2, 4096, 2048], P(None, ('dp', 'tensor')), may hold values from -6 to 6
- segment_ids: int32 [2, 4096], P(None, 'dp'), may hold values from 0 to 2, as said below
- decay_rates: float32 [16], P('tensor'), may hold values from 0.002 to 0.08
- gain_attn: bfloat16 [2048], P('dp'), may hold values from 0.25 to 1.75
- w_query: bfloat16 [2048, 2048], P('dp', 'tensor'), may hold values from -0.125 to 0.125
- w_key: bfloat16 [2048, 2048], P('dp', 'tensor'), may hold values from -0.125 to 0.125
- w_value: bfloat16 [2048, 2048], P('dp', 'tensor'), may hold values from -0.125 to 0.125
- w_gate: bfloat16 [2048, 2048], P('dp', 'tensor'), may hold values from -0.125 to 0.125
- w_out: bfloat16 [2048, 2048], P('tensor', 'dp'), may hold values from -0.125 to 0.125
- gain_ffn: bfloat16 [2048], P('dp'), may hold values from 0.25 to 1.75
- w_left: bfloat16 [2048, 5632], P('dp', 'tensor'), may hold values from -0.125 to 0.125
- w_right: bfloat16 [2048, 5632], P('dp', 'tensor'), may hold values from -0.125 to 0.125
- w_down: bfloat16 [5632, 2048], P('tensor', 'dp'), may hold values from -0.078125 to 0.078125
- cotangent: bfloat16 [2, 4096, 2048], P(None, ('dp', 'tensor')), may hold values from -6 to 6
Outputs:
- output: bfloat16 [2, 4096, 2048], P(None, ('dp', 'tensor'))
- grad_tokens: float32 [2, 4096, 2048], P(None, ('dp', 'tensor'))
- grad_gain_attn: float32 [2048], P('dp')
- grad_w_query: float32 [2048, 2048], P('dp', 'tensor')
- grad_w_key: float32 [2048, 2048], P('dp', 'tensor')
- grad_w_value: float32 [2048, 2048], P('dp', 'tensor')
- grad_w_gate: float32 [2048, 2048], P('dp', 'tensor')
- grad_w_out: float32 [2048, 2048], P('tensor', 'dp')
- grad_gain_ffn: float32 [2048], P('dp')
- grad_w_left: float32 [2048, 5632], P('dp', 'tensor')
- grad_w_right: float32 [2048, 5632], P('dp', 'tensor')
- grad_w_down: float32 [5632, 2048], P('tensor', 'dp')
Inputs may be any that keep to these rules, and one draw needn't show every extreme that they name: `segment_ids`: each micro-batch's 4096 tokens are 16 sequences of 256 tokens; within a sequence the ids never fall and 0, 1 and 2 each mark one document of at least 32 tokens; document 1 holds the sequence's two middle tokens.
All inputs are finite; a program needn't handle non-finite values.
Results may differ from a plain program's by a relative error of at most 0.015.
Values may be sent and summed in bfloat16 or wider, within the bound.
A program may use at most 256 MiB of HBM per device.

v0:
```python
import jax
import jax.numpy as jnp
from jax import lax
from jax.sharding import PartitionSpec as P

EPSILON = 1e-06


def scaled_rows(values):
    inverse = lax.rsqrt(jnp.mean(values * values, axis=-1, keepdims=True) + EPSILON)
    return (values * inverse, inverse)


def times_transposed(former, latter):
    return lax.dot_general(
        former, latter, (((1,), (1,)), ((), ())), preferred_element_type=jnp.float32
    )


def transposed_times(former, latter):
    return lax.dot_general(
        former, latter, (((0,), (0,)), ((), ())), preferred_element_type=jnp.float32
    )


def silu_slope(values):
    sigmoid = jax.nn.sigmoid(values)
    return sigmoid * (1.0 + values * (1.0 - sigmoid))


def norm_backward(grad_normed, unit_rows, inverse, gain_values):
    scaled_grad = grad_normed * gain_values
    return inverse * (
        scaled_grad - unit_rows * jnp.mean(scaled_grad * unit_rows, axis=-1, keepdims=True)
    )


def fetch_attention(gain_attn, joined_in, w_out):
    return (
        lax.all_gather(gain_attn, "dp", axis=0, tiled=True),
        lax.all_gather(joined_in, "dp", axis=0, tiled=True),
        lax.all_gather(w_out, "dp", axis=1, tiled=True),
    )


def fetch_feedforward(gain_ffn, joined_pair, w_down):
    return (
        lax.all_gather(gain_ffn, "dp", axis=0, tiled=True),
        lax.all_gather(joined_pair, "dp", axis=0, tiled=True),
        lax.all_gather(w_down, "dp", axis=1, tiled=True),
    )


def local(
    tokens,
    segment_ids,
    decay_rates,
    gain_attn,
    w_query,
    w_key,
    w_value,
    w_gate,
    w_out,
    gain_ffn,
    w_left,
    w_right,
    w_down,
    cotangent,
):
    batches, local_rows, model_width = tokens.shape
    length = segment_ids.shape[1]
    local_heads = decay_rates.shape[0]
    local_width = w_query.shape[1]
    head_width = local_width // local_heads
    local_units = w_left.shape[1]
    joined_in = jnp.concatenate([w_query, w_key, w_value, w_gate], axis=1)
    joined_pair = jnp.concatenate([w_left, w_right], axis=1)
    places = jnp.arange(length)
    offset = (places[:, None] - places[None, :]).astype(jnp.float32)
    decay_table = jnp.exp(-decay_rates[:, None, None] * jnp.maximum(offset, 0.0)[None])
    total_gain_attn = jnp.zeros((model_width,), jnp.float32)
    total_gain_ffn = jnp.zeros((model_width,), jnp.float32)
    total_in = jnp.zeros((model_width, 4 * local_width), jnp.float32)
    total_out = jnp.zeros((local_width, model_width), jnp.float32)
    total_pair = jnp.zeros((model_width, 2 * local_units), jnp.float32)
    total_down = jnp.zeros((local_units, model_width), jnp.float32)
    outputs = []
    gradients = []
    for micro_batch in range(batches):
        gain_full, weight_in, weight_out = fetch_attention(gain_attn, joined_in, w_out)
        inputs = tokens[micro_batch].astype(jnp.float32)
        unit_attn, inverse_attn = scaled_rows(inputs)
        normed = (unit_attn * gain_full.astype(jnp.float32)).astype(jnp.bfloat16)
        normed_all = lax.all_gather(normed, "tensor", axis=0, tiled=True)
        projected = jnp.dot(normed_all, weight_in, preferred_element_type=jnp.float32)
        query_pre = projected[:, :local_width]
        key_pre = projected[:, local_width : 2 * local_width]
        value_rows = (
            projected[:, 2 * local_width : 3 * local_width]
            .astype(jnp.bfloat16)
            .reshape(length, local_heads, head_width)
        )
        gate_proj = projected[:, 3 * local_width :]
        queries = (
            jax.nn.silu(query_pre).astype(jnp.bfloat16).reshape(length, local_heads, head_width)
        )
        key_rows = (
            jax.nn.silu(key_pre).astype(jnp.bfloat16).reshape(length, local_heads, head_width)
        )
        segments = segment_ids[micro_batch]
        allowed = (offset >= 0.0) & (segments[:, None] == segments[None, :])
        masked = jnp.where(allowed[None], decay_table, 0.0)
        scores = jnp.einsum("ihd,jhd->hij", queries, key_rows, preferred_element_type=jnp.float32)
        weights = (scores * masked).astype(jnp.bfloat16)
        mixed_heads = jnp.einsum(
            "hij,jhd->ihd", weights, value_rows, preferred_element_type=jnp.float32
        ).reshape(length, local_width)
        square_sum = lax.psum(jnp.sum(mixed_heads * mixed_heads, axis=-1), "tensor")
        inverse_mixed = lax.rsqrt(square_sum / model_width + EPSILON)[:, None]
        unit_mixed = mixed_heads * inverse_mixed
        branch = (unit_mixed * gate_proj).astype(jnp.bfloat16)
        middle = inputs + lax.psum_scatter(
            jnp.dot(branch, weight_out, preferred_element_type=jnp.float32),
            "tensor",
            scatter_dimension=0,
            tiled=True,
        )
        gain_ffn_full, weight_pair, weight_down = fetch_feedforward(gain_ffn, joined_pair, w_down)
        unit_ffn, inverse_ffn = scaled_rows(middle)
        normed_ffn = (unit_ffn * gain_ffn_full.astype(jnp.float32)).astype(jnp.bfloat16)
        normed_ffn_all = lax.all_gather(normed_ffn, "tensor", axis=0, tiled=True)
        both_proj = jnp.dot(normed_ffn_all, weight_pair, preferred_element_type=jnp.float32)
        left_proj = both_proj[:, :local_units]
        right_proj = both_proj[:, local_units:]
        joined = (left_proj * right_proj).astype(jnp.bfloat16)
        result = middle + lax.psum_scatter(
            jnp.dot(joined, weight_down, preferred_element_type=jnp.float32).astype(jnp.bfloat16),
            "tensor",
            scatter_dimension=0,
            tiled=True,
        ).astype(jnp.float32)
        outputs.append(result.astype(jnp.bfloat16))
        gain_ffn_full, weight_pair, weight_down = fetch_feedforward(gain_ffn, joined_pair, w_down)
        gain_full, weight_in, weight_out = fetch_attention(gain_attn, joined_in, w_out)
        upstream = cotangent[micro_batch]
        upstream_all = lax.all_gather(upstream, "tensor", axis=0, tiled=True)
        total_down = total_down + transposed_times(joined, upstream_all)
        grad_joined = times_transposed(upstream_all, weight_down)
        grad_left = (grad_joined * right_proj).astype(jnp.bfloat16)
        grad_right = (grad_joined * left_proj).astype(jnp.bfloat16)
        grad_pair = jnp.concatenate([grad_left, grad_right], axis=1)
        total_pair = total_pair + transposed_times(normed_ffn_all, grad_pair)
        grad_normed_ffn = lax.psum_scatter(
            times_transposed(grad_pair, weight_pair), "tensor", scatter_dimension=0, tiled=True
        )
        total_gain_ffn = total_gain_ffn + jnp.sum(grad_normed_ffn * unit_ffn, axis=0)
        grad_middle = upstream.astype(jnp.float32) + norm_backward(
            grad_normed_ffn, unit_ffn, inverse_ffn, gain_ffn_full.astype(jnp.float32)
        )
        grad_attn_out = grad_middle.astype(jnp.bfloat16)
        grad_out_all = lax.all_gather(grad_attn_out, "tensor", axis=0, tiled=True)
        total_out = total_out + transposed_times(branch, grad_out_all)
        grad_branch = times_transposed(grad_out_all, weight_out)
        grad_unit = grad_branch * gate_proj
        grad_gate = (grad_branch * unit_mixed).astype(jnp.bfloat16)
        dot_sum = lax.psum(jnp.sum(grad_unit * unit_mixed, axis=-1), "tensor")
        grad_mixed = (
            (inverse_mixed * (grad_unit - unit_mixed * (dot_sum / model_width)[:, None]))
            .astype(jnp.bfloat16)
            .reshape(length, local_heads, head_width)
        )
        grad_weights = jnp.einsum(
            "ihd,jhd->hij", grad_mixed, value_rows, preferred_element_type=jnp.float32
        )
        grad_scores = (grad_weights * masked).astype(jnp.bfloat16)
        grad_queries = jnp.einsum(
            "hij,jhd->ihd", grad_scores, key_rows, preferred_element_type=jnp.float32
        ).reshape(length, local_width)
        grad_keys = jnp.einsum(
            "hij,ihd->jhd", grad_scores, queries, preferred_element_type=jnp.float32
        ).reshape(length, local_width)
        grad_values = (
            jnp.einsum("hij,ihd->jhd", weights, grad_mixed, preferred_element_type=jnp.float32)
            .reshape(length, local_width)
            .astype(jnp.bfloat16)
        )
        grad_query_pre = (grad_queries * silu_slope(query_pre)).astype(jnp.bfloat16)
        grad_key_pre = (grad_keys * silu_slope(key_pre)).astype(jnp.bfloat16)
        grad_projected = jnp.concatenate(
            [grad_query_pre, grad_key_pre, grad_values, grad_gate], axis=1
        )
        total_in = total_in + transposed_times(normed_all, grad_projected)
        grad_normed = lax.psum_scatter(
            times_transposed(grad_projected, weight_in).astype(jnp.bfloat16),
            "tensor",
            scatter_dimension=0,
            tiled=True,
        ).astype(jnp.float32)
        total_gain_attn = total_gain_attn + jnp.sum(grad_normed * unit_attn, axis=0)
        gradients.append(
            grad_middle
            + norm_backward(grad_normed, unit_attn, inverse_attn, gain_full.astype(jnp.float32))
        )
    summed = (
        lax.psum_scatter(total_gain_attn, "dp", scatter_dimension=0, tiled=True),
        lax.psum_scatter(total_in, "dp", scatter_dimension=0, tiled=True),
        lax.psum_scatter(total_out, "dp", scatter_dimension=1, tiled=True),
        lax.psum_scatter(total_gain_ffn, "dp", scatter_dimension=0, tiled=True),
        lax.psum_scatter(total_pair, "dp", scatter_dimension=0, tiled=True),
        lax.psum_scatter(total_down, "dp", scatter_dimension=1, tiled=True),
    )
    gain_attn_grad, gain_ffn_grad = lax.psum((summed[0], summed[3]), "tensor")
    grad_in = summed[1]
    grad_pair_all = summed[4]
    return (
        jnp.stack(outputs),
        jnp.stack(gradients),
        gain_attn_grad,
        grad_in[:, :local_width],
        grad_in[:, local_width : 2 * local_width],
        grad_in[:, 2 * local_width : 3 * local_width],
        grad_in[:, 3 * local_width :],
        summed[2],
        gain_ffn_grad,
        grad_pair_all[:, :local_units],
        grad_pair_all[:, local_units:],
        summed[5],
    )


def solution(mesh):
    return jax.shard_map(
        local,
        mesh=mesh,
        in_specs=(
            P(None, ("dp", "tensor"), None),
            P(None, "dp"),
            P("tensor"),
            P("dp"),
            P("dp", "tensor"),
            P("dp", "tensor"),
            P("dp", "tensor"),
            P("dp", "tensor"),
            P("tensor", "dp"),
            P("dp"),
            P("dp", "tensor"),
            P("dp", "tensor"),
            P("tensor", "dp"),
            P(None, ("dp", "tensor"), None),
        ),
        out_specs=(
            P(None, ("dp", "tensor"), None),
            P(None, ("dp", "tensor"), None),
            P("dp"),
            P("dp", "tensor"),
            P("dp", "tensor"),
            P("dp", "tensor"),
            P("dp", "tensor"),
            P("tensor", "dp"),
            P("dp"),
            P("dp", "tensor"),
            P("dp", "tensor"),
            P("tensor", "dp"),
        ),
        check_vma=False,
    )
```

profile of v0, /device:TPU:0, one launch (start us, length us, event | category | flops | bytes accessed | tf_op | source)
XLA Modules:
  0.0 2061.7 jit_solution(93691799684135510)
XLA Ops:
  7.3 23.3 %all-gather.2 = bf16[16,1,128]{2,1,0:T(2,128)(2,1)S(1)} all-gather(bf16[1,1,128]{2,1,0:T(2,128)(2,1)} %bitcast.211), channel_id=1, replica_groups=mesh['dp'=16,'tensor'=2] {'dp'}, dimensions={0}, use_global_device_ids=true | all-gather | bytes 4352 | tf_op jit(solution)/shard_map/all_gather | solution.py:40
  32.1 2.5 fusion.21
  37.5 15.9 all-gather.17.cloned.1.call-done
  53.4 129.7 %all-gather.19.cloned.1.call-done = bf16[2048,4096]{1,0:T(8,128)(2,1)} async-done(((bf16[128,4096]{1,0:T(8,128)(2,1)}), bf16[2048,4096]{1,0:T(8,128)(2,1)}) %all-gather.19.cloned.1.call-update) | async-done | bytes 16777232 | tf_op jit(solution)/shard_map/all_gather | solution.py:41
  183.0 8.4 fusion.69
  197.6 7.0 all-gather.29.cloned.1.call-done
  204.7 8.5 fusion.72
  220.3 4.9 all-reduce.5
  226.7 33.2 %all-gather.21.cloned.1.call-done = bf16[1024,2048]{1,0:T(8,128)(2,1)} async-done(((bf16[1024,128]{1,0:T(8,128)(2,1)}), bf16[1024,2048]{1,0:T(8,128)(2,1)}) %all-gather.21.cloned.1.call-update) | async-done | bytes 4194320 | tf_op jit(solution)/shard_map/all_gather | solution.py:42
  259.9 4.8 fusion.70
  267.1 5.5 fusion.73
  272.7 18.0 all-gather.3
  290.7 4.1 reduce-scatter.13.cloned.1.call-done
  294.9 34.1 %reduce-scatter.17.cloned.1.call-done = f32[128,2048]{1,0:T(8,128)} async-done(((f32[256,2048]{1,0:T(8,128)}), f32[128,2048]{1,0:T(8,128)}) %reduce-scatter.17.cloned.1.call-update) | async-done | bytes 1048592 | tf_op jit(solution)/shard_map/reduce_scatter | solution.py:122
  328.9 2.4 multiply_reduce_fusion.7
  332.4 2.7 pad_maximum_fusion.9
  336.9 16.9 all-gather.23.cloned.1.call-done
  353.8 120.9 %all-gather.25.cloned.1.call-done = bf16[2048,5632]{1,0:T(8,128)(2,1)} async-done(((bf16[128,5632]{1,0:T(8,128)(2,1)}), bf16[2048,5632]{1,0:T(8,128)(2,1)}) %all-gather.25.cloned.1.call-update) | async-done | bytes 23068688 | tf_op jit(solution)/shard_map/all_gather | solution.py:49
  474.7 12.6 fusion.71
  487.3 10.9 all-gather.37.cloned.1.call-done
  498.2 99.4 %all-gather.27.cloned.1.call-done = bf16[2816,2048]{1,0:T(8,128)(2,1)} async-done(((bf16[2816,128]{1,0:T(8,128)(2,1)}), bf16[2816,2048]{1,0:T(8,128)(2,1)}) %all-gather.27.cloned.1.call-update) | async-done | bytes 11534352 | tf_op jit(solution)/shard_map/all_gather | solution.py:50
  597.6 10.9 multiply_convert_fusion.3
  608.5 12.6 fusion.4
  621.9 29.4 %reduce-scatter.21.cloned.1.call-done = f32[128,2048]{1,0:T(8,128)} async-done(((f32[256,2048]{1,0:T(8,128)}), f32[128,2048]{1,0:T(8,128)}) %reduce-scatter.21.cloned.1.call-update) | async-done | bytes 1048592 | tf_op jit(solution)/shard_map/reduce_scatter | solution.py:153
  651.3 3.0 multiply_reduce_fusion.1
  655.3 20.4 all-gather.31.cloned.1.call-done
  675.8 12.6 fusion.74
  688.3 11.0 all-gather.39.cloned.1.call-done
  699.3 11.0 multiply_convert_fusion.1
  710.4 13.0 fusion.2
  723.5 8.4 convolution_convert_fusion.2
  732.6 22.8 %reduce-scatter.25.cloned.1.call-done = f32[128,2048]{1,0:T(8,128)} async-done(((f32[256,2048]{1,0:T(8,128)}), f32[128,2048]{1,0:T(8,128)}) %reduce-scatter.25.cloned.1.call-update) | async-done | bytes 1048592 | tf_op jit(solution)/shard_map/reduce_scatter | solution.py:153
  755.4 2.2 multiply_reduce_fusion
  757.5 20.9 %reduce-scatter.19.cloned.1.call-done = bf16[128,2048]{1,0:T(8,128)(2,1)} async-done(((bf16[256,2048]{1,0:T(8,128)(2,1)}), bf16[128,2048]{1,0:T(8,128)(2,1)}) %reduce-scatter.19.cloned.1.call-update) | async-done | bytes 524304 | tf_op jit(solution)/shard_map/reduce_scatter | solution.py:136
  778.4 3.7 fusion.63
  783.2 20.4 all-gather.35.cloned.1.call-done
  803.6 5.1 multiply_reduce_fusion.2
  808.7 18.3 all-gather.33.cloned.1.call-done
  827.0 5.1 multiply_reduce_fusion.4
  832.1 5.0 all-reduce.4
  837.1 2.9 multiply_convert_fusion.17
  846.2 2.6 multiply_convert_fusion.13
  857.0 3.2 multiply_convert_fusion.16
  860.3 12.0 convolution_convert_fusion.1
  874.4 2.3 fusion.78
  878.2 2.3 multiply_convert_fusion.12
  880.6 11.7 convolution_convert_fusion
  892.4 8.5 convolution_convert_fusion.3
  901.2 17.5 fusion.52
  918.8 25.8 %convolution_add_fusion.1 = f32[2048,4096]{1,0:T(8,128)} fusion(f32[2048,4096]{1,0:T(8,128)} %fusion.52, bf16[256,2048]{1,0:T(8,128)(2,1)} %all-gather.29.cloned.1.call-done, bf16[256,1024]{1,0:T(8,128)(2,1)S(1)} %copy-done.31, bf16[256,1024]{1,0:T(8,128)(2,1)S(1)} %copy-done.30, bf16[256,1024]{1,0:T(8,128)(2,1)S(1)} %get-tuple-element.45, ...), kind=kOutput, calls=%fused_computation.1 | convolution fusion | flops 4311744512 | bytes 70254592 | tf_op jit(solution)/shard_map/dot_general | solution.py:21
  945.7 28.3 %fusion.3 = f32[2048,5632]{1,0:T(8,128)} fusion(bf16[256,2048]{1,0:T(8,128)(2,1)S(1)} %copy-done.47, bf16[256,2816]{1,0:T(8,128)(2,1)} %get-tuple-element.37, bf16[256,2816]{1,0:T(8,128)(2,1)} %copy-done.49), kind=kOutput, calls=%fused_computation.27 | convolution fusion | flops 5911347200 | bytes 50069504 | tf_op jit(solution)/shard_map/dot_general | solution.py:21
  974.1 35.7 %convolution_add_fusion = f32[2048,5632]{1,0:T(8,128)} fusion(f32[2048,5632]{1,0:T(8,128)} %fusion.3, bf16[256,2048]{1,0:T(8,128)(2,1)S(1)} %copy-done.46, bf16[256,2816]{1,0:T(8,128)(2,1)} %get-tuple-element.39, bf16[256,2816]{1,0:T(8,128)(2,1)S(1)} %copy-done.48), kind=kOutput, calls=%fused_computation | convolution fusion | flops 5922881536 | bytes 96206848 | tf_op jit(solution)/shard_map/dot_general | solution.py:21
  1012.4 4.6 convolution_add_fusion.3
  1018.4 10.9 fusion.32
  1029.3 15.8 convolution_add_fusion.2
  1049.1 64.0 %all-reduce.2 = (f32[2048]{0:T(1024)S(1)}, f32[2048]{0:T(1024)S(1)}) all-reduce(f32[2048]{0:T(1024)S(1)} %add.171, f32[2048]{0:T(1024)S(1)} %add.174), channel_id=12, replica_groups=mesh['dp'=16,'tensor'=2] {'dp'}, use_global_device_ids=true, to_apply=%region_26.27.clone | all-reduce | flops 4096 | bytes 32768
  1113.3 5.4 all-reduce.3
  1118.9 2.5 fusion.20
  1124.6 153.5 %reduce-scatter.29.cloned.1.call-done = f32[128,4096]{1,0:T(8,128)} async-done(((f32[2048,4096]{1,0:T(8,128)}), f32[128,4096]{1,0:T(8,128)}) %reduce-scatter.29.cloned.1.call-update) | async-done | bytes 2097168 | tf_op jit(solution)/shard_map/reduce_scatter | solution.py:206
  1278.1 2.9 fusion.66
  1281.0 433.6 %reduce-scatter.33.cloned.1.call-done = f32[128,5632]{1,0:T(8,128)} async-done(((f32[2048,5632]{1,0:T(8,128)}), f32[128,5632]{1,0:T(8,128)}) %reduce-scatter.33.cloned.1.call-update) | async-done | bytes 2883600 | tf_op jit(solution)/shard_map/reduce_scatter | solution.py:209
  1714.5 3.6 fusion.65
  1718.1 105.1 %reduce-scatter.31.cloned.1.call-done = f32[1024,128]{1,0:T(8,128)} async-done(((f32[1024,2048]{1,0:T(8,128)}), f32[1024,128]{1,0:T(8,128)}) %reduce-scatter.31.cloned.1.call-update) | async-done | bytes 524304 | tf_op jit(solution)/shard_map/reduce_scatter | solution.py:207
  1823.2 231.2 %reduce-scatter.35.cloned.1.call-done = f32[2816,128]{1,0:T(8,128)} async-done(((f32[2816,2048]{1,0:T(8,128)}), f32[2816,128]{1,0:T(8,128)}) %reduce-scatter.35.cloned.1.call-update) | async-done | bytes 1441808 | tf_op jit(solution)/shard_map/reduce_scatter | solution.py:210
  (286 shorter events, 57.7 us)
Async XLA Ops:
  7.2 27.5 %copy-start.55 = (bf16[128,1024]{1,0:T(8,128)(2,1)S(1)}, bf16[128,1024]{1,0:T(8,128)(2,1)}, u32[]{:S(2)}) copy-start(bf16[128,1024]{1,0:T(8,128)(2,1)} %param.21) | copy-start | bytes 786436
  7.2 27.5 %copy-start.56 = (bf16[128,1024]{1,0:T(8,128)(2,1)S(1)}, bf16[128,1024]{1,0:T(8,128)(2,1)}, u32[]{:S(2)}) copy-start(bf16[128,1024]{1,0:T(8,128)(2,1)} %param.20) | copy-start | bytes 786436
  7.2 27.5 %copy-start.57 = (bf16[128,1024]{1,0:T(8,128)(2,1)S(1)}, bf16[128,1024]{1,0:T(8,128)(2,1)}, u32[]{:S(2)}) copy-start(bf16[128,1024]{1,0:T(8,128)(2,1)} %param.19) | copy-start | bytes 786436
  7.2 27.5 %copy-start.58 = (bf16[128,1024]{1,0:T(8,128)(2,1)S(1)}, bf16[128,1024]{1,0:T(8,128)(2,1)}, u32[]{:S(2)}) copy-start(bf16[128,1024]{1,0:T(8,128)(2,1)} %param.18) | copy-start | bytes 786436
  7.2 46.1 %all-gather.17.cloned.1.call-start = ((), (), s32[]{:S(2)}) async-start(), calls=%async_computation.12 | async-start | bytes 1572864 | tf_op jit(solution)/shard_map/all_gather | solution.py:94
  34.6 148.4 %all-gather.19.cloned.1.call-start = ((), (), s32[]{:S(2)}) async-start(), calls=%async_computation.13 | async-start | bytes 17825792 | tf_op jit(solution)/shard_map/all_gather | solution.py:41
  35.8 168.9 %all-gather.29.cloned.1.call-start = ((), (), s32[]{:S(2)}) async-start(), calls=%async_computation.20 | async-start | bytes 1572864 | tf_op jit(solution)/shard_map/all_gather | solution.py:94
  36.5 223.4 %all-gather.21.cloned.1.call-start = ((), (), s32[]{:S(2)}) async-start(), calls=%async_computation.14 | async-start | bytes 4456448 | tf_op jit(solution)/shard_map/all_gather | solution.py:42
  37.1 257.8 %reduce-scatter.13.cloned.1.call-start = ((), (), s32[]{:S(2)}) async-start(), calls=%async_computation.15 | async-start | bytes 3145728 | tf_op jit(solution)/shard_map/reduce_scatter | solution.py:122
  37.2 178.9 %copy-start.85 = (f32[8]{0:T(128)}, f32[8]{0:T(128)S(1)}, u32[]{:S(2)}) copy-start(f32[8]{0:T(128)S(1)} %neg.23) | copy-start | bytes 100
  37.2 178.9 %copy-start.53 = (f32[256,256]{1,0:T(8,128)}, f32[256,256]{1,0:T(8,128)S(1)}, u32[]{:S(2)}) copy-start(f32[256,256]{1,0:T(8,128)S(1)} %convert_maximum_fusion) | copy-start | bytes 786436
  37.4 157.0 %copy-start.63 = (pred[256,256]{1,0:T(8,128)(4,1)}, pred[256,256]{1,0:T(8,128)(4,1)S(1)}, u32[]{:S(2)}) copy-start(pred[256,256]{1,0:T(8,128)(4,1)S(1)} %fusion.54) | copy-start | bytes 196612
  37.5 178.6 %copy-start.61 = (pred[256,256]{1,0:T(8,128)(4,1)}, pred[256,256]{1,0:T(8,128)(4,1)S(1)}, u32[]{:S(2)}) copy-start(pred[256,256]{1,0:T(8,128)(4,1)S(1)} %fusion.53) | copy-start | bytes 196612
  197.6 27.7 %copy-start.8 = (f32[256,1024]{1,0:T(8,128)}, f32[256,1024]{1,0:T(8,128)S(1)}, u32[]{:S(2)}) copy-start(f32[256,1024]{1,0:T(8,128)S(1)} %copy.74) | copy-start | bytes 3145732
  226.7 38.0 %copy-start.32 = (bf16[256,1024]{1,0:T(8,128)(2,1)}, bf16[256,1024]{1,0:T(8,128)(2,1)S(1)}, u32[]{:S(2)}) copy-start(bf16[256,1024]{1,0:T(8,128)(2,1)S(1)} %multiply_convert_fusion.23) | copy-start | bytes 1572868
  264.7 64.2 %reduce-scatter.17.cloned.1.call-start = ((), (), s32[]{:S(2)}) async-start(), calls=%async_computation.21 | async-start | bytes 3145728 | tf_op jit(solution)/shard_map/reduce_scatter | solution.py:122
  265.3 7.3 copy-start.10
  267.1 61.9 %copy-start.2 = (bf16[2,128,2048]{2,1,0:T(8,128)(2,1)S(1)}, bf16[2,128,2048]{2,1,0:T(8,128)(2,1)}, u32[]{:S(2)}) copy-start(bf16[2,128,2048]{2,1,0:T(8,128)(2,1)} %param.14) | copy-start | bytes 3145732
  272.6 81.2 %all-gather.23.cloned.1.call-start = ((), (), s32[]{:S(2)}) async-start(), calls=%async_computation.16 | async-start | bytes 1572864 | tf_op jit(solution)/shard_map/all_gather | solution.py:131
  290.7 487.7 %copy-start.51 = (f32[16,1,128]{2,1,0:T(1,128)}, f32[16,1,128]{2,1,0:T(1,128)S(1)}, u32[]{:S(2)}) copy-start(f32[16,1,128]{2,1,0:T(1,128)S(1)} %convert_element_type.247) | copy-start | bytes 24580
  331.3 447.1 %copy-start = (f32[128,2048]{1,0:T(8,128)}, f32[128,2048]{1,0:T(8,128)S(1)}, u32[]{:S(2)}) copy-start(f32[128,2048]{1,0:T(8,128)S(1)} %get-tuple-element.33) | copy-start | bytes 3145732
  331.3 447.1 %copy-start.4 = (f32[128,2048]{1,0:T(8,128)}, f32[128,2048]{1,0:T(8,128)S(1)}, u32[]{:S(2)}) copy-start(f32[128,2048]{1,0:T(8,128)S(1)} %get-tuple-element.70) | copy-start | bytes 3145732
  332.3 142.4 %all-gather.25.cloned.1.call-start = ((), (), s32[]{:S(2)}) async-start(), calls=%async_computation.17 | async-start | bytes 24510464 | tf_op jit(solution)/shard_map/all_gather | solution.py:49
  335.2 163.0 %all-gather.37.cloned.1.call-start = ((), (), s32[]{:S(2)}) async-start(), calls=%async_computation.34 | async-start | bytes 1572864 | tf_op jit(solution)/shard_map/all_gather | solution.py:146
  336.3 261.3 %all-gather.27.cloned.1.call-start = ((), (), s32[]{:S(2)}) async-start(), calls=%async_computation.18 | async-start | bytes 12255232 | tf_op jit(solution)/shard_map/all_gather | solution.py:50
  336.9 314.4 %reduce-scatter.21.cloned.1.call-start = ((), (), s32[]{:S(2)}) async-start(), calls=%async_computation.24 | async-start | bytes 3145728 | tf_op jit(solution)/shard_map/reduce_scatter | solution.py:153
  608.5 12.6 copy-start.49
  621.2 54.6 %all-gather.31.cloned.1.call-start = ((), (), s32[]{:S(2)}) async-start(), calls=%async_computation.22 | async-start | bytes 1572864 | tf_op jit(solution)/shard_map/all_gather | solution.py:131
  621.9 66.4 %copy-start.67 = (f32[128]{0:T(128)}, f32[128]{0:T(128)S(1)}, u32[]{:S(2)}) copy-start(f32[128]{0:T(128)S(1)} %add_rsqrt_fusion.2) | copy-start | bytes 1540
  654.3 45.0 %all-gather.39.cloned.1.call-start = ((), (), s32[]{:S(2)}) async-start(), calls=%async_computation.35 | async-start | bytes 1572864 | tf_op jit(solution)/shard_map/all_gather | solution.py:146
  655.1 100.3 %reduce-scatter.25.cloned.1.call-start = ((), (), s32[]{:S(2)}) async-start(), calls=%async_computation.27 | async-start | bytes 3145728 | tf_op jit(solution)/shard_map/reduce_scatter | solution.py:153
  710.4 13.1 copy-start.24
  723.4 55.0 %reduce-scatter.19.cloned.1.call-start = ((), (), s32[]{:S(2)}) async-start(), calls=%async_computation.23 | async-start | bytes 1572864 | tf_op jit(solution)/shard_map/reduce_scatter | solution.py:136
  731.9 46.5 %copy-start.68 = (f32[128]{0:T(128)S(1)}, f32[128]{0:T(128)}, u32[]{:S(2)}) copy-start(f32[128]{0:T(128)} %copy-done.67) | copy-start | bytes 1540
  731.9 46.6 %copy-start.71 = (f32[128]{0:T(128)S(1)}, f32[128]{0:T(128)}, u32[]{:S(2)}) copy-start(f32[128]{0:T(128)} %copy-done.70) | copy-start | bytes 1540
  731.9 71.7 %all-gather.35.cloned.1.call-start = ((), (), s32[]{:S(2)}) async-start(), calls=%async_computation.28 | async-start | bytes 1572864 | tf_op jit(solution)/shard_map/all_gather | solution.py:161
  732.6 49.5 %copy-start.80 = (f32[128]{0:T(128)}, f32[128]{0:T(128)S(1)}, u32[]{:S(2)}) copy-start(f32[128]{0:T(128)S(1)} %broadcast_multiply_fusion.5) | copy-start | bytes 1540
  757.5 24.5 %copy-start.77 = (f32[128]{0:T(128)}, f32[128]{0:T(128)S(1)}, u32[]{:S(2)}) copy-start(f32[128]{0:T(128)S(1)} %broadcast_multiply_fusion.3) | copy-start | bytes 1540
  757.5 46.0 %copy-start.11 = (f32[256,1024]{1,0:T(8,128)S(1)}, f32[256,1024]{1,0:T(8,128)}, u32[]{:S(2)}) copy-start(f32[256,1024]{1,0:T(8,128)} %copy-done.10) | copy-start | bytes 3145732
  782.1 44.9 %all-gather.33.cloned.1.call-start = ((), (), s32[]{:S(2)}) async-start(), calls=%async_computation.25 | async-start | bytes 1572864 | tf_op jit(solution)/shard_map/all_gather | solution.py:161
  782.7 44.3 %copy-start.9 = (f32[256,1024]{1,0:T(8,128)S(1)}, f32[256,1024]{1,0:T(8,128)}, u32[]{:S(2)}) copy-start(f32[256,1024]{1,0:T(8,128)} %copy-done.8) | copy-start | bytes 3145732
  782.7 264.3 %reduce-scatter.23.cloned.1.call-start = ((), (), s32[]{:S(2)}) async-start(), calls=%async_computation.26 | async-start | bytes 1572864 | tf_op jit(solution)/shard_map/reduce_scatter | solution.py:193
  832.1 9.2 copy-start.18
  860.3 12.2 copy-start.43
  860.3 13.2 copy-start.37
  872.3 174.8 %reduce-scatter.27.cloned.1.call-start = ((), (), s32[]{:S(2)}) async-start(), calls=%async_computation.29 | async-start | bytes 1572864 | tf_op jit(solution)/shard_map/reduce_scatter | solution.py:193
  880.6 11.8 copy-start.26
  892.3 226.5 %reduce-scatter.15.cloned.1.call-start = ((), (), s32[]{:S(2)}) async-start(), calls=%async_computation.19 | async-start | bytes 1572864 | tf_op jit(solution)/shard_map/reduce_scatter | solution.py:136
  892.4 8.8 copy-start.28
  892.4 8.8 copy-start.29
  900.9 17.8 copy-start.30
  900.9 17.8 copy-start.31
  901.0 377.1 %reduce-scatter.29.cloned.1.call-start = ((), (), s32[]{:S(2)}) async-start(), calls=%async_computation.30 | async-start | bytes 35651584 | tf_op jit(solution)/shard_map/reduce_scatter | solution.py:206
  944.5 29.5 %copy-start.46 = (bf16[256,2048]{1,0:T(8,128)(2,1)S(1)}, bf16[256,2048]{1,0:T(8,128)(2,1)}, u32[]{:S(2)}) copy-start(bf16[256,2048]{1,0:T(8,128)(2,1)} %all-gather.31.cloned.1.call-done) | copy-start | bytes 3145732
  944.5 29.5 %copy-start.48 = (bf16[256,2816]{1,0:T(8,128)(2,1)S(1)}, bf16[256,2816]{1,0:T(8,128)(2,1)}, u32[]{:S(2)}) copy-start(bf16[256,2816]{1,0:T(8,128)(2,1)} %get-tuple-element.38) | copy-start | bytes 4325380
  944.6 770.0 %reduce-scatter.33.cloned.1.call-start = ((), (), s32[]{:S(2)}) async-start(), calls=%async_computation.32 | async-start | bytes 49020928 | tf_op jit(solution)/shard_map/reduce_scatter | solution.py:209
  1009.8 813.4 %reduce-scatter.31.cloned.1.call-start = ((), (), s32[]{:S(2)}) async-start(), calls=%async_computation.31 | async-start | bytes 8912896 | tf_op jit(solution)/shard_map/reduce_scatter | solution.py:207
  1017.0 12.2 copy-start.25
  1017.0 1037.3 %reduce-scatter.35.cloned.1.call-start = ((), (), s32[]{:S(2)}) async-start(), calls=%async_computation.33 | async-start | bytes 24510464 | tf_op jit(solution)/shard_map/reduce_scatter | solution.py:210
  1018.4 10.9 copy-start.50
  1045.1 73.7 %copy-start.52 = (f32[16,1,128]{2,1,0:T(1,128)S(1)}, f32[16,1,128]{2,1,0:T(1,128)}, u32[]{:S(2)}) copy-start(f32[16,1,128]{2,1,0:T(1,128)} %copy-done.51) | copy-start | bytes 24580
  1045.1 73.7 %copy-start.72 = (f32[128]{0:T(128)S(1)}, f32[128]{0:T(128)}, u32[]{:S(2)}) copy-start(f32[128]{0:T(128)} %copy-done.70) | copy-start | bytes 1540
  1045.2 73.7 %copy-start.81 = (f32[128]{0:T(128)S(1)}, f32[128]{0:T(128)}, u32[]{:S(2)}) copy-start(f32[128]{0:T(128)} %copy-done.80) | copy-start | bytes 1540
  1045.2 73.6 %copy-start.1 = (f32[128,2048]{1,0:T(8,128)S(1)}, f32[128,2048]{1,0:T(8,128)}, u32[]{:S(2)}) copy-start(f32[128,2048]{1,0:T(8,128)} %copy-done) | copy-start | bytes 3145732
  (47 other events, 131.8 us)
Sparse Core Ops, SparseCore 0:
  34.7 18.5 all-gather.16
  56.1 126.8 all-gather.18
  185.1 19.4 all-gather.28
  206.7 53.2 all-gather.20
  264.8 29.9 reduce-scatter.12
  297.1 31.8 reduce-scatter.16
  332.5 21.2 all-gather.22
  356.0 118.7 all-gather.24
  476.8 21.2 all-gather.36
  500.2 97.3 all-gather.26
  621.3 29.9 reduce-scatter.20
  654.4 21.2 all-gather.30
  678.0 21.3 all-gather.38
  723.5 31.8 reduce-scatter.24
  758.0 20.3 reduce-scatter.18
  782.2 21.3 all-gather.34
  805.6 21.2 all-gather.32
  872.4 20.3 reduce-scatter.22
  895.6 20.3 reduce-scatter.26
  918.1 20.3 reduce-scatter.14
  944.7 333.3 reduce-scatter.28
  1282.3 432.1 reduce-scatter.32
  1719.2 103.9 reduce-scatter.30
  1827.8 226.5 reduce-scatter.34
where the time goes:
time: 2070 us; the launch traced here: 2060 us
  waiting for transfers between devices  1540 us (74%)
  matrix products  307 us (15%)
  blocking collectives  121 us (6%)
  other arithmetic  44.5 us (2%)
  local copies, waits for them, and re-layouts  28.7 us (1%)
    reduce_scatter x1, waiting for transfers between devices, local(): lax.psum_scatter(total_pair, 'dp', scatter_dimension=0, tiled=True)  434 us
    reduce_scatter x1, waiting for transfers between devices, local(): lax.psum_scatter(total_down, 'dp', scatter_dimension=1, tiled=True)  231 us
    reduce_scatter x1, waiting for transfers between devices, local(): lax.psum_scatter(total_in, 'dp', scatter_dimension=0, tiled=True)  153 us
    dot_general x8, matrix products, transposed_times(): lax.dot_general(former, latter, (((0,), (0,)), ((), ())), preferred_eleme...  140 us
    all_gather x1, waiting for transfers between devices, fetch_attention(): lax.all_gather(joined_in, 'dp', axis=0, tiled=True)  130 us
    all_gather x1, waiting for transfers between devices, fetch_feedforward(): lax.all_gather(joined_pair, 'dp', axis=0, tiled=True)  121 us
    reduce_scatter x1, waiting for transfers between devices, local(): lax.psum_scatter(total_out, 'dp', scatter_dimension=1, tiled=True)  105 us
    all_gather x1, waiting for transfers between devices, fetch_feedforward(): lax.all_gather(w_down, 'dp', axis=1, tiled=True)  99.4 us
  transfers between devices with their start and end apart: 24, of which 21 were waited for; matrix products, arithmetic and copies ran while one was open for 13% of the time, Pallas kernels for 0%

commit v1 on v0

v1 whole, which is shorter than its diff:
```python
import jax
import jax.numpy as jnp
from jax import lax
from jax.sharding import PartitionSpec as P

EPSILON = 1e-06


def scaled_rows(values):
    inverse = lax.rsqrt(jnp.mean(values * values, axis=-1, keepdims=True) + EPSILON)
    return (values * inverse, inverse)


def times_transposed(former, latter):
    return lax.dot_general(
        former, latter, (((1,), (1,)), ((), ())), preferred_element_type=jnp.float32
    )


def transposed_times(former, latter):
    return lax.dot_general(
        former, latter, (((0,), (0,)), ((), ())), preferred_element_type=jnp.float32
    )


def silu_slope(values):
    sigmoid = jax.nn.sigmoid(values)
    return sigmoid * (1.0 + values * (1.0 - sigmoid))


def norm_backward(grad_normed, unit_rows, inverse, gain_values):
    scaled_grad = grad_normed * gain_values
    return inverse * (
        scaled_grad - unit_rows * jnp.mean(scaled_grad * unit_rows, axis=-1, keepdims=True)
    )


def fetch_attention(gain_attn, joined_in, w_out):
    return (
        lax.all_gather(gain_attn, "dp", axis=0, tiled=True),
        lax.all_gather(joined_in, "dp", axis=0, tiled=True),
        lax.all_gather(w_out, "dp", axis=1, tiled=True),
    )


def fetch_feedforward(gain_ffn, joined_pair, w_down):
    return (
        lax.all_gather(gain_ffn, "dp", axis=0, tiled=True),
        lax.all_gather(joined_pair, "dp", axis=0, tiled=True),
        lax.all_gather(w_down, "dp", axis=1, tiled=True),
    )


def local(
    tokens,
    segment_ids,
    decay_rates,
    gain_attn,
    w_query,
    w_key,
    w_value,
    w_gate,
    w_out,
    gain_ffn,
    w_left,
    w_right,
    w_down,
    cotangent,
):
    batches, local_rows, model_width = tokens.shape
    length = segment_ids.shape[1]
    local_heads = decay_rates.shape[0]
    local_width = w_query.shape[1]
    head_width = local_width // local_heads
    local_units = w_left.shape[1]
    joined_in = jnp.concatenate([w_query, w_key, w_value, w_gate], axis=1)
    joined_pair = jnp.concatenate([w_left, w_right], axis=1)
    places = jnp.arange(length)
    offset = (places[:, None] - places[None, :]).astype(jnp.float32)
    decay_table = jnp.exp(-decay_rates[:, None, None] * jnp.maximum(offset, 0.0)[None])
    rows = batches * length
    flat = lambda values: values.reshape(rows, values.shape[-1])
    gain_full, weight_in, weight_out = fetch_attention(gain_attn, joined_in, w_out)
    inputs = tokens.astype(jnp.float32)
    unit_attn, inverse_attn = scaled_rows(inputs)
    normed = (unit_attn * gain_full.astype(jnp.float32)).astype(jnp.bfloat16)
    normed_all = flat(lax.all_gather(normed, "tensor", axis=1, tiled=True))
    upstream_all = flat(lax.all_gather(cotangent, "tensor", axis=1, tiled=True))
    projected = jnp.dot(normed_all, weight_in, preferred_element_type=jnp.float32)
    query_pre = projected[:, :local_width]
    key_pre = projected[:, local_width : 2 * local_width]
    heads = lambda values: values.astype(jnp.bfloat16).reshape(
        batches, length, local_heads, head_width
    )
    value_rows = heads(projected[:, 2 * local_width : 3 * local_width])
    gate_proj = projected[:, 3 * local_width :]
    queries = heads(jax.nn.silu(query_pre))
    key_rows = heads(jax.nn.silu(key_pre))
    allowed = (offset >= 0.0)[None] & (segment_ids[:, :, None] == segment_ids[:, None, :])
    masked = jnp.where(allowed[:, None], decay_table[None], 0.0)
    scores = jnp.einsum("bihd,bjhd->bhij", queries, key_rows, preferred_element_type=jnp.float32)
    weights = (scores * masked).astype(jnp.bfloat16)
    mixed_heads = flat(
        jnp.einsum(
            "bhij,bjhd->bihd", weights, value_rows, preferred_element_type=jnp.float32
        ).reshape(batches, length, local_width)
    )
    square_sum = lax.psum(jnp.sum(mixed_heads * mixed_heads, axis=-1), "tensor")
    inverse_mixed = lax.rsqrt(square_sum / model_width + EPSILON)[:, None]
    unit_mixed = mixed_heads * inverse_mixed
    branch = (unit_mixed * gate_proj).astype(jnp.bfloat16)

    def scatter_rows(values):
        return lax.psum_scatter(
            values.astype(jnp.bfloat16).reshape(batches, length, model_width),
            "tensor",
            scatter_dimension=1,
            tiled=True,
        ).astype(jnp.float32)

    middle = inputs + scatter_rows(
        jnp.dot(branch, weight_out, preferred_element_type=jnp.float32)
    )
    gain_ffn_full, weight_pair, weight_down = fetch_feedforward(gain_ffn, joined_pair, w_down)
    unit_ffn, inverse_ffn = scaled_rows(middle)
    normed_ffn = (unit_ffn * gain_ffn_full.astype(jnp.float32)).astype(jnp.bfloat16)
    normed_ffn_all = flat(lax.all_gather(normed_ffn, "tensor", axis=1, tiled=True))
    both_proj = jnp.dot(normed_ffn_all, weight_pair, preferred_element_type=jnp.float32)
    left_proj = both_proj[:, :local_units]
    right_proj = both_proj[:, local_units:]
    joined = (left_proj * right_proj).astype(jnp.bfloat16)
    result = middle + scatter_rows(
        jnp.dot(joined, weight_down, preferred_element_type=jnp.float32)
    )

    def over_dp(values, dimension):
        return lax.psum_scatter(
            values.astype(jnp.bfloat16), "dp", scatter_dimension=dimension, tiled=True
        ).astype(jnp.float32)

    grad_down = over_dp(transposed_times(joined, upstream_all), 1)
    grad_joined = times_transposed(upstream_all, weight_down)
    grad_left = (grad_joined * right_proj).astype(jnp.bfloat16)
    grad_right = (grad_joined * left_proj).astype(jnp.bfloat16)
    grad_pair = jnp.concatenate([grad_left, grad_right], axis=1)
    grad_pair_all = over_dp(transposed_times(normed_ffn_all, grad_pair), 0)
    grad_normed_ffn = scatter_rows(times_transposed(grad_pair, weight_pair))
    total_gain_ffn = jnp.sum(grad_normed_ffn * unit_ffn, axis=(0, 1))
    grad_middle = cotangent.astype(jnp.float32) + norm_backward(
        grad_normed_ffn, unit_ffn, inverse_ffn, gain_ffn_full.astype(jnp.float32)
    )
    grad_attn_out = grad_middle.astype(jnp.bfloat16)
    grad_out_all = flat(lax.all_gather(grad_attn_out, "tensor", axis=1, tiled=True))
    grad_out = over_dp(transposed_times(branch, grad_out_all), 1)
    grad_branch = times_transposed(grad_out_all, weight_out)
    grad_unit = grad_branch * gate_proj
    grad_gate = (grad_branch * unit_mixed).astype(jnp.bfloat16)
    dot_sum = lax.psum(jnp.sum(grad_unit * unit_mixed, axis=-1), "tensor")
    grad_mixed = heads(
        inverse_mixed * (grad_unit - unit_mixed * (dot_sum / model_width)[:, None])
    )
    grad_weights = jnp.einsum(
        "bihd,bjhd->bhij", grad_mixed, value_rows, preferred_element_type=jnp.float32
    )
    grad_scores = (grad_weights * masked).astype(jnp.bfloat16)
    joined_heads = lambda values: values.reshape(rows, local_width)
    grad_queries = joined_heads(
        jnp.einsum("bhij,bjhd->bihd", grad_scores, key_rows, preferred_element_type=jnp.float32)
    )
    grad_keys = joined_heads(
        jnp.einsum("bhij,bihd->bjhd", grad_scores, queries, preferred_element_type=jnp.float32)
    )
    grad_values = joined_heads(
        jnp.einsum("bhij,bihd->bjhd", weights, grad_mixed, preferred_element_type=jnp.float32)
    ).astype(jnp.bfloat16)
    grad_query_pre = (grad_queries * silu_slope(query_pre)).astype(jnp.bfloat16)
    grad_key_pre = (grad_keys * silu_slope(key_pre)).astype(jnp.bfloat16)
    grad_projected = jnp.concatenate([grad_query_pre, grad_key_pre, grad_values, grad_gate], axis=1)
    grad_in = over_dp(transposed_times(normed_all, grad_projected), 0)
    grad_normed = scatter_rows(times_transposed(grad_projected, weight_in))
    total_gain_attn = jnp.sum(grad_normed * unit_attn, axis=(0, 1))
    grad_tokens = grad_middle + norm_backward(
        grad_normed, unit_attn, inverse_attn, gain_full.astype(jnp.float32)
    )
    gains = lax.psum_scatter(
        lax.psum(jnp.stack([total_gain_attn, total_gain_ffn]), "tensor"),
        "dp",
        scatter_dimension=1,
        tiled=True,
    )
    return (
        result.astype(jnp.bfloat16),
        grad_tokens,
        gains[0],
        grad_in[:, :local_width],
        grad_in[:, local_width : 2 * local_width],
        grad_in[:, 2 * local_width : 3 * local_width],
        grad_in[:, 3 * local_width :],
        grad_out,
        gains[1],
        grad_pair_all[:, :local_units],
        grad_pair_all[:, local_units:],
        grad_down,
    )


def solution(mesh):
    return jax.shard_map(
        local,
        mesh=mesh,
        in_specs=(
            P(None, ("dp", "tensor"), None),
            P(None, "dp"),
            P("tensor"),
            P("dp"),
            P("dp", "tensor"),
            P("dp", "tensor"),
            P("dp", "tensor"),
            P("dp", "tensor"),
            P("tensor", "dp"),
            P("dp"),
            P("dp", "tensor"),
            P("dp", "tensor"),
            P("tensor", "dp"),
            P(None, ("dp", "tensor"), None),
        ),
        out_specs=(
            P(None, ("dp", "tensor"), None),
            P(None, ("dp", "tensor"), None),
            P("dp"),
            P("dp", "tensor"),
            P("dp", "tensor"),
            P("dp", "tensor"),
            P("dp", "tensor"),
            P("tensor", "dp"),
            P("dp"),
            P("dp", "tensor"),
            P("dp", "tensor"),
            P("tensor", "dp"),
        ),
        check_vma=False,
    )
```

time: 2070 us -> 1500 us (0.72)
  waiting for transfers between devices: 1540 us -> 1150 us
  matrix products: 307 us -> 170 us
  blocking collectives: 121 us -> 56.5 us
  local copies, waits for them, and re-layouts: 28.7 us -> 58.8 us
    reduce_scatter x12 -> x6, waiting for transfers between devices: 1030 us -> 470 us  [the longest x2 408 us: over_dp(): lax.psum_scatter(values.astype(jnp.bfloat16), 'dp', scatter_dimension=dim...]
    unnamed x24 -> x20, waiting for transfers between devices: 3.28 us -> 212 us
    dot_general x8 -> x4, matrix products: 140 us -> 52.1 us  [transposed_times(): lax.dot_general(former, latter, (((0,), (0,)), ((), ())), preferred_eleme...]
    unnamed x1 -> x0, blocking collectives: 64 us -> none
    dot_general x8 -> x4, matrix products: 81.5 us -> 56.4 us  [times_transposed(): lax.dot_general(former, latter, (((1,), (1,)), ((), ())), preferred_eleme...]
    unnamed x177 -> x65, local copies, waits for them, and re-layouts: 11.4 us -> 35.1 us
    all_gather x8 -> x4, waiting for transfers between devices: 121 us -> 105 us  [the longest x1 33 us: local(): lax.all_gather(grad_attn_out, 'tensor', axis=1, tiled=True)]
  transfers between devices with their start and end apart: 24 -> 17, of which waited for: 21 -> 16; matrix products, arithmetic and copies ran while one was open for 13% -> 11% of each run, Pallas kernels for 0% -> 0%
where the time goes in v1:
time: 1500 us; the launch traced here: 1490 us
  waiting for transfers between devices  1150 us (77%)
  matrix products  170 us (11%)
  local copies, waits for them, and re-layouts  58.8 us (4%)
  blocking collectives  56.5 us (4%)
  other arithmetic  39.3 us (3%)
    reduce_scatter x2, waiting for transfers between devices, over_dp(): lax.psum_scatter(values.astype(jnp.bfloat16), 'dp', scatter_dimension=dim...  408 us
    unnamed x20, waiting for transfers between devices  212 us
    all_gather x1, waiting for transfers between devices, fetch_attention(): lax.all_gather(joined_in, 'dp', axis=0, tiled=True)  130 us
    all_gather x1, waiting for transfers between devices, fetch_feedforward(): lax.all_gather(joined_pair, 'dp', axis=0, tiled=True)  121 us
    all_gather x1, waiting for transfers between devices, fetch_feedforward(): lax.all_gather(w_down, 'dp', axis=1, tiled=True)  99.8 us
    reduce_scatter x4, waiting for transfers between devices, scatter_rows(): lax.psum_scatter(values.astype(jnp.bfloat16).reshape(batches, length, mod...  61.8 us
    dot_general x4, matrix products, times_transposed(): lax.dot_general(former, latter, (((1,), (1,)), ((), ())), preferred_eleme...  56.4 us
    dot_general x4, matrix products, transposed_times(): lax.dot_general(former, latter, (((0,), (0,)), ((), ())), preferred_eleme...  52.1 us
  transfers between devices with their start and end apart: 17, of which 16 were waited for; matrix products, arithmetic and copies ran while one was open for 11% of the time, Pallas kernels for 0%

profile of v1, /device:TPU:0, one launch (start us, length us, event | category | flops | bytes accessed | tf_op | source)
XLA Modules:
  0.0 1493.9 jit_solution(15559554712629846349)
XLA Ops:
  7.3 1.6 fusion.20
  8.9 23.1 %all-gather = bf16[16,1,128]{2,1,0:T(2,128)(2,1)S(1)} all-gather(bf16[1,1,128]{2,1,0:T(2,128)(2,1)} %bitcast.145), channel_id=1, replica_groups=mesh['dp'=16,'tensor'=2] {'dp'}, dimensions={0}, use_global_device_ids=true | all-gather | bytes 4352 | tf_op jit(solution)/shard_map/all_gather | solution.py:40
  32.0 2.5 fusion.17
  37.3 27.9 %all-gather.11.cloned.1.call-done = bf16[2,256,2048]{2,1,0:T(8,128)(2,1)} async-done(((bf16[2,128,2048]{2,1,0:T(8,128)(2,1)}), bf16[2,256,2048]{2,1,0:T(8,128)(2,1)}) %all-gather.11.cloned.1.call-update) | async-done | bytes 2097168 | tf_op jit(solution)/shard_map/all_gather | solution.py:87
  65.1 129.7 %all-gather.13.cloned.1.call-done = bf16[2048,4096]{1,0:T(8,128)(2,1)} async-done(((bf16[128,4096]{1,0:T(8,128)(2,1)}), bf16[2048,4096]{1,0:T(8,128)(2,1)}) %all-gather.13.cloned.1.call-update) | async-done | bytes 16777232 | tf_op jit(solution)/shard_map/all_gather | solution.py:41
  194.8 12.3 fusion.38
  207.6 2.6 fusion.28
  211.5 2.4 copy.44
  213.9 2.5 copy.57
  216.3 2.4 copy.46
  218.8 2.4 fusion
  221.2 2.2 multiply_reduce_fusion.2
  223.4 2.1 copy.41
  225.5 4.9 psum.21
  230.5 2.1 multiply_convert_fusion.6
  232.6 15.8 %all-gather.15.cloned.1.call-done = bf16[1024,2048]{1,0:T(8,128)(2,1)} async-done(((bf16[1024,128]{1,0:T(8,128)(2,1)}), bf16[1024,2048]{1,0:T(8,128)(2,1)}) %all-gather.15.cloned.1.call-update) | async-done | bytes 4194320 | tf_op jit(solution)/shard_map/all_gather | solution.py:42
  248.4 5.9 convolution_convert_fusion.4
  254.9 18.5 %all-gather.1 = bf16[16,1,128]{2,1,0:T(2,128)(2,1)S(1)} all-gather(bf16[1,1,128]{2,1,0:T(2,128)(2,1)S(1)} %bitcast.146), channel_id=1, replica_groups=mesh['dp'=16,'tensor'=2] {'dp'}, dimensions={0}, use_global_device_ids=true | all-gather | bytes 4352 | tf_op jit(solution)/shard_map/all_gather | solution.py:48
  273.5 11.0 reduce-scatter.16.cloned.1.call-done
  284.5 1.7 multiply_reduce_fusion.1
  286.2 1.5 multiply_convert_fusion.5
  287.8 2.3 pad_maximum_fusion.6
  291.9 29.2 %all-gather.17.cloned.1.call-done = bf16[2,256,2048]{2,1,0:T(8,128)(2,1)} async-done(((bf16[2,128,2048]{2,1,0:T(8,128)(2,1)}), bf16[2,256,2048]{2,1,0:T(8,128)(2,1)}) %all-gather.17.cloned.1.call-update) | async-done | bytes 2097168 | tf_op jit(solution)/shard_map/all_gather | solution.py:127
  321.1 120.9 %all-gather.19.cloned.1.call-done = bf16[2048,5632]{1,0:T(8,128)(2,1)} async-done(((bf16[128,5632]{1,0:T(8,128)(2,1)}), bf16[2048,5632]{1,0:T(8,128)(2,1)}) %all-gather.19.cloned.1.call-update) | async-done | bytes 23068688 | tf_op jit(solution)/shard_map/all_gather | solution.py:49
  441.9 19.6 %fusion.39 = f32[512,5632]{1,0:T(8,128)} fusion(bf16[512,2048]{1,0:T(8,128)(2,1)} %bitcast.149, bf16[2048,5632]{1,0:T(8,128)(2,1)} %all-gather.19.cloned.1.call-done), kind=kOutput, calls=%fused_computation.97 | convolution fusion | flops 11811160064 | bytes 36700160 | tf_op jit(solution)/shard_map/dot_general | solution.py:128
  461.5 15.2 %all-gather.23.cloned.1.call-done = bf16[2,256,2048]{2,1,0:T(8,128)(2,1)} async-done(((bf16[2,128,2048]{2,1,0:T(8,128)(2,1)}), bf16[2,256,2048]{2,1,0:T(8,128)(2,1)}) %all-gather.23.cloned.1.call-update) | async-done | bytes 2097168 | tf_op jit(solution)/shard_map/all_gather | solution.py:88
  476.7 99.8 %all-gather.21.cloned.1.call-done = bf16[2816,2048]{1,0:T(8,128)(2,1)} async-done(((bf16[2816,128]{1,0:T(8,128)(2,1)}), bf16[2816,2048]{1,0:T(8,128)(2,1)}) %all-gather.21.cloned.1.call-update) | async-done | bytes 11534352 | tf_op jit(solution)/shard_map/all_gather | solution.py:50
  576.5 16.0 %multiply_convert_fusion.1 = (bf16[512,2816]{1,0:T(8,128)(2,1)}, bf16[512,2816]{1,0:T(8,128)(2,1)}, bf16[512,2816]{1,0:T(8,128)(2,1)}) fusion(f32[512,5632]{1,0:T(8,128)} %fusion.39, bf16[512,2048]{1,0:T(8,128)(2,1)} %bitcast.151, bf16[2816,2048]{1,0:T(8,128)(2,1)} %all-gather.21.cloned.1.call-done), kind=kOutput, calls=%fused_computation.7 | convolution fusion | flops 5914230784 | bytes 33816576 | tf_op jit(solution)/shard_map/dot_general | solution.py:15
  592.4 17.9 %fusion.7 = bf16[512,2048]{1,0:T(8,128)(2,1)} fusion(bf16[2048,5632]{1,0:T(8,128)(2,1)} %all-gather.19.cloned.1.call-done, bf16[512,2816]{1,0:T(8,128)(2,1)} %get-tuple-element.17, bf16[512,2816]{1,0:T(8,128)(2,1)} %get-tuple-element.16), kind=kOutput, calls=%fused_computation.21 | convolution fusion | flops 11823742976 | bytes 30932992 | tf_op jit(solution)/shard_map/dot_general | solution.py:15
  610.4 30.1 %reduce-scatter.20.cloned.1.call-done = bf16[2,128,2048]{2,1,0:T(8,128)(2,1)} async-done(((bf16[2,256,2048]{2,1,0:T(8,128)(2,1)}), bf16[2,128,2048]{2,1,0:T(8,128)(2,1)}) %reduce-scatter.20.cloned.1.call-update) | async-done | bytes 1048592 | tf_op jit(solution)/shard_map/reduce_scatter | solution.py:114
  640.5 2.1 fusion.16
  642.7 2.0 fusion.31
  645.0 33.0 %all-gather.25.cloned.1.call-done = bf16[2,256,2048]{2,1,0:T(8,128)(2,1)} async-done(((bf16[2,128,2048]{2,1,0:T(8,128)(2,1)}), bf16[2,256,2048]{2,1,0:T(8,128)(2,1)}) %all-gather.25.cloned.1.call-update) | async-done | bytes 2097168 | tf_op jit(solution)/shard_map/all_gather | solution.py:153
  678.0 7.9 multiply_reduce_fusion
  686.0 4.9 psum.22
  690.9 4.5 fusion.25
  696.7 2.4 copy.48
  699.1 3.3 fusion.1
  703.9 1.8 convolution_bitcast_fusion
  705.7 2.1 convolution_bitcast_fusion.1
  707.9 2.4 copy.49
  710.3 2.5 copy.85
  712.8 2.9 copy.45
  715.7 2.9 copy.47
  718.6 5.3 fusion.22
  723.8 14.6 convolution_convert_fusion.6
  738.9 10.8 convolution_convert_fusion.5
  749.8 20.6 %reduce-scatter.22.cloned.1.call-done = bf16[2,128,2048]{2,1,0:T(8,128)(2,1)} async-done(((bf16[2,256,2048]{2,1,0:T(8,128)(2,1)}), bf16[2,128,2048]{2,1,0:T(8,128)(2,1)}) %reduce-scatter.22.cloned.1.call-update) | async-done | bytes 1048592 | tf_op jit(solution)/shard_map/reduce_scatter | solution.py:114
  770.4 1.9 fusion.19
  773.8 6.3 convolution_convert_fusion.3
  780.1 6.4 copy.50
  786.6 11.2 convolution_convert_fusion.2
  797.7 15.2 %copy.52 = bf16[2816,2048]{0,1:T(8,128)(2,1)} copy(bf16[2816,2048]{1,0:T(8,128)(2,1)} %convolution_convert_fusion.2) | data formatting | bytes 23068672
  813.2 15.0 %convolution_convert_fusion.1 = bf16[2048,4096]{1,0:T(8,128)(2,1)} fusion(bf16[512,2048]{1,0:T(8,128)(2,1)} %bitcast.148, bf16[512,1024]{1,0:T(8,128)(2,1)} %get-tuple-element.24, bf16[512,1024]{1,0:T(8,128)(2,1)} %bitcast.130, bf16[512,1024]{1,0:T(8,128)(2,1)} %get-tuple-element.20, bf16[512,1024]{1,0:T(8,128)(2,1)} %get-tuple-element.19), kind=kOutput, calls=%fused_computation.1 | convolution fusion | flops 8615100416 | bytes 23068672 | tf_op jit(solution)/shard_map/dot_general | solution.py:21
  828.3 19.7 %convolution_convert_fusion = bf16[2048,5632]{1,0:T(8,128)(2,1)} fusion(bf16[512,2048]{1,0:T(8,128)(2,1)} %bitcast.150, bf16[512,2816]{1,0:T(8,128)(2,1)} %get-tuple-element.17, bf16[512,2816]{1,0:T(8,128)(2,1)} %get-tuple-element.16), kind=kOutput, calls=%fused_computation | convolution fusion | flops 11834228736 | bytes 30932992 | tf_op jit(solution)/shard_map/dot_general | solution.py:21
  848.0 5.2 fusion.12
  853.2 12.2 reduce-scatter.32.cloned.1.call-done
  866.3 4.9 psum.24
  871.8 69.7 %reduce-scatter.28.cloned.1.call-done = bf16[128,1024]{1,0:T(8,128)(2,1)} async-done(((bf16[2048,1024]{1,0:T(8,128)(2,1)}), bf16[128,1024]{1,0:T(8,128)(2,1)}) %reduce-scatter.28.cloned.1.call-update) | async-done | bytes 262160
  943.5 127.3 %reduce-scatter.30.cloned.1.call-done = bf16[128,2816]{1,0:T(8,128)(2,1)} async-done(((bf16[2048,2816]{1,0:T(8,128)(2,1)}), bf16[128,2816]{1,0:T(8,128)(2,1)}) %reduce-scatter.30.cloned.1.call-update) | async-done | bytes 720912
  1073.4 180.2 %reduce-scatter.24.cloned.1.call-done = bf16[128,4096]{1,0:T(8,128)(2,1)} async-done(((bf16[2048,4096]{1,0:T(8,128)(2,1)}), bf16[128,4096]{1,0:T(8,128)(2,1)}) %reduce-scatter.24.cloned.1.call-update) | async-done | bytes 1048592 | tf_op jit(solution)/shard_map/reduce_scatter | solution.py:137
  1253.6 2.6 fusion.37
  1256.2 227.8 %reduce-scatter.26.cloned.1.call-done = bf16[128,5632]{1,0:T(8,128)(2,1)} async-done(((bf16[2048,5632]{1,0:T(8,128)(2,1)}), bf16[128,5632]{1,0:T(8,128)(2,1)}) %reduce-scatter.26.cloned.1.call-update) | async-done | bytes 1441808 | tf_op jit(solution)/shard_map/reduce_scatter | solution.py:137
  1484.1 3.1 fusion.36
  (115 shorter events, 18.2 us)
Async XLA Ops:
  7.2 58.0 %all-gather.11.cloned.1.call-start = ((), (), s32[]{:S(2)}) async-start(), calls=%async_computation.9 | async-start | bytes 3145728 | tf_op jit(solution)/shard_map/all_gather | solution.py:87
  7.2 27.4 %copy-start.15 = (bf16[128,1024]{1,0:T(8,128)(2,1)S(1)}, bf16[128,1024]{1,0:T(8,128)(2,1)}, u32[]{:S(2)}) copy-start(bf16[128,1024]{1,0:T(8,128)(2,1)} %param.21) | copy-start | bytes 786436
  7.2 27.4 %copy-start.16 = (bf16[128,1024]{1,0:T(8,128)(2,1)S(1)}, bf16[128,1024]{1,0:T(8,128)(2,1)}, u32[]{:S(2)}) copy-start(bf16[128,1024]{1,0:T(8,128)(2,1)} %param.20) | copy-start | bytes 786436
  7.2 27.4 %copy-start.17 = (bf16[128,1024]{1,0:T(8,128)(2,1)S(1)}, bf16[128,1024]{1,0:T(8,128)(2,1)}, u32[]{:S(2)}) copy-start(bf16[128,1024]{1,0:T(8,128)(2,1)} %param.19) | copy-start | bytes 786436
  7.3 27.4 %copy-start.18 = (bf16[128,1024]{1,0:T(8,128)(2,1)S(1)}, bf16[128,1024]{1,0:T(8,128)(2,1)}, u32[]{:S(2)}) copy-start(bf16[128,1024]{1,0:T(8,128)(2,1)} %param.18) | copy-start | bytes 786436
  8.9 26.8 %copy-start.21 = (f32[2,128]{1,0:T(2,128)}, f32[2,128]{1,0:T(2,128)S(1)}, u32[]{:S(2)}) copy-start(f32[2,128]{1,0:T(2,128)S(1)} %add_rsqrt_fusion.2) | copy-start | bytes 3076
  32.0 3.7 copy-start.19
  34.5 2.0 copy-start.25
  34.6 2.1 copy-start.23
  34.6 160.2 %all-gather.13.cloned.1.call-start = ((), (), s32[]{:S(2)}) async-start(), calls=%async_computation.10 | async-start | bytes 17825792 | tf_op jit(solution)/shard_map/all_gather | solution.py:41
  35.7 212.6 %all-gather.15.cloned.1.call-start = ((), (), s32[]{:S(2)}) async-start(), calls=%async_computation.11 | async-start | bytes 4456448 | tf_op jit(solution)/shard_map/all_gather | solution.py:42
  36.5 248.0 %reduce-scatter.16.cloned.1.call-start = ((), (), s32[]{:S(2)}) async-start(), calls=%async_computation.12 | async-start | bytes 3145728 | tf_op jit(solution)/shard_map/reduce_scatter | solution.py:114
  37.3 181.5 %copy-start.3 = (f32[8,256,256]{2,1,0:T(8,128)}, f32[8,256,256]{2,1,0:T(8,128)S(1)}, u32[]{:S(2)}) copy-start(f32[8,256,256]{2,1,0:T(8,128)S(1)} %multiply_exponential_fusion) | copy-start | bytes 6291460
  207.1 4.4 copy-start.2
  207.5 13.6 copy-start.8
  221.2 2.2 copy-start.4
  225.5 7.0 copy-start.6
  232.6 21.7 %copy-start.13 = (bf16[512,1024]{1,0:T(8,128)(2,1)}, bf16[512,1024]{1,0:T(8,128)(2,1)S(1)}, u32[]{:S(2)}) copy-start(bf16[512,1024]{1,0:T(8,128)(2,1)S(1)} %multiply_convert_fusion.6) | copy-start | bytes 3145732
  254.3 0.7 copy-start.24
  254.3 30.2 %copy-start = (bf16[2,128,2048]{2,1,0:T(8,128)(2,1)S(1)}, bf16[2,128,2048]{2,1,0:T(8,128)(2,1)}, u32[]{:S(2)}) copy-start(bf16[2,128,2048]{2,1,0:T(8,128)(2,1)} %param.14) | copy-start | bytes 3145732
  254.3 66.8 %all-gather.17.cloned.1.call-start = ((), (), s32[]{:S(2)}) async-start(), calls=%async_computation.13 | async-start | bytes 3145728 | tf_op jit(solution)/shard_map/all_gather | solution.py:127
  284.5 1.7 copy-start.1
  286.2 1.6 copy-start.14
  287.8 154.1 %all-gather.19.cloned.1.call-start = ((), (), s32[]{:S(2)}) async-start(), calls=%async_computation.14 | async-start | bytes 24510464 | tf_op jit(solution)/shard_map/all_gather | solution.py:49
  290.2 186.5 %all-gather.23.cloned.1.call-start = ((), (), s32[]{:S(2)}) async-start(), calls=%async_computation.17 | async-start | bytes 3145728 | tf_op jit(solution)/shard_map/all_gather | solution.py:88
  290.9 285.5 %all-gather.21.cloned.1.call-start = ((), (), s32[]{:S(2)}) async-start(), calls=%async_computation.15 | async-start | bytes 12255232 | tf_op jit(solution)/shard_map/all_gather | solution.py:50
  291.7 348.9 %reduce-scatter.20.cloned.1.call-start = ((), (), s32[]{:S(2)}) async-start(), calls=%async_computation.18 | async-start | bytes 3145728 | tf_op jit(solution)/shard_map/reduce_scatter | solution.py:114
  610.3 32.3 %copy-start.7 = (bf16[2,128,2048]{2,1,0:T(8,128)(2,1)S(1)}, bf16[2,128,2048]{2,1,0:T(8,128)(2,1)}, u32[]{:S(2)}) copy-start(bf16[2,128,2048]{2,1,0:T(8,128)(2,1)} %param.27) | copy-start | bytes 3145732
  610.4 67.7 %all-gather.25.cloned.1.call-start = ((), (), s32[]{:S(2)}) async-start(), calls=%async_computation.19 | async-start | bytes 3145728 | tf_op jit(solution)/shard_map/all_gather | solution.py:153
  640.5 2.1 copy-start.11
  644.7 125.7 %reduce-scatter.22.cloned.1.call-start = ((), (), s32[]{:S(2)}) async-start(), calls=%async_computation.20 | async-start | bytes 3145728 | tf_op jit(solution)/shard_map/reduce_scatter | solution.py:114
  699.1 3.3 copy-start.5
  699.1 3.3 copy-start.12
  702.4 1.4 copy-start.10
  703.9 1.8 copy-start.9
  738.4 109.6 %reduce-scatter.18.cloned.1.call-start = ((), (), s32[]{:S(2)}) async-start(), calls=%async_computation.16 | async-start | bytes 3145728 | tf_op jit(solution)/shard_map/reduce_scatter | solution.py:114
  749.7 20.7 %copy-start.20 = (f32[16,1,128]{2,1,0:T(1,128)S(1)}, f32[16,1,128]{2,1,0:T(1,128)}, u32[]{:S(2)}) copy-start(f32[16,1,128]{2,1,0:T(1,128)} %copy-done.19) | copy-start | bytes 24580
  749.7 20.7 %copy-start.22 = (f32[2,128]{1,0:T(2,128)S(1)}, f32[2,128]{1,0:T(2,128)}, u32[]{:S(2)}) copy-start(f32[2,128]{1,0:T(2,128)} %copy-done.21) | copy-start | bytes 3076
  749.7 115.7 %reduce-scatter.32.cloned.1.call-start = ((), (), s32[]{:S(2)}) async-start(), calls=%async_computation.25 | async-start | bytes 1114112
  773.8 167.8 %reduce-scatter.28.cloned.1.call-start = ((), (), s32[]{:S(2)}) async-start(), calls=%async_computation.23 | async-start | bytes 4456448
  786.5 284.3 %reduce-scatter.30.cloned.1.call-start = ((), (), s32[]{:S(2)}) async-start(), calls=%async_computation.24 | async-start | bytes 12255232
  813.0 440.7 %reduce-scatter.24.cloned.1.call-start = ((), (), s32[]{:S(2)}) async-start(), calls=%async_computation.21 | async-start | bytes 17825792 | tf_op jit(solution)/shard_map/reduce_scatter | solution.py:137
  828.2 655.8 %reduce-scatter.26.cloned.1.call-start = ((), (), s32[]{:S(2)}) async-start(), calls=%async_computation.22 | async-start | bytes 24510464 | tf_op jit(solution)/shard_map/reduce_scatter | solution.py:137
Sparse Core Ops, SparseCore 0:
  34.7 30.3 all-gather.10
  67.9 126.8 all-gather.12
  196.9 51.3 all-gather.14
  254.4 30.0 reduce-scatter.15
  287.9 33.1 all-gather.16
  323.2 118.7 all-gather.18
  443.5 33.0 all-gather.22
  479.0 97.3 all-gather.20
  610.5 30.0 reduce-scatter.19
  644.8 33.1 all-gather.24
  738.6 31.8 reduce-scatter.21
  772.6 31.8 reduce-scatter.17
  808.1 57.3 reduce-scatter.31
  869.7 71.8 reduce-scatter.27
  945.5 125.2 reduce-scatter.29
  1075.3 178.3 reduce-scatter.23
  1258.2 225.8 reduce-scatter.25

commit v2 on v1

v2 whole, which is shorter than its diff:
```python
import functools

import jax
import jax.numpy as jnp
from jax import lax
from jax.experimental import pallas as pl
from jax.experimental.pallas import tpu as pltpu
from jax.sharding import PartitionSpec as P

EPSILON = 1e-06
LAYERS = 4
CORES = 2
LANES = 128
AHEAD = 3
SUMS = 3
FETCH = 3
MESH = pl.DeviceIdType.MESH


class Place:
    def __init__(self, mids):
        place = lax.axis_index("dp")
        self.mids = mids
        self.t = lax.axis_index("tensor")
        self.k = lax.rem(place, CORES)
        self.m = lax.rem(lax.div(place, CORES), mids)
        self.z = lax.div(place, CORES * mids)

    def device(self, z, m, k):
        return ((z * self.mids + m) * CORES + k, self.t)

    def layer(self, step):
        return lax.rem(self.z + step, LAYERS)

    def mid(self, step):
        return lax.rem(self.m + step, self.mids)

    def row(self, core, batch, half, part):
        return pl.multiple_of(((core * 2 + batch) * 2 + half) * part, part)

    def weight_peers(self):
        peers = [self.device(self.z, self.m, 1 - self.k)]
        for step in range(1, LAYERS):
            for core in range(CORES):
                peers.append(self.device(self.layer(step), self.m, core))
        for step in range(1, self.mids):
            peers.append(self.device(self.z, self.mid(step), self.k))
        return peers


def greet(peers):
    barrier = pltpu.get_barrier_semaphore()
    for peer in peers:
        pl.semaphore_signal(barrier, inc=1, device_id=peer, device_id_type=MESH)
    pl.semaphore_wait(barrier, len(peers))


def remote(source, target, send, receive, peer):
    return pltpu.make_async_remote_copy(
        src_ref=source,
        dst_ref=target,
        send_sem=send,
        recv_sem=receive,
        device_id=peer,
        device_id_type=MESH,
    )


class Gather:
    def __init__(self, place, source, target, sems):
        self.source, self.target = source, target
        self.send, self.receive, self.local = sems
        here = place
        self.hops = []
        sibling = 1 - here.k
        own = target.at[here.z, here.m, here.k]
        self.hops.append(
            remote(
                source.at[sibling],
                own,
                self.send.at[0],
                self.receive.at[0],
                here.device(here.z, here.m, sibling),
            )
        )
        self.arrivals = self.hops[:]
        for step in range(1, LAYERS):
            for core in range(CORES):
                slot = 1 + (step - 1) * CORES
                hop = functools.partial(
                    remote,
                    source.at[core],
                    own,
                    self.send.at[slot + core],
                    peer=here.device(here.layer(step), here.m, core),
                )
                self.hops.append(hop(self.receive.at[slot + here.k]))
                self.arrivals.append(hop(self.receive.at[slot + core]))
        self.keep = pltpu.make_async_copy(source.at[here.k], own, self.local)
        base = 1 + (LAYERS - 1) * CORES
        row = target.at[:, here.m]
        self.crossings = [
            remote(
                row,
                row,
                self.send.at[base + step - 1],
                self.receive.at[base + step - 1],
                here.device(here.z, here.mid(step), here.k),
            )
            for step in range(1, here.mids)
        ]

    def start(self):
        self.keep.start()
        for hop in self.hops:
            hop.start()

    def cross(self):
        self.keep.wait()
        for hop in self.arrivals:
            hop.wait_recv()
        for crossing in self.crossings:
            crossing.start()

    def arrive(self):
        for crossing in self.crossings:
            crossing.wait_recv()

    def finish(self):
        for hop in self.hops + self.crossings:
            hop.wait_send()


class Reduce:
    def __init__(self, place, source, crossed, landed, output, slots, sems):
        self.place, self.source, self.crossed, self.landed = place, source, crossed, landed
        self.output = output
        self.own_slot, self.cross_slot, self.sum_slot, self.land_slot, self.out_slot = slots
        send, receive, local = sems
        here = place
        self.crossings = [
            remote(
                source.at[:, here.mid(step)],
                crossed.at[step - 1],
                send.at[step - 1],
                receive.at[step - 1],
                here.device(here.z, here.mid(step), here.k),
            )
            for step in range(1, here.mids)
        ]
        base = here.mids - 1
        sibling = 1 - here.k
        self.hops = [
            remote(
                self.sum_slot.at[here.z, sibling],
                landed.at[here.k, 0],
                send.at[base],
                receive.at[base],
                here.device(here.z, here.m, sibling),
            )
        ]
        self.arrivals = self.hops[:]
        for step in range(1, LAYERS):
            for core in range(CORES):
                slot = base + 1 + (step - 1) * CORES
                hop = functools.partial(
                    remote,
                    self.sum_slot.at[here.layer(step), core],
                    landed.at[here.k, step],
                    send.at[slot + core],
                    peer=here.device(here.layer(step), here.m, core),
                )
                self.hops.append(hop(receive.at[slot + here.k]))
                self.arrivals.append(hop(receive.at[slot + core]))
        self.keep = pltpu.make_async_copy(
            self.sum_slot.at[here.z, here.k], landed.at[here.k, 0], local.at[0]
        )
        self.load_own = pltpu.make_async_copy(source.at[:, here.m], self.own_slot, local.at[1])
        self.load_cross = pltpu.make_async_copy(crossed, self.cross_slot, local.at[2])
        self.load_land = pltpu.make_async_copy(landed, self.land_slot, local.at[3])
        self.store = pltpu.make_async_copy(self.out_slot, output, local.at[4])

    def start(self):
        for crossing in self.crossings:
            crossing.start()

    def load(self):
        self.load_own.start()
        for crossing in self.crossings:
            crossing.wait_recv()
        self.load_cross.start()

    def add(self):
        self.load_own.wait()
        self.load_cross.wait()

        @pl.loop(0, LAYERS * CORES)
        def _(at):
            layer, core = lax.div(at, CORES), lax.rem(at, CORES)
            total = self.own_slot[layer, core].astype(jnp.float32)
            for step in range(1, self.place.mids):
                total += self.cross_slot[step - 1, layer, core].astype(jnp.float32)
            self.sum_slot[layer, core] = total.astype(jnp.bfloat16)

        self.keep.start()
        for hop in self.hops:
            hop.start()

    def release(self):
        for hop in self.hops:
            hop.wait_send()

    def fetch(self):
        self.keep.wait()
        for hop in self.arrivals:
            hop.wait_recv()
        self.load_land.start()

    def total(self):
        self.load_land.wait()

        @pl.loop(0, CORES)
        def _(core):
            total = self.land_slot[core, 0].astype(jnp.float32)
            for step in range(1, LAYERS):
                total += self.land_slot[core, step].astype(jnp.float32)
            self.out_slot[core] = total

        self.store.start()

    def finish(self):
        for crossing in self.crossings:
            crossing.wait_send()


def dots(left, right, left_axis, right_axis):
    return lax.dot_general(
        left, right, (((left_axis,), (right_axis,)), ((), ())), preferred_element_type=jnp.float32
    )


class Reducer:
    def __init__(self, chunks):
        self.chunks = chunks
        self.produced = self.started = self.ticks = 0

    def launch(self):
        while self.started < min(self.produced, self.ticks + AHEAD + 1):
            self.chunks[self.started].start()
            self.started += 1

    def produce(self):
        self.produced += 1
        self.launch()

    def tick(self):
        at, chunks = self.ticks, self.chunks
        count = len(chunks)
        if at < count:
            assert at < self.started
            chunks[at].load()
        if 1 <= at <= count:
            if at - 1 >= SUMS:
                chunks[at - 1 - SUMS].release()
            chunks[at - 1].add()
        if FETCH <= at < count + FETCH:
            chunks[at - FETCH].fetch()
        if FETCH + 1 <= at:
            if at - FETCH - 1 >= 2:
                chunks[at - FETCH - 3].store.wait()
            chunks[at - FETCH - 1].total()
        self.ticks += 1
        self.launch()

    def drain(self):
        count = len(self.chunks)
        while self.ticks < count + FETCH + 1:
            self.tick()
        for chunk in self.chunks[-2:]:
            chunk.store.wait()
        for chunk in self.chunks[-SUMS:]:
            chunk.release()
        for chunk in self.chunks:
            chunk.finish()


class Spread:
    def __init__(self, here, buffer, part, send, receive):
        sibling = here.device(here.z, here.m, 1 - here.k)
        other = (here.device(here.z, here.m, here.k)[0], 1 - here.t)
        self.across, self.beside, self.onward = [], [], []
        for batch in range(2):
            own = buffer.at[pl.ds(here.row(here.k, batch, here.t, part), part)]
            theirs = buffer.at[pl.ds(here.row(here.k, batch, 1 - here.t, part), part)]
            self.across.append(remote(own, own, send.at[batch], receive.at[batch], other))
            self.beside.append(remote(own, own, send.at[2 + batch], receive.at[2 + batch], sibling))
            self.onward.append(
                remote(theirs, theirs, send.at[4 + batch], receive.at[4 + batch], sibling)
            )

    def start(self, batch):
        self.across[batch].start()
        self.beside[batch].start()

    def forward(self):
        for batch in range(2):
            self.across[batch].wait_recv()
            self.onward[batch].start()

    def arrive(self):
        for copy in self.beside + self.onward:
            copy.wait_recv()

    def finish(self):
        for copy in self.across + self.beside + self.onward:
            copy.wait_send()


def backward_kernel(mids, *refs):
    f32, bf16 = jnp.float32, jnp.bfloat16
    (
        rates,
        onehot,
        gains,
        inverse,
        tokens,
        middle,
        cotangent,
        normed_ffn_hbm,
        upstream_hbm,
        normed_hbm,
        act_hbm,
        partial_hbm,
        result_hbm,
        saved_hbm,
        values_hbm,
        weights_hbm,
        out_f,
        out_qkv,
        out_go,
        out_gain,
        grad_tokens,
        result,
        p_f,
        p_qkv,
        p_go,
        p_gain,
        *rest,
    ) = refs
    crossed, landed, rest = rest[:4], rest[4:8], rest[8:]
    (
        normed,
        upstream,
        grad_out,
        act,
        stage,
        own_slot,
        cross_slot,
        sum_slot,
        land_slot,
        out_slot,
        saved,
        values,
        weights,
        projected,
        branch,
        total,
        part,
        part_in,
        across,
        across_in,
        kept,
        grad_middle,
        dot_sum,
        table,
        same,
        columns,
        send,
        receive,
        local,
        row_send,
        row_receive,
        load_sem,
        stage_sem,
        free,
    ) = rest
    rows, width = normed.shape
    half = rows // CORES
    part_rows = half // 4
    length = 2 * part_rows
    heads, units = saved_hbm.shape[0], act_hbm.shape[0]
    here = Place(mids)
    sibling = here.device(here.z, here.m, 1 - here.k)
    other = (here.device(here.z, here.m, here.k)[0], 1 - here.t)
    greet(here.weight_peers() + [other])

    chunks = []
    lists = [(p_f, index, 0, out_f, act.shape[-1]) for index in range(units)]
    for index in range(heads):
        lists.append((p_qkv, index, 1, out_qkv, 3 * LANES))
        lists.append((p_go, index, 2, out_go, 2 * LANES))
    lists.append((p_gain, 0, 3, out_gain, LANES))
    for at, (source, index, kind, output, wide) in enumerate(lists):
        slots = [
            slot.at[(at % slot.shape[0],) + (slice(None),) * (len(slot.shape) - 2) + (pl.ds(0, wide),)]
            for slot in (own_slot, cross_slot, sum_slot, land_slot, out_slot)
        ]
        chunks.append(
            Reduce(
                here,
                source.at[index],
                crossed[kind].at[index],
                landed[kind].at[index],
                output.at[index],
                slots,
                (send.at[at], receive.at[at], local.at[at]),
            )
        )
    reducer = Reducer(chunks)

    def load(source, target, at):
        return pltpu.make_async_copy(source, target, load_sem.at[at])

    loads = {
        "normed_ffn": load(normed_ffn_hbm, normed, 0),
        "upstream": load(upstream_hbm, upstream, 1),
        "part": load(partial_hbm.at[pl.ds(here.k * half, half)], part, 2),
        "normed": load(normed_hbm, normed, 3),
    }
    acts = [load(act_hbm.at[at], act.at[at % 2], 4 + at % 2) for at in range(units)]
    head_loads = [
        (
            load(saved_hbm.at[at], saved.at[at % 2], 6 + at % 2),
            load(values_hbm.at[at], values.at[at % 2], 8 + at % 2),
            load(weights_hbm.at[at], weights.at[at % 2], 10 + at % 2),
        )
        for at in range(heads)
    ]
    loads["normed_ffn"].start()
    acts[0].start()
    loads["upstream"].start()
    loads["part"].start()

    def swap_beside(source, at):
        return remote(source, part_in, row_send.at[12 + at], row_receive.at[12 + at], sibling)

    def swap_across(batch, at):
        block = pl.ds(batch * part_rows, part_rows)
        return remote(
            across.at[block],
            across_in.at[block],
            row_send.at[15 + 2 * at + batch],
            row_receive.at[15 + 2 * at + batch],
            other,
        )

    beside = swap_beside(partial_hbm.at[pl.ds((1 - here.k) * half, half)], 0)
    beside.start()

    down = lax.broadcasted_iota(jnp.int32, (length, length), 0)
    right = lax.broadcasted_iota(jnp.int32, (length, length), 1)
    offset = (down - right).astype(f32)
    for head in range(heads):
        decay = jnp.exp(-rates[head] * jnp.maximum(offset, 0.0))
        table[head] = jnp.where(down >= right, decay, 0.0)
    for sequence in range(rows // length):
        marks = onehot[pl.ds(sequence * length, length), :]
        same[sequence] = dots(marks, marks, 1, 1)

    per_block = 2 * LANES
    group = per_block // (CORES * p_f.shape[4])
    turns = mids // group

    def store_block(slot, at, first, value):
        layer, chip = lax.div(at, turns), lax.rem(at, turns) * group
        shaped = value.astype(bf16).reshape(group, CORES, p_f.shape[4], value.shape[-1])
        stage[slot, layer, pl.ds(chip, group), :, :, pl.ds(first, value.shape[-1])] = shaped

    def stage_out(slot, target):
        wide = target.shape[-1]
        return pltpu.make_async_copy(
            stage.at[slot, :, :, :, :, pl.ds(0, wide)], target, stage_sem.at[slot]
        )

    pending = [None, None]

    def flush(slot):
        if pending[slot] is not None:
            pending[slot].wait()
            pending[slot] = None
            reducer.produce()

    def unit_chunk(at):
        slot = at % 2
        if at + 1 < units:
            acts[at + 1].start()
        acts[at].wait()
        flush(slot)

        @pl.loop(0, width // per_block)
        def _(block):
            where = pl.ds(pl.multiple_of(block * per_block, per_block), per_block)
            store_block(slot, block, 0, dots(normed[:, where], act[slot, :, : 2 * LANES], 0, 0))
            store_block(
                slot, block, 2 * LANES, dots(upstream[:, where], act[slot, :, 2 * LANES :], 0, 0)
            )

        flush(1 - slot)
        pending[slot] = stage_out(slot, p_f.at[at])
        pending[slot].start()

    step_rows = 16

    def row_loop(count):
        return pl.loop(0, count // step_rows)

    def at_rows(base, index):
        return pl.ds(pl.multiple_of(base + index * step_rows, step_rows), step_rows)

    def reduce_beside(own):
        def leave(batch):
            @row_loop(part_rows)
            def _(index):
                base = batch * length + (1 - here.t) * part_rows
                value = own(base, index) + part_in[at_rows(base, index), :].astype(f32)
                across[at_rows(batch * part_rows, index), :] = value.astype(bf16)

        def keep(batch):
            @row_loop(part_rows)
            def _(index):
                base = batch * length + here.t * part_rows
                value = own(base, index) + part_in[at_rows(base, index), :].astype(f32)
                kept[at_rows(batch * part_rows, index), :] = value

        return leave, keep

    loads["normed_ffn"].wait()
    loads["upstream"].wait()
    unit_chunk(0)
    unit_chunk(1)
    loads["part"].wait()
    beside.wait_recv()
    leave, keep = reduce_beside(lambda base, index: part[at_rows(base, index), :].astype(f32))
    crossings = [swap_across(batch, 0) for batch in range(2)]
    for batch in range(2):
        leave(batch)
        crossings[batch].start()
    for batch in range(2):
        keep(batch)
    for at in range(2, 6):
        unit_chunk(at)
    reducer.tick()
    columns[...] = jnp.zeros_like(columns)
    rows_go = Spread(here, grad_out, part_rows, row_send.at[pl.ds(0, 6)], row_receive.at[pl.ds(0, 6)])
    rows_dot = Spread(here, dot_sum, part_rows, row_send.at[pl.ds(6, 6)], row_receive.at[pl.ds(6, 6)])

    for batch in range(2):
        crossings[batch].wait_recv()
        base = here.row(here.k, batch, here.t, part_rows)

        @row_loop(part_rows)
        def _(index):
            here_rows = at_rows(batch * part_rows, index)
            grad = kept[here_rows, :] + across_in[here_rows, :].astype(f32)
            mid = middle[here_rows, :]
            scale = lax.rsqrt(jnp.mean(mid * mid, axis=-1, keepdims=True) + EPSILON)
            unit = mid * scale
            weighted = grad * unit
            columns[1] += weighted[:8] + weighted[8:]
            scaled = grad * gains[1:2, :]
            slope = cotangent[here_rows, :].astype(f32) + scale * (
                scaled - unit * jnp.mean(scaled * unit, axis=-1, keepdims=True)
            )
            grad_middle[here_rows, :] = slope
            rounded = slope.astype(bf16)
            grad_out[at_rows(base, index), :] = rounded
            attended = mid - tokens[here_rows, :].astype(f32)
            inner = jnp.mean(rounded.astype(f32) * attended, axis=-1, keepdims=True)
            dot_sum[at_rows(base, index), :] = jnp.broadcast_to(inner, (step_rows, LANES))

        rows_go.start(batch)
        rows_dot.start(batch)
    for at in range(6, 9):
        unit_chunk(at)
    reducer.tick()
    rows_go.forward()
    rows_dot.forward()
    for at in range(9, units):
        unit_chunk(at)
    for copy in head_loads[0]:
        copy.start()
    loads["normed"].start()
    reducer.tick()
    rows_go.arrive()
    rows_dot.arrive()
    loads["normed"].wait()
    beside.wait_send()
    beside = swap_beside(result_hbm.at[pl.ds((1 - here.k) * half, half)], 1)
    beside.start()
    load_part = load(result_hbm.at[pl.ds(here.k * half, half)], part, 2)
    load_part.start()

    for head in range(heads):
        slot = head % 2
        if head + 1 < heads:
            for copy in head_loads[head + 1]:
                copy.start()
        for copy in head_loads[head]:
            copy.wait()

        @pl.loop(0, rows // length)
        def _(sequence):
            where = pl.ds(pl.multiple_of(sequence * length, length), length)
            query_pre = saved[slot, where, 0:LANES]
            key_pre = saved[slot, where, LANES : 2 * LANES]
            gate = saved[slot, where, 2 * LANES : 3 * LANES]
            scale = inverse[where, :]
            unit = saved[slot, where, 3 * LANES : 4 * LANES] * scale
            grad_branch = dots(grad_out[where, :], weights[slot, :, 4 * LANES :], 1, 0)
            grad_unit = grad_branch * gate
            branch[where, :] = (unit * gate).astype(bf16)
            projected[where, 3 * LANES :] = (grad_branch * unit).astype(bf16)
            grad_mixed = (scale * (grad_unit - unit * dot_sum[where, :])).astype(bf16)
            query_gate = 1.0 / (1.0 + jnp.exp(-query_pre))
            key_gate = 1.0 / (1.0 + jnp.exp(-key_pre))
            queries = (query_pre * query_gate).astype(bf16)
            keys = (key_pre * key_gate).astype(bf16)
            masked = table[head] * same[sequence]
            mixing = (dots(queries, keys, 1, 1) * masked).astype(bf16)
            grad_scores = (
                dots(grad_mixed, values[slot, where, :], 1, 1) * masked
            ).astype(bf16)
            grad_queries = dots(grad_scores, keys, 1, 0)
            grad_keys = dots(grad_scores, queries, 0, 0)
            projected[where, 0:LANES] = (
                grad_queries * (query_gate * (1.0 + query_pre * (1.0 - query_gate)))
            ).astype(bf16)
            projected[where, LANES : 2 * LANES] = (
                grad_keys * (key_gate * (1.0 + key_pre * (1.0 - key_gate)))
            ).astype(bf16)
            projected[where, 2 * LANES : 3 * LANES] = dots(mixing, grad_mixed, 0, 0).astype(bf16)
            product = dots(projected[where, :], weights[slot, :, : 4 * LANES], 1, 1)
            if head == 0:
                total[where, :] = product
            else:
                total[where, :] += product

        flush(0)
        flush(1)
        reducer.tick()

        @pl.loop(0, width // per_block)
        def _(block):
            where = pl.ds(pl.multiple_of(block * per_block, per_block), per_block)
            product = dots(normed[:, where], projected[...], 0, 0)
            store_block(0, block, 0, product[:, : 3 * LANES])
            store_block(1, block, 0, product[:, 3 * LANES :])
            store_block(1, block, LANES, dots(grad_out[:, where], branch[...], 0, 0))

        pending[0] = stage_out(0, p_qkv.at[head])
        pending[1] = stage_out(1, p_go.at[head])
        pending[0].start()
        pending[1].start()
        if head == heads - 1:
            beside.wait_send()

            @row_loop(half)
            def _(index):
                part[at_rows(0, index), :] = total[
                    at_rows((1 - here.k) * half, index), :
                ].astype(bf16)

            pl.semaphore_wait(free.at[0], 1)
            beside = swap_beside(part, 2)
            beside.start()
        flush(0)
        flush(1)
        if head == 0:
            load_part.wait()
            beside.wait_recv()
            leave, keep = reduce_beside(
                lambda base, index: part[at_rows(base, index), :].astype(f32)
            )
            for crossing in crossings:
                crossing.wait_send()
            crossings = [swap_across(batch, 1) for batch in range(2)]
            for batch in range(2):
                leave(batch)
                crossings[batch].start()
            for batch in range(2):
                keep(batch)
            pl.semaphore_signal(free.at[0], inc=1, device_id=sibling, device_id_type=MESH)
        if head == 2:
            for crossing in crossings:
                crossing.wait_recv()
                crossing.wait_send()

            @row_loop(2 * part_rows)
            def _(index):
                here_rows = at_rows(0, index)
                value = kept[here_rows, :] + across_in[here_rows, :].astype(f32)
                across[here_rows, :] = (middle[here_rows, :] + value).astype(bf16)

            store_result = load(across, result, 12)
            store_result.start()
            pl.semaphore_signal(free.at[1], inc=1, device_id=other, device_id_type=MESH)
        if head % 2 == 1:
            reducer.tick()

    beside.wait_recv()
    leave, keep = reduce_beside(
        lambda base, index: total[at_rows(here.k * half + base, index), :]
    )
    crossings = [swap_across(batch, 2) for batch in range(2)]
    store_result.wait()
    pl.semaphore_wait(free.at[1], 1)
    for batch in range(2):
        leave(batch)
        crossings[batch].start()
    for batch in range(2):
        keep(batch)
    reducer.tick()
    for batch in range(2):
        crossings[batch].wait_recv()

        @row_loop(part_rows)
        def _(index):
            here_rows = at_rows(batch * part_rows, index)
            grad = kept[here_rows, :] + across_in[here_rows, :].astype(f32)
            value = tokens[here_rows, :].astype(f32)
            scale = lax.rsqrt(jnp.mean(value * value, axis=-1, keepdims=True) + EPSILON)
            unit = value * scale
            weighted = grad * unit
            columns[0] += weighted[:8] + weighted[8:]
            scaled = grad * gains[0:1, :]
            grad_tokens[here_rows, :] = grad_middle[here_rows, :] + scale * (
                scaled - unit * jnp.mean(scaled * unit, axis=-1, keepdims=True)
            )

    lane = lax.broadcasted_iota(jnp.int32, (8, LANES), 1)

    @pl.loop(0, width // per_block)
    def _(block):
        where = pl.ds(pl.multiple_of(block * per_block, per_block), per_block)
        first = jnp.where(lane == 0, 1.0, 0.0).astype(bf16)
        second = jnp.where(lane == 1, 1.0, 0.0).astype(bf16)
        value = dots(columns[0, :, where].astype(bf16), first, 0, 0)
        value += dots(columns[1, :, where].astype(bf16), second, 0, 0)
        store_block(0, block, 0, value)

    pending[0] = stage_out(0, p_gain.at[0])
    pending[0].start()
    flush(0)
    reducer.drain()
    beside.wait_send()
    for crossing in crossings:
        crossing.wait_send()
    rows_go.finish()
    rows_dot.finish()


def backward(mids, small, large):
    f32, bf16 = jnp.float32, jnp.bfloat16
    shape = jax.ShapeDtypeStruct
    rates, onehot, gains, inverse, tokens, middle, cotangent = small
    normed_ffn, upstream, normed, act, partial, result, saved, values, weights = large
    rows, width = normed.shape
    heads, units = saved.shape[0], act.shape[0]
    block_rows = width // (LAYERS * mids * CORES)
    widths = ((units, 3 * LANES), (heads, 3 * LANES), (heads, 2 * LANES), (1, LANES))
    chunks = sum(count for count, _ in widths)
    hops = mids + (LAYERS - 1) * CORES
    anywhere = pl.BlockSpec(memory_space=pl.ANY)
    vmem = pl.BlockSpec(memory_space=pltpu.VMEM)
    smem = pl.BlockSpec(memory_space=pltpu.SMEM)
    widest = 3 * LANES
    half, own = rows // CORES, rows // (2 * CORES)
    length = own
    outs = [shape((count, CORES, block_rows, wide), f32) for count, wide in widths]
    sums = [shape((count, LAYERS, mids, CORES, block_rows, wide), bf16) for count, wide in widths]
    cross = [
        shape((count, mids - 1, LAYERS, CORES, block_rows, wide), bf16) for count, wide in widths
    ]
    land = [shape((count, CORES, LAYERS, block_rows, wide), bf16) for count, wide in widths]
    return pl.pallas_call(
        functools.partial(backward_kernel, mids),
        name="backward",
        out_shape=(*outs, shape((own, width), f32), shape((own, width), bf16), *sums, *cross, *land),
        in_specs=[smem] + [vmem] * 6 + [anywhere] * 9,
        out_specs=(anywhere,) * 4 + (vmem,) + (anywhere,) * 13,
        scratch_shapes=[
            pltpu.VMEM((rows, width), bf16),
            pltpu.VMEM((rows, width), bf16),
            pltpu.VMEM((rows, width), bf16),
            pltpu.VMEM((2, rows, widest), bf16),
            pltpu.VMEM((2, LAYERS, mids, CORES, block_rows, widest), bf16),
            pltpu.VMEM((2, LAYERS, CORES, block_rows, widest), bf16),
            pltpu.VMEM((2, mids - 1, LAYERS, CORES, block_rows, widest), bf16),
            pltpu.VMEM((SUMS, LAYERS, CORES, block_rows, widest), bf16),
            pltpu.VMEM((2, CORES, LAYERS, block_rows, widest), bf16),
            pltpu.VMEM((2, CORES, block_rows, widest), f32),
            pltpu.VMEM((2, rows, 4 * LANES), f32),
            pltpu.VMEM((2, rows, LANES), bf16),
            pltpu.VMEM((2, width, 5 * LANES), bf16),
            pltpu.VMEM((rows, 4 * LANES), bf16),
            pltpu.VMEM((rows, LANES), bf16),
            pltpu.VMEM((rows, width), f32),
            pltpu.VMEM((half, width), bf16),
            pltpu.VMEM((half, width), bf16),
            pltpu.VMEM((own, width), bf16),
            pltpu.VMEM((own, width), bf16),
            pltpu.VMEM((own, width), f32),
            pltpu.VMEM((own, width), f32),
            pltpu.VMEM((rows, LANES), f32),
            pltpu.VMEM((heads, length, length), f32),
            pltpu.VMEM((rows // length, length, length), f32),
            pltpu.VMEM((2, 8, width), f32),
            pltpu.SemaphoreType.DMA((chunks, hops)),
            pltpu.SemaphoreType.DMA((chunks, hops)),
            pltpu.SemaphoreType.DMA((chunks, 5)),
            pltpu.SemaphoreType.DMA((21,)),
            pltpu.SemaphoreType.DMA((21,)),
            pltpu.SemaphoreType.DMA((13,)),
            pltpu.SemaphoreType.DMA((2,)),
            pltpu.SemaphoreType.REGULAR((2,)),
        ],
        compiler_params=pltpu.CompilerParams(
            collective_id=1, has_side_effects=True, vmem_limit_bytes=63 * 2**20
        ),
    )(*small, *large)[:6]


class Gatherer:
    def __init__(self, chunks):
        self.chunks = chunks
        self.started = self.crossed = 0

    def launch(self):
        while self.started < min(len(self.chunks), self.crossed + AHEAD + 1):
            self.chunks[self.started].start()
            self.started += 1

    def cross(self, count=1):
        for _ in range(count):
            if self.crossed < len(self.chunks):
                self.chunks[self.crossed].cross()
                self.crossed += 1
                self.launch()

    def arrive(self, at):
        self.cross(at + 1 - self.crossed)
        self.chunks[at].arrive()


def forward_kernel(mids, *refs):
    f32, bf16 = jnp.float32, jnp.bfloat16
    (
        rates,
        own_marks,
        tokens,
        cotangent,
        shard_g,
        shard_a,
        shard_f,
        full_g,
        full_a,
        full_f,
        normed_hbm,
        normed_ffn_hbm,
        upstream_hbm,
        act_hbm,
        partial_hbm,
        result_hbm,
        saved_hbm,
        values_hbm,
        marks,
        gains,
        inverse,
        middle,
        normed,
        normed_ffn,
        upstream,
        total,
        grad_total,
        weights,
        out_weights,
        saved,
        values,
        act,
        branch,
        part,
        part_in,
        across,
        across_in,
        kept,
        squares,
        squares_in,
        squares_across,
        squares_across_in,
        table,
        same,
        gain_columns,
        send,
        receive,
        local,
        row_send,
        row_receive,
        load_sem,
        store_sem,
    ) = refs
    rows, width = normed.shape
    half = rows // CORES
    part_rows = half // 4
    length = 2 * part_rows
    heads, units = full_a.shape[0], full_f.shape[0]
    here = Place(mids)
    sibling = here.device(here.z, here.m, 1 - here.k)
    other = (here.device(here.z, here.m, here.k)[0], 1 - here.t)
    greet(here.weight_peers() + [other])

    chunks = []
    for source, target in ((shard_g, full_g), (shard_a, full_a), (shard_f, full_f)):
        for index in range(source.shape[0]):
            at = len(chunks)
            chunks.append(
                Gather(
                    here,
                    source.at[index],
                    target.at[index],
                    (send.at[at], receive.at[at], local.at[at]),
                )
            )
    gatherer = Gatherer(chunks)
    gatherer.launch()

    step_rows = 16

    def row_loop(count):
        return pl.loop(0, count // step_rows)

    def at_rows(base, index):
        return pl.ds(pl.multiple_of(base + index * step_rows, step_rows), step_rows)

    def spread(buffer, at):
        window = pl.ds(6 * at, 6)
        return Spread(here, buffer, part_rows, row_send.at[window], row_receive.at[window])

    rows_normed, rows_up = spread(normed, 0), spread(upstream, 1)
    rows_ffn, rows_inverse = spread(normed_ffn, 2), spread(inverse, 3)
    lone = lambda source, target, at, peer: remote(
        source, target, row_send.at[24 + at], row_receive.at[24 + at], peer
    )

    own_half = pl.ds(pl.multiple_of(here.k * half, half), half)
    far_half = pl.ds(pl.multiple_of((1 - here.k) * half, half), half)
    marks[own_half, :] = own_marks[...]
    marks_copy = lone(own_marks, marks.at[own_half], 0, sibling)
    marks_copy.start()

    gatherer.arrive(0)
    load_gain = pltpu.make_async_copy(full_g.at[0], gain_columns, load_sem.at[0])
    load_gain.start()
    load_gain.wait()
    down = lax.broadcasted_iota(jnp.int32, (8, LANES), 0)
    right = lax.broadcasted_iota(jnp.int32, (8, LANES), 1)
    pick = jnp.where(down == right, 1.0, 0.0).astype(bf16)
    gains[...] = dots(pick, gain_columns[...].reshape(width, LANES), 1, 1)

    for batch in range(2):
        base = here.row(here.k, batch, here.t, part_rows)

        @row_loop(part_rows)
        def _(index):
            here_rows = at_rows(batch * part_rows, index)
            value = tokens[here_rows, :].astype(f32)
            scale = lax.rsqrt(jnp.mean(value * value, axis=-1, keepdims=True) + EPSILON)
            normed[at_rows(base, index), :] = (value * scale * gains[0:1, :]).astype(bf16)

        rows_normed.start(batch)
    for batch in range(2):
        base = here.row(here.k, batch, here.t, part_rows)
        upstream[pl.ds(base, part_rows), :] = cotangent[pl.ds(batch * part_rows, part_rows), :]
        rows_up.start(batch)

    down = lax.broadcasted_iota(jnp.int32, (length, length), 0)
    right = lax.broadcasted_iota(jnp.int32, (length, length), 1)
    offset = (down - right).astype(f32)
    for head in range(heads):
        decay = jnp.exp(-rates[head] * jnp.maximum(offset, 0.0))
        table[head] = jnp.where(down >= right, decay, 0.0)
    marks_copy.wait_recv()
    for sequence in range(rows // length):
        mark = marks[pl.ds(sequence * length, length), :]
        same[sequence] = dots(mark, mark, 1, 1)
    squares[...] = jnp.zeros_like(squares)

    def weight(slot, first, last):
        return weights[slot, :, :, :, :, first * LANES : last * LANES].reshape(
            width, (last - first) * LANES
        )

    def store(source, target, at):
        copy = pltpu.make_async_copy(source, target, store_sem.at[at])
        copy.start()
        return copy

    stores = []
    gatherer.cross()
    rows_normed.forward()
    rows_normed.arrive()
    stores.append(store(normed, normed_hbm, 0))
    gatherer.cross()
    rows_up.forward()

    pending = [[], []]
    for head in range(heads):
        slot = head % 2
        gatherer.arrive(1 + head)
        load = pltpu.make_async_copy(full_a.at[head], weights.at[slot], load_sem.at[slot])
        load_out = pltpu.make_async_copy(
            full_a.at[head, :, :, :, :, pl.ds(4 * LANES, LANES)],
            out_weights.at[:, :, :, :, pl.ds(head * LANES, LANES)],
            load_sem.at[2 + head],
        )
        load.start()
        load_out.start()
        for copy in pending[slot]:
            copy.wait()
        load.wait()

        @pl.loop(0, rows // length)
        def _(sequence):
            where = pl.ds(pl.multiple_of(sequence * length, length), length)
            product = dots(normed[where, :], weight(slot, 0, 4), 1, 0)
            query_pre, key_pre = product[:, :LANES], product[:, LANES : 2 * LANES]
            value = product[:, 2 * LANES : 3 * LANES].astype(bf16)
            gate = product[:, 3 * LANES :]
            queries = (query_pre / (1.0 + jnp.exp(-query_pre))).astype(bf16)
            keys = (key_pre / (1.0 + jnp.exp(-key_pre))).astype(bf16)
            masked = table[head] * same[sequence]
            mixing = (dots(queries, keys, 1, 1) * masked).astype(bf16)
            mixed = dots(mixing, value, 1, 0)
            saved[slot, where, : 2 * LANES] = product[:, : 2 * LANES]
            saved[slot, where, 2 * LANES : 3 * LANES] = gate
            saved[slot, where, 3 * LANES :] = mixed
            values[slot, where, :] = value
            branch[where, head * LANES : (head + 1) * LANES] = (mixed * gate).astype(bf16)
            squares[where, :] += jnp.broadcast_to(
                jnp.sum(mixed * mixed, axis=-1, keepdims=True), (length, LANES)
            )

        pending[slot] = [
            store(saved.at[slot], saved_hbm.at[head], 4 + slot),
            store(values.at[slot], values_hbm.at[head], 6 + slot),
        ]
        load_out.wait()
        gatherer.cross()
    stores += pending[0] + pending[1]

    @pl.loop(0, half // length)
    def _(block):
        base = (1 - here.k) * half + block * length
        where = pl.ds(pl.multiple_of(base, length), length)
        to = pl.ds(pl.multiple_of(block * length, length), length)
        part[to, :] = dots(branch[where, :], out_weights[...].reshape(width, -1), 1, 1).astype(bf16)

    beside = lone(part, part_in, 1, sibling)
    beside.start()
    beside_squares = lone(squares.at[far_half], squares_in, 2, sibling)
    beside_squares.start()

    @pl.loop(0, half // length)
    def _(block):
        base = here.k * half + block * length
        where = pl.ds(pl.multiple_of(base, length), length)
        total[where, :] = dots(branch[where, :], out_weights[...].reshape(width, -1), 1, 1)

    beside.wait_recv()
    beside_squares.wait_recv()
    crossings = []
    for batch in range(2):
        block = pl.ds(batch * part_rows, part_rows)
        crossings.append(
            (
                lone(across.at[block], across_in.at[block], 3 + batch, other),
                lone(squares_across.at[block], squares_across_in.at[block], 5 + batch, other),
            )
        )

        @row_loop(part_rows)
        def _(index):
            base = batch * length + (1 - here.t) * part_rows
            value = total[at_rows(here.k * half + base, index), :]
            value += part_in[at_rows(base, index), :].astype(f32)
            to = at_rows(batch * part_rows, index)
            across[to, :] = value.astype(bf16)
            squares_across[to, :] = (
                squares[at_rows(here.k * half + base, index), :]
                + squares_in[at_rows(base, index), :]
            )

        for copy in crossings[batch]:
            copy.start()
    for batch in range(2):

        @row_loop(part_rows)
        def _(index):
            base = batch * length + here.t * part_rows
            value = total[at_rows(here.k * half + base, index), :]
            to = at_rows(batch * part_rows, index)
            kept[to, :] = value + part_in[at_rows(base, index), :].astype(f32)

    gatherer.cross()
    rows_up.arrive()
    stores.append(store(upstream, upstream_hbm, 1))
    for batch in range(2):
        for copy in crossings[batch]:
            copy.wait_recv()
        base = here.row(here.k, batch, here.t, part_rows)

        @row_loop(part_rows)
        def _(index):
            here_rows = at_rows(batch * part_rows, index)
            from_rows = batch * length + here.t * part_rows
            square = (
                squares[at_rows(here.k * half + from_rows, index), :]
                + squares_in[at_rows(from_rows, index), :]
                + squares_across_in[here_rows, :]
            )
            scale = lax.rsqrt(square / width + EPSILON)
            inverse[at_rows(base, index), :] = scale
            attended = (kept[here_rows, :] + across_in[here_rows, :].astype(f32)) * scale[:, :1]
            mid = tokens[here_rows, :].astype(f32) + attended
            middle[here_rows, :] = mid
            scale = lax.rsqrt(jnp.mean(mid * mid, axis=-1, keepdims=True) + EPSILON)
            normed_ffn[at_rows(base, index), :] = (mid * scale * gains[1:2, :]).astype(bf16)

        rows_ffn.start(batch)
        rows_inverse.start(batch)
    gatherer.cross()
    rows_ffn.forward()
    rows_inverse.forward()
    gatherer.cross()
    rows_ffn.arrive()
    rows_inverse.arrive()
    stores.append(store(normed_ffn, normed_ffn_hbm, 2))

    pending = [None, None]
    for at in range(units):
        slot = at % 2
        gatherer.arrive(1 + heads + at)
        load = pltpu.make_async_copy(
            full_f.at[at], weights.at[slot, :, :, :, :, pl.ds(0, 3 * LANES)], load_sem.at[slot]
        )
        load.start()
        if pending[slot] is not None:
            pending[slot].wait()
        gatherer.cross()
        load.wait()

        @pl.loop(0, rows // length)
        def _(block):
            where = pl.ds(pl.multiple_of(block * length, length), length)
            product = dots(normed_ffn[where, :], weight(slot, 0, 2), 1, 0)
            left, right = product[:, :LANES], product[:, LANES:]
            grad_joined = dots(upstream[where, :], weight(slot, 2, 3), 1, 0)
            act[slot, where, :LANES] = (grad_joined * right).astype(bf16)
            act[slot, where, LANES : 2 * LANES] = (grad_joined * left).astype(bf16)
            act[slot, where, 2 * LANES :] = (left * right).astype(bf16)
            out = dots(act[slot, where, 2 * LANES :], weight(slot, 2, 3), 1, 1)
            grad = dots(act[slot, where, : 2 * LANES], weight(slot, 0, 2), 1, 1)
            if at == 0:
                total[where, :] = out
                grad_total[where, :] = grad
            else:
                total[where, :] += out
                grad_total[where, :] += grad

        pending[slot] = store(act.at[slot], act_hbm.at[at], 8 + slot)

    for copy in stores:
        copy.wait()
    rows_normed.finish()
    rows_ffn.finish()

    @row_loop(rows)
    def _(index):
        normed[at_rows(0, index), :] = grad_total[at_rows(0, index), :].astype(bf16)

    grads = store(normed, partial_hbm, 0)

    @row_loop(rows)
    def _(index):
        normed_ffn[at_rows(0, index), :] = total[at_rows(0, index), :].astype(bf16)

    outs = store(normed_ffn, result_hbm, 1)
    for copy in pending + [grads, outs]:
        copy.wait()
    for chunk in chunks:
        chunk.finish()
    rows_up.finish()
    rows_inverse.finish()
    marks_copy.wait_send()
    beside.wait_send()
    beside_squares.wait_send()
    for pair in crossings:
        for copy in pair:
            copy.wait_send()


def forward(mids, rates, marks, tokens, cotangent, shards):
    f32, bf16 = jnp.float32, jnp.bfloat16
    shape = jax.ShapeDtypeStruct
    own, width = tokens.shape
    rows, half = 4 * own, 2 * own
    length = own
    heads, units = shards[1].shape[0], shards[2].shape[0]
    block_rows = shards[0].shape[2]
    full = [shape((w.shape[0], LAYERS, mids) + w.shape[1:], bf16) for w in shards]
    chunks = 1 + heads + units
    hops = 1 + (LAYERS - 1) * CORES + mids - 1
    anywhere = pl.BlockSpec(memory_space=pl.ANY)
    vmem = pl.BlockSpec(memory_space=pltpu.VMEM)
    smem = pl.BlockSpec(memory_space=pltpu.SMEM)
    block = (LAYERS, mids, CORES, block_rows)
    return pl.pallas_call(
        functools.partial(forward_kernel, mids),
        name="forward",
        out_shape=(
            *full,
            *[shape((rows, width), bf16)] * 3,
            shape((units, rows, 3 * LANES), bf16),
            *[shape((rows, width), bf16)] * 2,
            shape((heads, rows, 4 * LANES), f32),
            shape((heads, rows, LANES), bf16),
            shape((rows, LANES), bf16),
            shape((8, width), f32),
            shape((rows, LANES), f32),
            shape((own, width), f32),
        ),
        in_specs=[smem] + [vmem] * 3 + [anywhere] * 3,
        out_specs=(anywhere,) * 11 + (vmem,) * 4,
        scratch_shapes=[
            pltpu.VMEM((rows, width), bf16),
            pltpu.VMEM((rows, width), bf16),
            pltpu.VMEM((rows, width), bf16),
            pltpu.VMEM((rows, width), f32),
            pltpu.VMEM((rows, width), f32),
            pltpu.VMEM((2, *block, 5 * LANES), bf16),
            pltpu.VMEM((*block, heads * LANES), bf16),
            pltpu.VMEM((2, rows, 4 * LANES), f32),
            pltpu.VMEM((2, rows, LANES), bf16),
            pltpu.VMEM((2, rows, 3 * LANES), bf16),
            pltpu.VMEM((rows, heads * LANES), bf16),
            pltpu.VMEM((half, width), bf16),
            pltpu.VMEM((half, width), bf16),
            pltpu.VMEM((own, width), bf16),
            pltpu.VMEM((own, width), bf16),
            pltpu.VMEM((own, width), f32),
            pltpu.VMEM((rows, LANES), f32),
            pltpu.VMEM((half, LANES), f32),
            pltpu.VMEM((own, LANES), f32),
            pltpu.VMEM((own, LANES), f32),
            pltpu.VMEM((heads, length, length), f32),
            pltpu.VMEM((rows // length, length, length), f32),
            pltpu.VMEM((*block, LANES), bf16),
            pltpu.SemaphoreType.DMA((chunks, hops)),
            pltpu.SemaphoreType.DMA((chunks, hops)),
            pltpu.SemaphoreType.DMA((chunks,)),
            pltpu.SemaphoreType.DMA((31,)),
            pltpu.SemaphoreType.DMA((31,)),
            pltpu.SemaphoreType.DMA((2 + heads,)),
            pltpu.SemaphoreType.DMA((10,)),
        ],
        compiler_params=pltpu.CompilerParams(
            collective_id=0, has_side_effects=True, vmem_limit_bytes=63 * 2**20
        ),
    )(rates, marks, tokens, cotangent, *shards)


def split_heads(weight, halves):
    return weight.reshape(weight.shape[0], CORES, -1, LANES)


def pack(parts):
    joined = jnp.concatenate([split_heads(part, CORES) for part in parts], axis=-1)
    return joined.transpose(2, 1, 0, 3)


def unpack(packed):
    blocks, cores, rows, width = packed.shape
    parts = packed.reshape(blocks, cores, rows, width // LANES, LANES).transpose(3, 2, 1, 0, 4)
    return [parts[index].reshape(rows, -1) for index in range(width // LANES)]


def local(
    mids,
    tokens,
    segment_ids,
    decay_rates,
    gain_attn,
    w_query,
    w_key,
    w_value,
    w_gate,
    w_out,
    gain_ffn,
    w_left,
    w_right,
    w_down,
    cotangent,
):
    f32, bf16 = jnp.float32, jnp.bfloat16
    batches, local_rows, model_width = tokens.shape
    core = lax.rem(lax.axis_index("dp"), CORES)
    heads = decay_rates.shape[0] // CORES
    rates = lax.dynamic_slice_in_dim(decay_rates, core * heads, heads)
    own = lambda values: values.reshape(batches * local_rows, model_width)
    marks = (segment_ids.reshape(-1)[:, None] == jnp.arange(LANES)[None, :]).astype(bf16)
    gain_columns = jnp.pad(
        jnp.stack([gain_attn, gain_ffn], axis=1), ((0, 0), (0, LANES - 2))
    )
    shards = (
        jnp.stack([gain_columns] * CORES)[None],
        pack([w_query, w_key, w_value, w_gate, w_out.T]),
        pack([w_left, w_right, w_down.T]),
    )
    (
        _,
        full_a,
        _,
        normed,
        normed_ffn,
        upstream,
        act,
        partial,
        result,
        saved,
        values,
        marks,
        gains,
        inverse,
        middle,
    ) = forward(mids, rates, marks, own(tokens), own(cotangent), shards)
    full_a = full_a.reshape(heads, model_width, -1)
    of, oqkv, ogo, ogain, grad_tokens, result = backward(
        mids,
        (rates, marks, gains, inverse, own(tokens), middle, own(cotangent)),
        (normed_ffn, upstream, normed, act, partial, result, saved, values, full_a),
    )
    result = result.reshape(tokens.shape)
    grad_tokens = grad_tokens.reshape(tokens.shape)
    grad_gains = lax.psum(jnp.sum(ogain[0], axis=0)[:, :2], "tensor").T
    oa = jnp.concatenate([oqkv, ogo], axis=-1)
    grad_query, grad_key, grad_value, grad_gate_proj, grad_out = unpack(oa)
    grad_w_left, grad_w_right, grad_down = unpack(of)
    return (
        result,
        grad_tokens,
        grad_gains[0],
        grad_query,
        grad_key,
        grad_value,
        grad_gate_proj,
        grad_out.T,
        grad_gains[1],
        grad_w_left,
        grad_w_right,
        grad_down.T,
    )


def solution(mesh):
    return jax.shard_map(
        functools.partial(local, mesh.shape["dp"] // (LAYERS * CORES)),
        mesh=mesh,
        in_specs=(
            P(None, ("dp", "tensor"), None),
            P(None, "dp"),
            P("tensor"),
            P("dp"),
            P("dp", "tensor"),
            P("dp", "tensor"),
            P("dp", "tensor"),
            P("dp", "tensor"),
            P("tensor", "dp"),
            P("dp"),
            P("dp", "tensor"),
            P("dp", "tensor"),
            P("tensor", "dp"),
            P(None, ("dp", "tensor"), None),
        ),
        out_specs=(
            P(None, ("dp", "tensor"), None),
            P(None, ("dp", "tensor"), None),
            P("dp"),
            P("dp", "tensor"),
            P("dp", "tensor"),
            P("dp", "tensor"),
            P("dp", "tensor"),
            P("tensor", "dp"),
            P("dp"),
            P("dp", "tensor"),
            P("dp", "tensor"),
            P("tensor", "dp"),
        ),
        check_vma=False,
    )
```

time: 1500 us -> 818 us (0.55)
  waiting for transfers between devices: 1150 us -> 0 us
  Pallas kernels: 0 us -> 759 us
  matrix products: 170 us -> 0 us
  blocking collectives: 56.5 us -> 7.64 us
  other arithmetic: 39.3 us -> 8.23 us
  local copies, waits for them, and re-layouts: 58.8 us -> 38.3 us
    pallas_call x0 -> x2, Pallas kernels: none -> 759 us  [the longest x1 380 us: forward(): pl.pallas_call(functools.partial(forward_kernel, mids), name='forward', o...]
    all_gather x8 -> x0, waiting for transfers between devices: 471 us -> none  [the longest x1 130 us: fetch_attention(): lax.all_gather(joined_in, 'dp', axis=0, tiled=True)]
    reduce_scatter x6 -> x0, waiting for transfers between devices: 470 us -> none  [the longest x2 408 us: over_dp(): lax.psum_scatter(values.astype(jnp.bfloat16), 'dp', scatter_dimension=dim...]
    unnamed x20 -> x0, waiting for transfers between devices: 212 us -> none
    dot_general x18 -> x0, matrix products: 170 us -> none  [the longest x4 56.4 us: times_transposed(): lax.dot_general(former, latter, (((1,), (1,)), ((), ())), preferred_eleme...]
    all_gather x2 -> x0, blocking collectives: 41.7 us -> none  [the longest x1 23.1 us: fetch_attention(): lax.all_gather(gain_attn, 'dp', axis=0, tiled=True)]
    unnamed x65 -> x35, local copies, waits for them, and re-layouts: 35.1 us -> 18.4 us
  transfers between devices with their start and end apart: 17 -> 0, of which waited for: 16 -> 0; matrix products, arithmetic and copies ran while one was open for 11% -> 0% of each run, Pallas kernels for 0% -> 0%
where the time goes in v2:
time: 818 us; the launch traced here: 814 us
  Pallas kernels  759 us (93%)
  local copies, waits for them, and re-layouts  38.3 us (5%)
  other arithmetic  8.23 us (1%)
    pallas_call x1, Pallas kernels, forward(): pl.pallas_call(functools.partial(forward_kernel, mids), name='forward', o...  380 us
    pallas_call x1, Pallas kernels, backward(): pl.pallas_call(functools.partial(backward_kernel, mids), name='backward',...  379 us
    unnamed x35, local copies, waits for them, and re-layouts  18.4 us

profile of v2, /device:TPU:0, one launch (start us, length us, event | category | flops | bytes accessed | tf_op | source)
XLA Modules:
  0.0 813.9 jit_solution(8892584327570097962)
XLA Ops:
  0.6 0.0 copy-start.6
  0.7 0.0 copy-start.5
  0.7 1.3 dynamic_slice.3.refs_0_
  2.0 0.7 pad_maximum_fusion.1
  2.7 0.7 copy.152
  3.3 0.1 copy.121
  3.5 0.6 maximum_bitcast_fusion.1.refs_4_
  4.1 0.0 copy-start.7
  4.1 0.8 fusion.refs_1_
  4.9 1.1 copy.122
  6.0 0.0 copy-start.4
  6.1 0.2 copy.126
  6.2 1.2 copy.123
  7.4 0.2 copy.127
  7.6 0.0 copy-done.5
  7.6 0.2 copy.124
  7.8 0.2 copy.128
  8.0 0.0 copy-done.6
  8.0 0.2 copy.125
  8.1 0.2 copy.129
  8.3 0.0 copy-done.7
  8.3 0.2 copy.130
  8.5 0.0 copy-done.4
  8.5 0.3 copy.131
  8.9 0.4 copy.133
  9.3 1.5 copy.132
  10.7 0.4 copy.134
  11.1 1.5 copy.135
  12.6 1.8 maximum_bitcast_fusion.refs_6_
  14.3 0.7 constant_dynamic-update-slice_fusion.4
  15.0 0.7 constant_dynamic-update-slice_fusion.3
  15.8 0.7 constant_dynamic-update-slice_fusion.2
  16.5 0.7 constant_dynamic-update-slice_fusion.1
  17.2 0.7 constant_dynamic-update-slice_fusion
  17.9 379.6 %forward.1 = (bf16[1,4,2,2,128,128]{5,4,3,2,1,0:T(8,128)(2,1)}, bf16[4,4,2,2,128,640]{5,4,3,2,1,0:T(8,128)(2,1)}, bf16[11,4,2,2,128,384]{5,4,3,2,1,0:T(8,128)(2,...) custom-call(f32[4]{0:T(128)} %dynamic_slice.3.refs_0_, ...), custom_call_target="tpu_custom_call" | custom-call | tf_op jit(solution)/shard_map/forward/pallas_call | solution.py:1226
  397.6 379.0 %backward.1 = (f32[11,2,128,384]{3,2,1,0:T(8,128)}, f32[4,2,128,384]{3,2,1,0:T(8,128)}, f32[4,2,128,256]{3,2,1,0:T(8,128)}, f32[1,2,128,128]{3,2,1,0:T(8,128)}, ...) custom-call(f32[4]{0:T(128)} %dynamic_slice.3.refs_0_, ...), custom_call_target="tpu_custom_call" | custom-call | tf_op jit(solution)/shard_map/backward/pallas_call | solution.py:785
  776.6 0.9 reduce_sum.9
  777.5 7.6 psum.7
  785.1 0.7 slice_reduce_fusion
  785.8 3.4 pad_maximum_fusion
  789.3 2.1 copy.136
  791.4 1.2 fusion.2
  792.6 0.0 copy-start.1
  792.6 0.8 copy.141
  793.4 0.0 copy-start
  793.5 1.0 copy.149
  794.5 0.0 copy-done.1
  794.5 1.0 copy.148
  795.5 0.0 copy-done
  795.5 1.0 copy.147
  796.6 1.0 copy.146
  797.6 5.7 copy.142
  803.3 2.5 fusion.1
  805.8 1.2 copy.145
  807.0 0.1 copy.144
  807.2 1.5 copy.151
  808.7 0.1 copy.143
  808.8 0.0 copy-start.3
  808.8 1.5 copy.150
  810.4 0.0 copy-done.3
  810.4 0.0 copy-start.2
  810.4 1.0 copy.159
  811.4 1.0 copy-done.2
  812.4 1.3 copy.160
  (6 shorter events, 0.2 us)
Async XLA Ops:
  0.6 7.3 copy-start.6
  0.7 6.9 copy-start.5
  4.1 4.2 copy-start.7
  6.0 2.5 copy-start.4
  792.6 1.9 copy-start.1
  793.4 2.1 copy-start
  808.8 1.6 copy-start.3
  810.4 2.0 copy-start.2

commit v3 on v2

--- a/solution.py
+++ b/solution.py
@@ -11,9 +11,12 @@
 LAYERS = 4
 CORES = 2
 LANES = 128
-AHEAD = 3
+AHEAD = 1
+BEFORE = 3
+LEAD = 2
+BEHIND = 2
 SUMS = 3
-FETCH = 3
+FETCH = 2
 MESH = pl.DeviceIdType.MESH
 
 
@@ -44,7 +47,8 @@
             for core in range(CORES):
                 peers.append(self.device(self.layer(step), self.m, core))
         for step in range(1, self.mids):
-            peers.append(self.device(self.z, self.mid(step), self.k))
+            for core in range(CORES):
+                peers.append(self.device(self.z, self.mid(step), core))
         return peers
 
 
@@ -66,69 +70,165 @@
     )
 
 
+def apart(one, layer):
+    near = jnp.logical_and(one - layer <= 2, layer - one <= 2)
+    return jnp.logical_and(one != layer, near)
+
+
+def relayed(here, layer):
+    first, last = layer == 0, layer == LAYERS - 1
+    if not (first or last):
+        return None, None
+    return (here == LAYERS - 2, LAYERS - 1) if first else (here == 1, 0)
+
+
 class Gather:
     def __init__(self, place, source, target, sems):
-        self.source, self.target = source, target
+        self.place, self.source, self.target = place, source, target
         self.send, self.receive, self.local = sems
         here = place
-        self.hops = []
-        sibling = 1 - here.k
-        own = target.at[here.z, here.m, here.k]
-        self.hops.append(
-            remote(
-                source.at[sibling],
-                own,
-                self.send.at[0],
-                self.receive.at[0],
-                here.device(here.z, here.m, sibling),
-            )
-        )
-        self.arrivals = self.hops[:]
-        for step in range(1, LAYERS):
+        self.own = target.at[here.z, here.m, here.k]
+        self.keep = pltpu.make_async_copy(source.at[here.k], self.own, self.local)
+        self.beside = remote(
+            source.at[1 - here.k],
+            self.own,
+            self.send.at[0],
+            self.receive.at[0],
+            here.device(here.z, here.m, 1 - here.k),
+        )
+        self.sides = 1 + LAYERS * CORES
+        self.crosses = self.sides + (here.mids - 1) * CORES
+
+    @staticmethod
+    def semaphores(mids):
+        return 1 + LAYERS * CORES + (mids - 1) * (CORES + LAYERS)
+
+    def hop(self, layer, core, origin):
+        here = self.place
+        arrival = 1 + (here.z * CORES + here.k if origin is None else origin * CORES + core)
+        return remote(
+            self.source.at[core],
+            self.own,
+            self.send.at[1 + layer * CORES + core],
+            self.receive.at[arrival],
+            here.device(layer, here.m, core),
+        )
+
+    def pass_on(self, layer, core, goal):
+        here = self.place
+        block = self.target.at[layer, here.m, core]
+        return remote(
+            block,
+            block,
+            self.send.at[1 + here.z * CORES + core],
+            self.receive.at[1 + layer * CORES + core],
+            here.device(goal, here.m, here.k),
+        )
+
+    def side(self, step, core, wait):
+        here = self.place
+        at = self.sides + (step - 1) * CORES
+        return remote(
+            self.source.at[core],
+            self.own,
+            self.send.at[at + core],
+            self.receive.at[at + (core if wait else here.k)],
+            here.device(here.z, here.mid(step), core),
+        )
+
+    def crossing(self, step, layer):
+        here = self.place
+        at = self.crosses + (step - 1) * LAYERS + layer
+        block = self.target.at[layer, here.m]
+        return remote(
+            block,
+            block,
+            self.send.at[at],
+            self.receive.at[at],
+            here.device(here.z, here.mid(step), here.k),
+        )
+
+    def start(self):
+        here = self.place
+        self.keep.start()
+        self.beside.start()
+        for step in range(1, here.mids):
             for core in range(CORES):
-                slot = 1 + (step - 1) * CORES
-                hop = functools.partial(
-                    remote,
-                    source.at[core],
-                    own,
-                    self.send.at[slot + core],
-                    peer=here.device(here.layer(step), here.m, core),
-                )
-                self.hops.append(hop(self.receive.at[slot + here.k]))
-                self.arrivals.append(hop(self.receive.at[slot + core]))
-        self.keep = pltpu.make_async_copy(source.at[here.k], own, self.local)
-        base = 1 + (LAYERS - 1) * CORES
-        row = target.at[:, here.m]
-        self.crossings = [
-            remote(
-                row,
-                row,
-                self.send.at[base + step - 1],
-                self.receive.at[base + step - 1],
-                here.device(here.z, here.mid(step), here.k),
-            )
-            for step in range(1, here.mids)
-        ]
-
-    def start(self):
-        self.keep.start()
-        for hop in self.hops:
-            hop.start()
+                self.side(step, core, False).start()
+        for layer in range(LAYERS):
+
+            @pl.when(apart(here.z, layer))
+            def _():
+                for core in range(CORES):
+                    self.hop(layer, core, None).start()
+
+    def relay(self):
+        for layer in (0, LAYERS - 1):
+            mine, goal = relayed(self.place.z, layer)
+
+            @pl.when(mine)
+            def _():
+                for core in range(CORES):
+                    self.hop(layer, core, layer).wait_recv()
+                    self.pass_on(layer, core, goal).start()
 
     def cross(self):
+        here = self.place
+        for layer in range(LAYERS):
+            awaited = here.z != layer
+            mine, _ = relayed(here.z, layer)
+            if mine is not None:
+                awaited = jnp.logical_and(awaited, jnp.logical_not(mine))
+
+            @pl.when(awaited)
+            def _():
+                for core in range(CORES):
+                    self.hop(layer, core, layer).wait_recv()
+
+            @pl.when(here.z != layer)
+            def _():
+                for step in range(1, here.mids):
+                    self.crossing(step, layer).start()
+
+    def arrive(self):
+        here = self.place
         self.keep.wait()
-        for hop in self.arrivals:
-            hop.wait_recv()
-        for crossing in self.crossings:
-            crossing.start()
-
-    def arrive(self):
-        for crossing in self.crossings:
-            crossing.wait_recv()
+        self.beside.wait_recv()
+        for step in range(1, here.mids):
+            for core in range(CORES):
+                self.side(step, core, True).wait_recv()
+        for layer in range(LAYERS):
+
+            @pl.when(here.z != layer)
+            def _():
+                for step in range(1, here.mids):
+                    self.crossing(step, layer).wait_recv()
 
     def finish(self):
-        for hop in self.hops + self.crossings:
-            hop.wait_send()
+        here = self.place
+        self.beside.wait_send()
+        for step in range(1, here.mids):
+            for core in range(CORES):
+                self.side(step, core, False).wait_send()
+        for layer in range(LAYERS):
+
+            @pl.when(apart(here.z, layer))
+            def _():
+                for core in range(CORES):
+                    self.hop(layer, core, None).wait_send()
+
+            mine, goal = relayed(here.z, layer)
+            if mine is not None:
+
+                @pl.when(mine)
+                def _():
+                    for core in range(CORES):
+                        self.pass_on(layer, core, goal).wait_send()
+
+            @pl.when(here.z != layer)
+            def _():
+                for step in range(1, here.mids):
+                    self.crossing(step, layer).wait_send()
 
 
 class Reduce:
@@ -242,10 +342,11 @@
 class Reducer:
     def __init__(self, chunks):
         self.chunks = chunks
+        self.ahead = BEHIND
         self.produced = self.started = self.ticks = 0
 
     def launch(self):
-        while self.started < min(self.produced, self.ticks + AHEAD + 1):
+        while self.started < min(self.produced, self.ticks + self.ahead + 1):
             self.chunks[self.started].start()
             self.started += 1
 
@@ -255,26 +356,27 @@
 
     def tick(self):
         at, chunks = self.ticks, self.chunks
-        count = len(chunks)
+        count, landed = len(chunks), at - FETCH
         if at < count:
             assert at < self.started
             chunks[at].load()
-        if 1 <= at <= count:
-            if at - 1 >= SUMS:
-                chunks[at - 1 - SUMS].release()
-            chunks[at - 1].add()
-        if FETCH <= at < count + FETCH:
-            chunks[at - FETCH].fetch()
-        if FETCH + 1 <= at:
-            if at - FETCH - 1 >= 2:
-                chunks[at - FETCH - 3].store.wait()
-            chunks[at - FETCH - 1].total()
         self.ticks += 1
         self.launch()
+        if 0 <= landed:
+            chunks[landed].fetch()
+        if at < count:
+            if at >= SUMS:
+                chunks[at - SUMS].release()
+            chunks[at].add()
+        if 0 <= landed:
+            if landed >= 2:
+                chunks[landed - 2].store.wait()
+            chunks[landed].total()
 
     def drain(self):
         count = len(self.chunks)
-        while self.ticks < count + FETCH + 1:
+        self.ahead = AHEAD
+        while self.ticks < count + FETCH:
             self.tick()
         for chunk in self.chunks[-2:]:
             chunk.store.wait()
@@ -335,6 +437,7 @@
         saved_hbm,
         values_hbm,
         weights_hbm,
+        weights_go_hbm,
         out_f,
         out_qkv,
         out_go,
@@ -432,7 +535,12 @@
         (
             load(saved_hbm.at[at], saved.at[at % 2], 6 + at % 2),
             load(values_hbm.at[at], values.at[at % 2], 8 + at % 2),
-            load(weights_hbm.at[at], weights.at[at % 2], 10 + at % 2),
+            load(weights_hbm.at[at], weights.at[at % 2, :, pl.ds(0, 3 * LANES)], 10 + at % 2),
+            load(
+                weights_go_hbm.at[at],
+                weights.at[at % 2, :, pl.ds(3 * LANES, 2 * LANES)],
+                13 + at % 2,
+            ),
         )
         for at in range(heads)
     ]
@@ -549,7 +657,8 @@
         keep(batch)
     for at in range(2, 6):
         unit_chunk(at)
-    reducer.tick()
+        if at % 2 == 1:
+            reducer.tick()
     columns[...] = jnp.zeros_like(columns)
     rows_go = Spread(here, grad_out, part_rows, row_send.at[pl.ds(0, 6)], row_receive.at[pl.ds(0, 6)])
     rows_dot = Spread(here, dot_sum, part_rows, row_send.at[pl.ds(6, 6)], row_receive.at[pl.ds(6, 6)])
@@ -582,7 +691,8 @@
         rows_dot.start(batch)
     for at in range(6, 9):
         unit_chunk(at)
-    reducer.tick()
+        if at == 7:
+            reducer.tick()
     rows_go.forward()
     rows_dot.forward()
     for at in range(9, units):
@@ -704,8 +814,7 @@
             store_result = load(across, result, 12)
             store_result.start()
             pl.semaphore_signal(free.at[1], inc=1, device_id=other, device_id_type=MESH)
-        if head % 2 == 1:
-            reducer.tick()
+        reducer.tick()
 
     beside.wait_recv()
     leave, keep = reduce_beside(
@@ -763,7 +872,7 @@
     f32, bf16 = jnp.float32, jnp.bfloat16
     shape = jax.ShapeDtypeStruct
     rates, onehot, gains, inverse, tokens, middle, cotangent = small
-    normed_ffn, upstream, normed, act, partial, result, saved, values, weights = large
+    normed_ffn, upstream, normed, act, partial, result, saved, values, weights, weights_go = large
     rows, width = normed.shape
     heads, units = saved.shape[0], act.shape[0]
     block_rows = width // (LAYERS * mids * CORES)
@@ -786,7 +895,7 @@
         functools.partial(backward_kernel, mids),
         name="backward",
         out_shape=(*outs, shape((own, width), f32), shape((own, width), bf16), *sums, *cross, *land),
-        in_specs=[smem] + [vmem] * 6 + [anywhere] * 9,
+        in_specs=[smem] + [vmem] * 6 + [anywhere] * 10,
         out_specs=(anywhere,) * 4 + (vmem,) + (anywhere,) * 13,
         scratch_shapes=[
             pltpu.VMEM((rows, width), bf16),
@@ -794,10 +903,10 @@
             pltpu.VMEM((rows, width), bf16),
             pltpu.VMEM((2, rows, widest), bf16),
             pltpu.VMEM((2, LAYERS, mids, CORES, block_rows, widest), bf16),
-            pltpu.VMEM((2, LAYERS, CORES, block_rows, widest), bf16),
-            pltpu.VMEM((2, mids - 1, LAYERS, CORES, block_rows, widest), bf16),
+            pltpu.VMEM((1, LAYERS, CORES, block_rows, widest), bf16),
+            pltpu.VMEM((1, mids - 1, LAYERS, CORES, block_rows, widest), bf16),
             pltpu.VMEM((SUMS, LAYERS, CORES, block_rows, widest), bf16),
-            pltpu.VMEM((2, CORES, LAYERS, block_rows, widest), bf16),
+            pltpu.VMEM((1, CORES, LAYERS, block_rows, widest), bf16),
             pltpu.VMEM((2, CORES, block_rows, widest), f32),
             pltpu.VMEM((2, rows, 4 * LANES), f32),
             pltpu.VMEM((2, rows, LANES), bf16),
@@ -820,7 +929,7 @@
             pltpu.SemaphoreType.DMA((chunks, 5)),
             pltpu.SemaphoreType.DMA((21,)),
             pltpu.SemaphoreType.DMA((21,)),
-            pltpu.SemaphoreType.DMA((13,)),
+            pltpu.SemaphoreType.DMA((15,)),
             pltpu.SemaphoreType.DMA((2,)),
             pltpu.SemaphoreType.REGULAR((2,)),
         ],
@@ -833,19 +942,26 @@
 class Gatherer:
     def __init__(self, chunks):
         self.chunks = chunks
-        self.started = self.crossed = 0
+        self.started = self.crossed = self.passed = 0
+
+    def relay(self, at):
+        if at < len(self.chunks) and self.passed == at:
+            self.chunks[at].relay()
+            self.passed += 1
 
     def launch(self):
-        while self.started < min(len(self.chunks), self.crossed + AHEAD + 1):
+        while self.started < min(len(self.chunks), self.crossed + BEFORE + 1):
             self.chunks[self.started].start()
             self.started += 1
 
     def cross(self, count=1):
         for _ in range(count):
             if self.crossed < len(self.chunks):
+                self.relay(self.crossed)
                 self.chunks[self.crossed].cross()
                 self.crossed += 1
                 self.launch()
+                self.relay(self.crossed)
 
     def arrive(self, at):
         self.cross(at + 1 - self.crossed)
@@ -860,10 +976,12 @@
         tokens,
         cotangent,
         shard_g,
-        shard_a,
+        shard_go,
+        shard_qkv,
         shard_f,
         full_g,
-        full_a,
+        full_go,
+        full_qkv,
         full_f,
         normed_hbm,
         normed_ffn_hbm,
@@ -912,24 +1030,26 @@
     half = rows // CORES
     part_rows = half // 4
     length = 2 * part_rows
-    heads, units = full_a.shape[0], full_f.shape[0]
+    heads, units = full_qkv.shape[0], full_f.shape[0]
     here = Place(mids)
     sibling = here.device(here.z, here.m, 1 - here.k)
     other = (here.device(here.z, here.m, here.k)[0], 1 - here.t)
     greet(here.weight_peers() + [other])
 
     chunks = []
-    for source, target in ((shard_g, full_g), (shard_a, full_a), (shard_f, full_f)):
-        for index in range(source.shape[0]):
-            at = len(chunks)
-            chunks.append(
-                Gather(
-                    here,
-                    source.at[index],
-                    target.at[index],
-                    (send.at[at], receive.at[at], local.at[at]),
-                )
+    pairs = [(shard_g, full_g, 0)]
+    for index in range(heads):
+        pairs += [(shard_go, full_go, index), (shard_qkv, full_qkv, index)]
+    pairs += [(shard_f, full_f, index) for index in range(units)]
+    for at, (source, target, index) in enumerate(pairs):
+        chunks.append(
+            Gather(
+                here,
+                source.at[index],
+                target.at[index],
+                (send.at[at], receive.at[at], local.at[at]),
             )
+        )
     gatherer = Gatherer(chunks)
     gatherer.launch()
 
@@ -1015,17 +1135,31 @@
     pending = [[], []]
     for head in range(heads):
         slot = head % 2
-        gatherer.arrive(1 + head)
-        load = pltpu.make_async_copy(full_a.at[head], weights.at[slot], load_sem.at[slot])
+        gatherer.cross(3 + 2 * head + LEAD - gatherer.crossed)
+        gatherer.arrive(1 + 2 * head)
         load_out = pltpu.make_async_copy(
-            full_a.at[head, :, :, :, :, pl.ds(4 * LANES, LANES)],
+            full_go.at[head, :, :, :, :, pl.ds(LANES, LANES)],
             out_weights.at[:, :, :, :, pl.ds(head * LANES, LANES)],
-            load_sem.at[2 + head],
+            load_sem.at[4 + head],
+        )
+        load_gate = pltpu.make_async_copy(
+            full_go.at[head, :, :, :, :, pl.ds(0, LANES)],
+            weights.at[slot, :, :, :, :, pl.ds(3 * LANES, LANES)],
+            load_sem.at[2 + slot],
+        )
+        load_gate.start()
+        gatherer.cross(3 + 2 * head + LEAD - gatherer.crossed)
+        gatherer.arrive(2 + 2 * head)
+        load = pltpu.make_async_copy(
+            full_qkv.at[head],
+            weights.at[slot, :, :, :, :, pl.ds(0, 3 * LANES)],
+            load_sem.at[slot],
         )
         load.start()
         load_out.start()
         for copy in pending[slot]:
             copy.wait()
+        load_gate.wait()
         load.wait()
 
         @pl.loop(0, rows // length)
@@ -1054,7 +1188,6 @@
             store(values.at[slot], values_hbm.at[head], 6 + slot),
         ]
         load_out.wait()
-        gatherer.cross()
     stores += pending[0] + pending[1]
 
     @pl.loop(0, half // length)
@@ -1148,7 +1281,8 @@
     pending = [None, None]
     for at in range(units):
         slot = at % 2
-        gatherer.arrive(1 + heads + at)
+        gatherer.cross(2 + 2 * heads + at + 1 - gatherer.crossed)
+        gatherer.arrive(1 + 2 * heads + at)
         load = pltpu.make_async_copy(
             full_f.at[at], weights.at[slot, :, :, :, :, pl.ds(0, 3 * LANES)], load_sem.at[slot]
         )
@@ -1156,6 +1290,11 @@
         if pending[slot] is not None:
             pending[slot].wait()
         gatherer.cross()
+        if at == units - 1:
+            for copy in stores:
+                copy.wait()
+            rows_normed.finish()
+            rows_ffn.finish()
         load.wait()
 
         @pl.loop(0, rows // length)
@@ -1172,28 +1311,17 @@
             if at == 0:
                 total[where, :] = out
                 grad_total[where, :] = grad
+            elif at == units - 1:
+                normed[where, :] = (total[where, :] + out).astype(bf16)
+                normed_ffn[where, :] = (grad_total[where, :] + grad).astype(bf16)
             else:
                 total[where, :] += out
                 grad_total[where, :] += grad
 
         pending[slot] = store(act.at[slot], act_hbm.at[at], 8 + slot)
 
-    for copy in stores:
-        copy.wait()
-    rows_normed.finish()
-    rows_ffn.finish()
-
-    @row_loop(rows)
-    def _(index):
-        normed[at_rows(0, index), :] = grad_total[at_rows(0, index), :].astype(bf16)
-
-    grads = store(normed, partial_hbm, 0)
-
-    @row_loop(rows)
-    def _(index):
-        normed_ffn[at_rows(0, index), :] = total[at_rows(0, index), :].astype(bf16)
-
-    outs = store(normed_ffn, result_hbm, 1)
+    grads = store(normed_ffn, partial_hbm, 0)
+    outs = store(normed, result_hbm, 1)
     for copy in pending + [grads, outs]:
         copy.wait()
     for chunk in chunks:
@@ -1214,11 +1342,11 @@
     own, width = tokens.shape
     rows, half = 4 * own, 2 * own
     length = own
-    heads, units = shards[1].shape[0], shards[2].shape[0]
+    heads, units = shards[1].shape[0], shards[3].shape[0]
     block_rows = shards[0].shape[2]
     full = [shape((w.shape[0], LAYERS, mids) + w.shape[1:], bf16) for w in shards]
-    chunks = 1 + heads + units
-    hops = 1 + (LAYERS - 1) * CORES + mids - 1
+    chunks = 1 + 2 * heads + units
+    hops = Gather.semaphores(mids)
     anywhere = pl.BlockSpec(memory_space=pl.ANY)
     vmem = pl.BlockSpec(memory_space=pltpu.VMEM)
     smem = pl.BlockSpec(memory_space=pltpu.SMEM)
@@ -1238,15 +1366,15 @@
             shape((rows, LANES), f32),
             shape((own, width), f32),
         ),
-        in_specs=[smem] + [vmem] * 3 + [anywhere] * 3,
-        out_specs=(anywhere,) * 11 + (vmem,) * 4,
+        in_specs=[smem] + [vmem] * 3 + [anywhere] * 4,
+        out_specs=(anywhere,) * 12 + (vmem,) * 4,
         scratch_shapes=[
             pltpu.VMEM((rows, width), bf16),
             pltpu.VMEM((rows, width), bf16),
             pltpu.VMEM((rows, width), bf16),
             pltpu.VMEM((rows, width), f32),
             pltpu.VMEM((rows, width), f32),
-            pltpu.VMEM((2, *block, 5 * LANES), bf16),
+            pltpu.VMEM((2, *block, 4 * LANES), bf16),
             pltpu.VMEM((*block, heads * LANES), bf16),
             pltpu.VMEM((2, rows, 4 * LANES), f32),
             pltpu.VMEM((2, rows, LANES), bf16),
@@ -1269,7 +1397,7 @@
             pltpu.SemaphoreType.DMA((chunks,)),
             pltpu.SemaphoreType.DMA((31,)),
             pltpu.SemaphoreType.DMA((31,)),
-            pltpu.SemaphoreType.DMA((2 + heads,)),
+            pltpu.SemaphoreType.DMA((4 + heads,)),
             pltpu.SemaphoreType.DMA((10,)),
         ],
         compiler_params=pltpu.CompilerParams(
@@ -1322,12 +1450,14 @@
     )
     shards = (
         jnp.stack([gain_columns] * CORES)[None],
-        pack([w_query, w_key, w_value, w_gate, w_out.T]),
+        pack([w_gate, w_out.T]),
+        pack([w_query, w_key, w_value]),
         pack([w_left, w_right, w_down.T]),
     )
     (
         _,
-        full_a,
+        full_go,
+        full_qkv,
         _,
         normed,
         normed_ffn,
@@ -1342,11 +1472,12 @@
         inverse,
         middle,
     ) = forward(mids, rates, marks, own(tokens), own(cotangent), shards)
-    full_a = full_a.reshape(heads, model_width, -1)
+    full_go = full_go.reshape(heads, model_width, -1)
+    full_qkv = full_qkv.reshape(heads, model_width, -1)
     of, oqkv, ogo, ogain, grad_tokens, result = backward(
         mids,
         (rates, marks, gains, inverse, own(tokens), middle, own(cotangent)),
-        (normed_ffn, upstream, normed, act, partial, result, saved, values, full_a),
+        (normed_ffn, upstream, normed, act, partial, result, saved, values, full_qkv, full_go),
     )
     result = result.reshape(tokens.shape)
     grad_tokens = grad_tokens.reshape(tokens.shape)

time: 818 us -> 770 us (0.941)
  Pallas kernels: 759 us -> 710 us
    pallas_call x1, Pallas kernels: 380 us -> 353 us  [forward(): pl.pallas_call(functools.partial(forward_kernel, mids), name='forward', o...]
    pallas_call x1, Pallas kernels: 379 us -> 357 us  [backward(): pl.pallas_call(functools.partial(backward_kernel, mids), name='backward',...]
    unnamed x35 -> x31, local copies, waits for them, and re-layouts: 18.4 us -> 15.2 us
where the time goes in v3:
time: 770 us; the launch traced here: 765 us
  Pallas kernels  710 us (92%)
  local copies, waits for them, and re-layouts  34.7 us (5%)
  other arithmetic  10 us (1%)
  blocking collectives  9.3 us (1%)
    pallas_call x1, Pallas kernels, backward(): pl.pallas_call(functools.partial(backward_kernel, mids), name='backward',...  357 us
    pallas_call x1, Pallas kernels, forward(): pl.pallas_call(functools.partial(forward_kernel, mids), name='forward', o...  353 us

profile of v3, /device:TPU:0, one launch (start us, length us, event | category | flops | bytes accessed | tf_op | source)
XLA Modules:
  0.0 765.2 jit_solution(789056601212430690)
XLA Ops:
  0.6 0.0 copy-start.6
  0.7 0.0 copy-start.5
  0.7 1.3 dynamic_slice.3.refs_0_
  2.0 0.7 pad_maximum_fusion.1
  2.7 0.7 copy.152
  3.3 0.1 copy.121
  3.5 0.6 maximum_bitcast_fusion.3.refs_4_
  4.1 0.8 fusion.refs_1_
  4.9 1.1 copy.125
  6.0 0.0 copy-start.7
  6.1 0.2 copy.128
  6.2 1.1 copy.126
  7.4 0.2 copy.129
  7.6 0.0 copy-done.5
  7.6 0.0 copy-start.3
  7.6 0.2 copy.127
  7.7 0.2 copy.130
  7.9 1.0 maximum_bitcast_fusion.1.refs_6_
  8.9 0.0 copy-done.6
  8.9 0.2 copy.122
  9.1 0.0 copy-start.4
  9.1 0.2 copy.123
  9.3 0.0 copy-done.7
  9.3 0.2 copy.124
  9.5 0.9 maximum_bitcast_fusion.2.refs_5_
  10.4 0.0 copy-done.3
  10.4 0.3 copy.131
  10.7 0.4 copy.133
  11.1 0.0 copy-done.4
  11.1 0.3 copy.132
  11.4 0.4 copy.134
  11.8 1.5 copy.135
  13.3 1.7 maximum_bitcast_fusion.refs_7_
  15.0 353.1 %forward.1 = (bf16[1,4,2,2,128,128]{5,4,3,2,1,0:T(8,128)(2,1)}, bf16[4,4,2,2,128,256]{5,4,3,2,1,0:T(8,128)(2,1)}, bf16[4,4,2,2,128,384]{5,4,3,2,1,0:T(8,128)(2,1...) custom-call(f32[4]{0:T(128)} %dynamic_slice.3.refs_0_, ...), custom_call_target="tpu_custom_call" | custom-call | tf_op jit(solution)/shard_map/forward/pallas_call | solution.py:1354
  368.1 356.7 %backward.1 = (f32[11,2,128,384]{3,2,1,0:T(8,128)}, f32[4,2,128,384]{3,2,1,0:T(8,128)}, f32[4,2,128,256]{3,2,1,0:T(8,128)}, f32[1,2,128,128]{3,2,1,0:T(8,128)}, ...) custom-call(f32[4]{0:T(128)} %dynamic_slice.3.refs_0_, ...), custom_call_target="tpu_custom_call" | custom-call | tf_op jit(solution)/shard_map/backward/pallas_call | solution.py:894
  724.9 0.9 reduce_sum.9
  725.8 9.3 %psum.7 = f32[2,128]{0,1:T(8,128)S(1)} all-reduce(f32[2,128]{0,1:T(8,128)S(1)} %slice_bitcast_fusion), channel_id=1, replica_groups=mesh['dp'=16,'tensor'=2] {'tensor'}, use_global_device_ids=true, to_apply=%region_1.2 | all-reduce | flops 256 | bytes 2048 | tf_op jit(solution)/shard_map/psum | solution.py:1484
  735.1 0.7 slice_reduce_fusion
  735.8 3.4 pad_maximum_fusion
  739.2 2.4 copy.136
  741.7 1.2 fusion.2
  742.8 0.0 copy-start.1
  742.8 0.0 copy-start
  742.8 0.8 copy.141
  743.7 1.0 copy.149
  744.7 0.0 copy-done.1
  744.7 1.0 copy.148
  745.7 0.0 copy-done
  745.8 1.0 copy.147
  746.8 1.0 copy.146
  747.8 5.7 copy.142
  753.5 2.5 fusion.1
  756.1 1.2 copy.145
  757.2 0.1 copy.144
  757.4 1.5 copy.151
  758.9 0.1 copy.143
  759.1 0.0 copy-start.2
  759.1 1.5 copy.150
  760.6 0.0 copy-done.2
  760.6 1.0 copy.155
  761.6 3.1 copy.156
  (6 shorter events, 0.2 us)
Async XLA Ops:
  0.6 8.3 %copy-start.6 = (bf16[128,1024]{1,0:T(8,128)(2,1)S(1)}, bf16[128,1024]{1,0:T(8,128)(2,1)}, u32[]{:S(2)}) copy-start(bf16[128,1024]{1,0:T(8,128)(2,1)} %param.21) | copy-start | bytes 786436
  0.7 6.9 copy-start.5
  6.0 3.3 copy-start.7
  7.6 2.8 copy-start.3
  9.1 2.0 copy-start.4
  742.8 1.9 copy-start.1
  742.8 2.9 copy-start
  759.1 1.6 copy-start.2

commit v4 on v3

--- a/solution.py
+++ b/solution.py
@@ -12,11 +12,12 @@
 CORES = 2
 LANES = 128
 AHEAD = 1
-BEFORE = 3
-LEAD = 2
+BEFORE = 4
+LEAD = 3
+SIDEWAYS = (9, 13)
 BEHIND = 2
-SUMS = 3
-FETCH = 2
+SUMS = 4
+FETCH = 3
 MESH = pl.DeviceIdType.MESH
 
 
@@ -83,9 +84,10 @@
 
 
 class Gather:
-    def __init__(self, place, source, target, sems):
+    def __init__(self, place, source, target, sems, sideways):
         self.place, self.source, self.target = place, source, target
         self.send, self.receive, self.local = sems
+        self.sideways = sideways
         here = place
         self.own = target.at[here.z, here.m, here.k]
         self.keep = pltpu.make_async_copy(source.at[here.k], self.own, self.local)
@@ -172,7 +174,31 @@
                     self.hop(layer, core, layer).wait_recv()
                     self.pass_on(layer, core, goal).start()
 
-    def cross(self):
+    def climb(self, step, layer):
+        here = self.place
+        at = self.crosses + (step - 1) * LAYERS
+        block = self.target.at[here.z, here.mid(step)]
+        return remote(
+            block,
+            block,
+            self.send.at[at + layer],
+            self.receive.at[at + here.z],
+            here.device(layer, here.m, here.k),
+        )
+
+    def climbed(self, step, layer, goal):
+        here = self.place
+        at = self.crosses + (step - 1) * LAYERS
+        block = self.target.at[layer, here.mid(step)]
+        return remote(
+            block,
+            block,
+            self.send.at[at + here.z],
+            self.receive.at[at + layer],
+            here.device(goal, here.m, here.k),
+        )
+
+    def wait_layers(self, then):
         here = self.place
         for layer in range(LAYERS):
             awaited = here.z != layer
@@ -185,15 +211,61 @@
                 for core in range(CORES):
                     self.hop(layer, core, layer).wait_recv()
 
+            then(layer)
+
+    def cross(self):
+        here = self.place
+        if self.sideways:
+            for step in range(1, here.mids):
+                for core in range(CORES):
+                    self.side(step, core, True).wait_recv()
+            for layer in range(LAYERS):
+
+                @pl.when(apart(here.z, layer))
+                def _():
+                    for step in range(1, here.mids):
+                        self.climb(step, layer).start()
+
+            return
+
+        def send_on(layer):
             @pl.when(here.z != layer)
             def _():
                 for step in range(1, here.mids):
                     self.crossing(step, layer).start()
 
+        self.wait_layers(send_on)
+
+    def relay_on(self):
+        if self.sideways:
+            here = self.place
+            for layer in (0, LAYERS - 1):
+                mine, goal = relayed(here.z, layer)
+
+                @pl.when(mine)
+                def _():
+                    for step in range(1, here.mids):
+                        self.climbed(step, layer, goal).wait_recv()
+                        self.climbed(step, layer, goal).start()
+
     def arrive(self):
         here = self.place
         self.keep.wait()
         self.beside.wait_recv()
+        if self.sideways:
+            self.wait_layers(lambda layer: None)
+            for layer in range(LAYERS):
+                awaited = here.z != layer
+                mine, _ = relayed(here.z, layer)
+                if mine is not None:
+                    awaited = jnp.logical_and(awaited, jnp.logical_not(mine))
+
+                @pl.when(awaited)
+                def _():
+                    for step in range(1, here.mids):
+                        self.climbed(step, layer, layer).wait_recv()
+
+            return
         for step in range(1, here.mids):
             for core in range(CORES):
                 self.side(step, core, True).wait_recv()
@@ -216,6 +288,9 @@
             def _():
                 for core in range(CORES):
                     self.hop(layer, core, None).wait_send()
+                if self.sideways:
+                    for step in range(1, here.mids):
+                        self.climb(step, layer).wait_send()
 
             mine, goal = relayed(here.z, layer)
             if mine is not None:
@@ -224,61 +299,95 @@
                 def _():
                     for core in range(CORES):
                         self.pass_on(layer, core, goal).wait_send()
-
-            @pl.when(here.z != layer)
-            def _():
-                for step in range(1, here.mids):
-                    self.crossing(step, layer).wait_send()
+                    if self.sideways:
+                        for step in range(1, here.mids):
+                            self.climbed(step, layer, goal).wait_send()
+
+            if not self.sideways:
+
+                @pl.when(here.z != layer)
+                def _():
+                    for step in range(1, here.mids):
+                        self.crossing(step, layer).wait_send()
 
 
 class Reduce:
-    def __init__(self, place, source, crossed, landed, output, slots, sems):
+    def __init__(self, place, source, crossed, landed, passed, stores, slots, sems):
         self.place, self.source, self.crossed, self.landed = place, source, crossed, landed
-        self.output = output
-        self.own_slot, self.cross_slot, self.sum_slot, self.land_slot, self.out_slot = slots
-        send, receive, local = sems
+        self.passed = passed
+        (
+            self.own_slot,
+            self.cross_slot,
+            self.sum_slot,
+            self.land_slot,
+            self.out_slot,
+            self.turn_slot,
+            self.pass_slot,
+        ) = slots
+        self.send, self.receive, local = sems
         here = place
         self.crossings = [
             remote(
                 source.at[:, here.mid(step)],
                 crossed.at[step - 1],
-                send.at[step - 1],
-                receive.at[step - 1],
+                self.send.at[step - 1],
+                self.receive.at[step - 1],
                 here.device(here.z, here.mid(step), here.k),
             )
             for step in range(1, here.mids)
         ]
-        base = here.mids - 1
-        sibling = 1 - here.k
-        self.hops = [
-            remote(
-                self.sum_slot.at[here.z, sibling],
-                landed.at[here.k, 0],
-                send.at[base],
-                receive.at[base],
-                here.device(here.z, here.m, sibling),
-            )
-        ]
-        self.arrivals = self.hops[:]
-        for step in range(1, LAYERS):
-            for core in range(CORES):
-                slot = base + 1 + (step - 1) * CORES
-                hop = functools.partial(
-                    remote,
-                    self.sum_slot.at[here.layer(step), core],
-                    landed.at[here.k, step],
-                    send.at[slot + core],
-                    peer=here.device(here.layer(step), here.m, core),
-                )
-                self.hops.append(hop(receive.at[slot + here.k]))
-                self.arrivals.append(hop(receive.at[slot + core]))
+        self.base = here.mids
+        self.beside = remote(
+            self.sum_slot.at[here.z, 1 - here.k],
+            landed.at[here.k, here.z],
+            self.send.at[here.mids - 1],
+            self.receive.at[here.mids - 1],
+            here.device(here.z, here.m, 1 - here.k),
+        )
         self.keep = pltpu.make_async_copy(
-            self.sum_slot.at[here.z, here.k], landed.at[here.k, 0], local.at[0]
+            self.sum_slot.at[here.z, here.k], landed.at[here.k, here.z], local.at[0]
         )
         self.load_own = pltpu.make_async_copy(source.at[:, here.m], self.own_slot, local.at[1])
         self.load_cross = pltpu.make_async_copy(crossed, self.cross_slot, local.at[2])
         self.load_land = pltpu.make_async_copy(landed, self.land_slot, local.at[3])
-        self.store = pltpu.make_async_copy(self.out_slot, output, local.at[4])
+        self.load_pass = pltpu.make_async_copy(passed, self.pass_slot, local.at[4])
+        self.turned = self.turn_slot is not None
+        self.stores = [
+            pltpu.make_async_copy(piece(self.out_slot, self.turn_slot), target, local.at[5 + at])
+            for at, (piece, target) in enumerate(stores)
+        ]
+
+    @staticmethod
+    def semaphores(mids):
+        return mids + LAYERS * CORES + 1
+
+    def hop(self, layer, core, origin):
+        here = self.place
+        arrival = here.z * CORES + here.k if origin is None else origin * CORES + core
+        return remote(
+            self.sum_slot.at[layer, core],
+            self.landed.at[here.k, here.z],
+            self.send.at[self.base + layer * CORES + core],
+            self.receive.at[self.base + arrival],
+            here.device(layer, here.m, core),
+        )
+
+    def far(self, layer, goal):
+        here = self.place
+        at = self.base + LAYERS * CORES
+        return remote(
+            self.sum_slot.at[layer],
+            self.passed,
+            self.send.at[at],
+            self.receive.at[at],
+            here.device(goal, here.m, here.k),
+        )
+
+    def ends(self):
+        return (
+            (self.place.z == 0, LAYERS - 1, LAYERS - 2),
+            (self.place.z == LAYERS - 1, 0, 1),
+        )
 
     def start(self):
         for crossing in self.crossings:
@@ -291,6 +400,7 @@
         self.load_cross.start()
 
     def add(self):
+        here = self.place
         self.load_own.wait()
         self.load_cross.wait()
 
@@ -298,35 +408,98 @@
         def _(at):
             layer, core = lax.div(at, CORES), lax.rem(at, CORES)
             total = self.own_slot[layer, core].astype(jnp.float32)
-            for step in range(1, self.place.mids):
+            for step in range(1, here.mids):
                 total += self.cross_slot[step - 1, layer, core].astype(jnp.float32)
             self.sum_slot[layer, core] = total.astype(jnp.bfloat16)
 
+        for end, layer, goal in self.ends():
+
+            @pl.when(end)
+            def _():
+                self.far(layer, goal).start()
+
         self.keep.start()
-        for hop in self.hops:
-            hop.start()
+        self.beside.start()
+        for layer in range(LAYERS):
+            now = apart(here.z, layer)
+            if layer in (0, LAYERS - 1):
+                now = jnp.logical_and(now, here.z != (1 if layer == 0 else LAYERS - 2))
+
+            @pl.when(now)
+            def _():
+                for core in range(CORES):
+                    self.hop(layer, core, None).start()
+
+    def relay(self):
+        for _, layer, goal in self.ends():
+
+            @pl.when(self.place.z == goal)
+            def _():
+                self.far(layer, goal).wait_recv()
+                self.load_pass.start()
+                self.load_pass.wait()
+
+                @pl.loop(0, CORES)
+                def _(core):
+                    total = self.sum_slot[layer, core].astype(jnp.float32)
+                    total += self.pass_slot[core].astype(jnp.float32)
+                    self.sum_slot[layer, core] = total.astype(jnp.bfloat16)
+
+                for core in range(CORES):
+                    self.hop(layer, core, None).start()
 
     def release(self):
-        for hop in self.hops:
-            hop.wait_send()
+        self.beside.wait_send()
+        for layer in range(LAYERS):
+
+            @pl.when(apart(self.place.z, layer))
+            def _():
+                for core in range(CORES):
+                    self.hop(layer, core, None).wait_send()
+
+        for end, layer, goal in self.ends():
+
+            @pl.when(end)
+            def _():
+                self.far(layer, goal).wait_send()
 
     def fetch(self):
         self.keep.wait()
-        for hop in self.arrivals:
-            hop.wait_recv()
+        self.beside.wait_recv()
+        for layer in range(LAYERS):
+
+            @pl.when(apart(self.place.z, layer))
+            def _():
+                for core in range(CORES):
+                    self.hop(layer, core, layer).wait_recv()
+
         self.load_land.start()
 
     def total(self):
         self.load_land.wait()
+        here = self.place
+        present = [
+            jnp.logical_or(here.z == layer, apart(here.z, layer)) for layer in range(LAYERS)
+        ]
 
         @pl.loop(0, CORES)
         def _(core):
-            total = self.land_slot[core, 0].astype(jnp.float32)
-            for step in range(1, LAYERS):
-                total += self.land_slot[core, step].astype(jnp.float32)
+            total = None
+            for layer in range(LAYERS):
+                value = self.land_slot[core, layer].astype(jnp.float32)
+                if layer in (0, LAYERS - 1):
+                    value = jnp.where(present[layer], value, 0.0)
+                total = value if total is None else total + value
             self.out_slot[core] = total
-
-        self.store.start()
+            if self.turned:
+                self.turn_slot[core] = total[:, -LANES:].T
+
+        for store in self.stores:
+            store.start()
+
+    def stored(self):
+        for store in self.stores:
+            store.wait()
 
     def finish(self):
         for crossing in self.crossings:
@@ -356,12 +529,14 @@
 
     def tick(self):
         at, chunks = self.ticks, self.chunks
-        count, landed = len(chunks), at - FETCH
+        count, passed, landed = len(chunks), at - 1, at - FETCH
         if at < count:
             assert at < self.started
             chunks[at].load()
         self.ticks += 1
         self.launch()
+        if 0 <= passed < count:
+            chunks[passed].relay()
         if 0 <= landed:
             chunks[landed].fetch()
         if at < count:
@@ -370,7 +545,7 @@
             chunks[at].add()
         if 0 <= landed:
             if landed >= 2:
-                chunks[landed - 2].store.wait()
+                chunks[landed - 2].stored()
             chunks[landed].total()
 
     def drain(self):
@@ -379,7 +554,7 @@
         while self.ticks < count + FETCH:
             self.tick()
         for chunk in self.chunks[-2:]:
-            chunk.store.wait()
+            chunk.stored()
         for chunk in self.chunks[-SUMS:]:
             chunk.release()
         for chunk in self.chunks:
@@ -438,9 +613,14 @@
         values_hbm,
         weights_hbm,
         weights_go_hbm,
-        out_f,
-        out_qkv,
-        out_go,
+        out_query,
+        out_key,
+        out_value,
+        out_gate,
+        out_out,
+        out_left,
+        out_right,
+        out_down,
         out_gain,
         grad_tokens,
         result,
@@ -450,7 +630,7 @@
         p_gain,
         *rest,
     ) = refs
-    crossed, landed, rest = rest[:4], rest[4:8], rest[8:]
+    crossed, landed, passed, rest = rest[:4], rest[4:8], rest[8:12], rest[12:]
     (
         normed,
         upstream,
@@ -462,6 +642,9 @@
         sum_slot,
         land_slot,
         out_slot,
+        turn_slot,
+        pass_slot,
+        gain_slot,
         saved,
         values,
         weights,
@@ -498,23 +681,52 @@
     greet(here.weight_peers() + [other])
 
     chunks = []
-    lists = [(p_f, index, 0, out_f, act.shape[-1]) for index in range(units)]
+    lists = []
+
+    def columns_of(target, index, count, place):
+        for core in range(CORES):
+            where = pl.ds((core * count + index) * LANES, LANES)
+            yield (
+                lambda out, turn, core=core: out.at[core, :, pl.ds(place * LANES, LANES)],
+                target.at[:, where],
+            )
+
+    def rows_of(target, index, count):
+        for core in range(CORES):
+            where = pl.ds((core * count + index) * LANES, LANES)
+            yield (lambda out, turn, core=core: turn.at[core], target.at[where])
+
+    for index in range(units):
+        stores = [
+            *columns_of(out_left, index, units, 0),
+            *columns_of(out_right, index, units, 1),
+            *rows_of(out_down, index, units),
+        ]
+        lists.append((p_f, index, 0, stores, True))
     for index in range(heads):
-        lists.append((p_qkv, index, 1, out_qkv, 3 * LANES))
-        lists.append((p_go, index, 2, out_go, 2 * LANES))
-    lists.append((p_gain, 0, 3, out_gain, LANES))
-    for at, (source, index, kind, output, wide) in enumerate(lists):
+        stores = []
+        for place, target in enumerate((out_query, out_key, out_value)):
+            stores += columns_of(target, index, heads, place)
+        lists.append((p_qkv, index, 1, stores, False))
+        stores = [*columns_of(out_gate, index, heads, 0), *rows_of(out_out, index, heads)]
+        lists.append((p_go, index, 2, stores, True))
+    lists.append((p_gain, 0, 3, [], False))
+    for at, (source, index, kind, stores, turned) in enumerate(lists):
+        wide = source.shape[-1]
         slots = [
             slot.at[(at % slot.shape[0],) + (slice(None),) * (len(slot.shape) - 2) + (pl.ds(0, wide),)]
             for slot in (own_slot, cross_slot, sum_slot, land_slot, out_slot)
         ]
+        slots.append(turn_slot.at[at % 2] if turned else None)
+        slots.append(pass_slot.at[:, :, pl.ds(0, wide)])
         chunks.append(
             Reduce(
                 here,
                 source.at[index],
                 crossed[kind].at[index],
                 landed[kind].at[index],
-                output.at[index],
+                passed[kind].at[index],
+                stores,
                 slots,
                 (send.at[at], receive.at[at], local.at[at]),
             )
@@ -861,6 +1073,15 @@
     pending[0].start()
     flush(0)
     reducer.drain()
+    gain_sum = chunks[-1].out_slot[0] + chunks[-1].out_slot[1]
+    gain_slot[0] = gain_sum
+    gain_copy = remote(
+        gain_slot.at[0], gain_slot.at[1], row_send.at[21], row_receive.at[21], other
+    )
+    gain_copy.start()
+    gain_copy.wait_recv()
+    out_gain[...] = (gain_sum + gain_slot[1]).T[:8]
+    gain_copy.wait_send()
     beside.wait_send()
     for crossing in crossings:
         crossing.wait_send()
@@ -878,14 +1099,18 @@
     block_rows = width // (LAYERS * mids * CORES)
     widths = ((units, 3 * LANES), (heads, 3 * LANES), (heads, 2 * LANES), (1, LANES))
     chunks = sum(count for count, _ in widths)
-    hops = mids + (LAYERS - 1) * CORES
+    hops = Reduce.semaphores(mids)
     anywhere = pl.BlockSpec(memory_space=pl.ANY)
     vmem = pl.BlockSpec(memory_space=pltpu.VMEM)
     smem = pl.BlockSpec(memory_space=pltpu.SMEM)
     widest = 3 * LANES
     half, own = rows // CORES, rows // (2 * CORES)
     length = own
-    outs = [shape((count, CORES, block_rows, wide), f32) for count, wide in widths]
+    inner, outer = CORES * heads * LANES, CORES * units * LANES
+    outs = [shape((block_rows, inner), f32)] * 4 + [shape((inner, block_rows), f32)]
+    outs += [shape((block_rows, outer), f32)] * 2 + [shape((outer, block_rows), f32)]
+    outs.append(shape((8, block_rows), f32))
+    passed = [shape((count, CORES, block_rows, wide), bf16) for count, wide in widths]
     sums = [shape((count, LAYERS, mids, CORES, block_rows, wide), bf16) for count, wide in widths]
     cross = [
         shape((count, mids - 1, LAYERS, CORES, block_rows, wide), bf16) for count, wide in widths
@@ -894,9 +1119,9 @@
     return pl.pallas_call(
         functools.partial(backward_kernel, mids),
         name="backward",
-        out_shape=(*outs, shape((own, width), f32), shape((own, width), bf16), *sums, *cross, *land),
+        out_shape=(*outs, shape((own, width), f32), shape((own, width), bf16), *sums, *cross, *land, *passed),
         in_specs=[smem] + [vmem] * 6 + [anywhere] * 10,
-        out_specs=(anywhere,) * 4 + (vmem,) + (anywhere,) * 13,
+        out_specs=(anywhere,) * 8 + (vmem,) * 2 + (anywhere,) * 17,
         scratch_shapes=[
             pltpu.VMEM((rows, width), bf16),
             pltpu.VMEM((rows, width), bf16),
@@ -908,6 +1133,9 @@
             pltpu.VMEM((SUMS, LAYERS, CORES, block_rows, widest), bf16),
             pltpu.VMEM((1, CORES, LAYERS, block_rows, widest), bf16),
             pltpu.VMEM((2, CORES, block_rows, widest), f32),
+            pltpu.VMEM((2, CORES, LANES, block_rows), f32),
+            pltpu.VMEM((CORES, block_rows, widest), bf16),
+            pltpu.VMEM((2, block_rows, LANES), f32),
             pltpu.VMEM((2, rows, 4 * LANES), f32),
             pltpu.VMEM((2, rows, LANES), bf16),
             pltpu.VMEM((2, width, 5 * LANES), bf16),
@@ -926,9 +1154,9 @@
             pltpu.VMEM((2, 8, width), f32),
             pltpu.SemaphoreType.DMA((chunks, hops)),
             pltpu.SemaphoreType.DMA((chunks, hops)),
-            pltpu.SemaphoreType.DMA((chunks, 5)),
-            pltpu.SemaphoreType.DMA((21,)),
-            pltpu.SemaphoreType.DMA((21,)),
+            pltpu.SemaphoreType.DMA((chunks, 11)),
+            pltpu.SemaphoreType.DMA((22,)),
+            pltpu.SemaphoreType.DMA((22,)),
             pltpu.SemaphoreType.DMA((15,)),
             pltpu.SemaphoreType.DMA((2,)),
             pltpu.SemaphoreType.REGULAR((2,)),
@@ -936,13 +1164,18 @@
         compiler_params=pltpu.CompilerParams(
             collective_id=1, has_side_effects=True, vmem_limit_bytes=63 * 2**20
         ),
-    )(*small, *large)[:6]
+    )(*small, *large)[:11]
 
 
 class Gatherer:
     def __init__(self, chunks):
         self.chunks = chunks
-        self.started = self.crossed = self.passed = 0
+        self.started = self.crossed = self.passed = self.climbed = 0
+
+    def relay_on(self, last):
+        while self.climbed < last:
+            self.chunks[self.climbed].relay_on()
+            self.climbed += 1
 
     def relay(self, at):
         if at < len(self.chunks) and self.passed == at:
@@ -962,9 +1195,11 @@
                 self.crossed += 1
                 self.launch()
                 self.relay(self.crossed)
+                self.relay_on(self.crossed - 1)
 
     def arrive(self, at):
         self.cross(at + 1 - self.crossed)
+        self.relay_on(at + 1)
         self.chunks[at].arrive()
 
 
@@ -1048,6 +1283,7 @@
                 source.at[index],
                 target.at[index],
                 (send.at[at], receive.at[at], local.at[at]),
+                at in SIDEWAYS,
             )
         )
     gatherer = Gatherer(chunks)
@@ -1415,12 +1651,6 @@
     return joined.transpose(2, 1, 0, 3)
 
 
-def unpack(packed):
-    blocks, cores, rows, width = packed.shape
-    parts = packed.reshape(blocks, cores, rows, width // LANES, LANES).transpose(3, 2, 1, 0, 4)
-    return [parts[index].reshape(rows, -1) for index in range(width // LANES)]
-
-
 def local(
     mids,
     tokens,
@@ -1474,30 +1704,19 @@
     ) = forward(mids, rates, marks, own(tokens), own(cotangent), shards)
     full_go = full_go.reshape(heads, model_width, -1)
     full_qkv = full_qkv.reshape(heads, model_width, -1)
-    of, oqkv, ogo, ogain, grad_tokens, result = backward(
+    *grads, grad_gains, grad_tokens, result = backward(
         mids,
         (rates, marks, gains, inverse, own(tokens), middle, own(cotangent)),
         (normed_ffn, upstream, normed, act, partial, result, saved, values, full_qkv, full_go),
     )
     result = result.reshape(tokens.shape)
-    grad_tokens = grad_tokens.reshape(tokens.shape)
-    grad_gains = lax.psum(jnp.sum(ogain[0], axis=0)[:, :2], "tensor").T
-    oa = jnp.concatenate([oqkv, ogo], axis=-1)
-    grad_query, grad_key, grad_value, grad_gate_proj, grad_out = unpack(oa)
-    grad_w_left, grad_w_right, grad_down = unpack(of)
     return (
         result,
-        grad_tokens,
+        grad_tokens.reshape(tokens.shape),
         grad_gains[0],
-        grad_query,
-        grad_key,
-        grad_value,
-        grad_gate_proj,
-        grad_out.T,
+        *grads[:5],
         grad_gains[1],
-        grad_w_left,
-        grad_w_right,
-        grad_down.T,
+        *grads[5:],
     )
 
 

time: 770 us -> 739 us (0.960)
  local copies, waits for them, and re-layouts: 34.7 us -> 20.8 us
  blocking collectives: 9.3 us -> 0 us
    pallas_call x1, Pallas kernels: 353 us -> 341 us  [forward(): pl.pallas_call(functools.partial(forward_kernel, mids), name='forward', o...]
    psum x1 -> x0, blocking collectives: 9.3 us -> none  [local(): grad_gains = lax.psum(jnp.sum(ogain[0], axis=0)[:, :2], 'tensor').T]
    pallas_call x1, Pallas kernels: 357 us -> 365 us  [backward(): pl.pallas_call(functools.partial(backward_kernel, mids), name='backward',...]
    unnamed x31 -> x45, local copies, waits for them, and re-layouts: 15.2 us -> 16 us
where the time goes in v4:
time: 739 us; the launch traced here: 734 us
  Pallas kernels  706 us (96%)
  local copies, waits for them, and re-layouts  20.8 us (3%)
    pallas_call x1, Pallas kernels, backward(): pl.pallas_call(functools.partial(backward_kernel, mids), name='backward',...  365 us
    pallas_call x1, Pallas kernels, forward(): pl.pallas_call(functools.partial(forward_kernel, mids), name='forward', o...  341 us
    unnamed x45, local copies, waits for them, and re-layouts  16 us

profile of v4, /device:TPU:0, one launch (start us, length us, event | category | flops | bytes accessed | tf_op | source)
XLA Modules:
  0.0 733.8 jit_solution(9930920930322114969)
XLA Ops:
  0.6 0.0 copy-start.13
  0.7 0.0 copy-start.12
  0.7 1.3 dynamic_slice.3.refs_0_
  2.0 0.7 pad_maximum_fusion
  2.7 0.7 copy.59
  3.3 0.1 copy.44
  3.5 0.6 maximum_bitcast_fusion.3.refs_4_
  4.1 0.8 fusion.refs_1_
  4.9 1.1 copy.48
  6.0 0.2 copy.51
  6.2 0.0 copy-start.4
  6.2 1.2 copy.49
  7.4 0.2 copy.52
  7.6 1.1 copy.50
  8.8 0.2 copy.53
  8.9 1.0 maximum_bitcast_fusion.1.refs_6_
  9.9 0.0 copy-done.12
  9.9 0.0 copy-start.5
  9.9 0.2 copy.45
  10.1 0.2 copy.46
  10.3 0.0 copy-done.13
  10.3 0.2 copy.47
  10.5 0.9 maximum_bitcast_fusion.2.refs_5_
  11.4 0.0 copy-done.4
  11.4 0.0 copy-start.6
  11.4 0.3 copy.54
  11.7 0.4 copy.56
  12.1 0.0 copy-done.5
  12.1 0.3 copy.55
  12.4 0.4 copy.57
  12.8 0.0 copy-done.6
  12.8 0.4 copy.58
  13.2 1.7 maximum_bitcast_fusion.refs_7_
  14.9 340.6 %forward.1 = (bf16[1,4,2,2,128,128]{5,4,3,2,1,0:T(8,128)(2,1)}, bf16[4,4,2,2,128,256]{5,4,3,2,1,0:T(8,128)(2,1)}, bf16[4,4,2,2,128,384]{5,4,3,2,1,0:T(8,128)(2,1...) custom-call(f32[4]{0:T(128)} %dynamic_slice.3.refs_0_, ...), custom_call_target="tpu_custom_call" | custom-call | tf_op jit(solution)/shard_map/forward/pallas_call | solution.py:1590
  355.5 365.5 %backward.1 = (f32[128,1024]{1,0:T(8,128)}, f32[128,1024]{1,0:T(8,128)}, f32[128,1024]{1,0:T(8,128)}, f32[128,1024]{1,0:T(8,128)}, f32[1024,128]{1,0:T(8,128)}, ...) custom-call(f32[4]{0:T(128)} %dynamic_slice.3.refs_0_, ...), custom_call_target="tpu_custom_call" | custom-call | tf_op jit(solution)/shard_map/backward/pallas_call | solution.py:1119
  721.0 0.0 copy-start
  721.0 1.4 slice_bitcast_fusion
  722.3 0.0 copy-start.11
  722.3 2.4 copy.70
  724.7 0.0 copy-done
  724.7 0.0 copy-start.10
  724.7 0.0 copy-start.9
  724.7 0.0 copy-start.8
  724.7 1.3 copy.71
  726.0 0.0 copy-done.11
  726.0 0.0 copy-start.7
  726.0 0.0 copy-start.3
  726.0 0.8 copy.72
  726.8 0.0 copy-done.10
  726.8 0.8 copy.73
  727.6 0.0 copy-done.9
  727.6 0.0 copy-start.2
  727.6 0.8 copy.74
  728.4 0.0 copy-done.8
  728.4 0.8 copy.75
  729.2 0.0 copy-done.7
  729.2 0.8 copy.76
  730.0 0.0 copy-done.3
  730.0 0.0 copy-start.1
  730.0 1.1 copy.77
  731.1 0.0 copy-done.2
  731.1 1.1 copy.78
  732.2 0.0 copy-done.1
  732.2 1.1 copy.79
  (1 shorter events, 0.0 us)
Async XLA Ops:
  0.6 9.7 %copy-start.13 = (bf16[1024,128]{1,0:T(8,128)(2,1)S(1)}, bf16[1024,128]{1,0:T(8,128)(2,1)}, u32[]{:S(2)}) copy-start(bf16[1024,128]{1,0:T(8,128)(2,1)} %param.22) | copy-start | bytes 786436
  0.7 9.3 %copy-start.12 = (bf16[128,1024]{1,0:T(8,128)(2,1)S(1)}, bf16[128,1024]{1,0:T(8,128)(2,1)}, u32[]{:S(2)}) copy-start(bf16[128,1024]{1,0:T(8,128)(2,1)} %param.21) | copy-start | bytes 786436
  6.2 5.1 copy-start.4
  9.9 2.1 copy-start.5
  11.4 1.4 copy-start.6
  721.0 3.7 copy-start
  722.3 3.7 copy-start.11
  724.7 2.1 copy-start.10
  724.7 2.9 copy-start.9
  724.7 3.7 copy-start.8
  726.0 3.2 copy-start.7
  726.0 4.0 copy-start.3
  727.6 3.5 copy-start.2
  730.0 2.2 copy-start.1

commit v5 on v4

--- a/solution.py
+++ b/solution.py
@@ -15,9 +15,14 @@
 BEFORE = 4
 LEAD = 3
 SIDEWAYS = (9, 13)
+SLICE = 32
+CLIMBS = {0: 4}
+EARLY = 6
+NEAR = 2
+LAG = 2
 BEHIND = 2
-SUMS = 4
-FETCH = 3
+SUMS = 6
+FETCH = 5
 MESH = pl.DeviceIdType.MESH
 
 
@@ -312,6 +317,8 @@
 
 
 class Reduce:
+    sideways = False
+
     def __init__(self, place, source, crossed, landed, passed, stores, slots, sems):
         self.place, self.source, self.crossed, self.landed = place, source, crossed, landed
         self.passed = passed
@@ -359,7 +366,7 @@
 
     @staticmethod
     def semaphores(mids):
-        return mids + LAYERS * CORES + 1
+        return max(mids + LAYERS * CORES + 1, LAYERS + 2 + (mids - 1) * CORES)
 
     def hop(self, layer, core, origin):
         here = self.place
@@ -407,10 +414,14 @@
         @pl.loop(0, LAYERS * CORES)
         def _(at):
             layer, core = lax.div(at, CORES), lax.rem(at, CORES)
-            total = self.own_slot[layer, core].astype(jnp.float32)
-            for step in range(1, here.mids):
-                total += self.cross_slot[step - 1, layer, core].astype(jnp.float32)
-            self.sum_slot[layer, core] = total.astype(jnp.bfloat16)
+
+            @pl.loop(0, self.own_slot.shape[2] // SLICE)
+            def _(index):
+                where = pl.ds(pl.multiple_of(index * SLICE, SLICE), SLICE)
+                total = self.own_slot[layer, core, where].astype(jnp.float32)
+                for step in range(1, here.mids):
+                    total += self.cross_slot[step - 1, layer, core, where].astype(jnp.float32)
+                self.sum_slot[layer, core, where] = total.astype(jnp.bfloat16)
 
         for end, layer, goal in self.ends():
 
@@ -506,6 +517,220 @@
             crossing.wait_send()
 
 
+class Climb(Reduce):
+    sideways = True
+
+    def __init__(self, place, source, climbed, landed, passed, stores, slots, sems):
+        self.place, self.source, self.climbed_to, self.landed = place, source, climbed, landed
+        self.passed = passed
+        (
+            self.own_slot,
+            self.climb_slot,
+            self.sum_slot,
+            self.land_slot,
+            self.out_slot,
+            self.turn_slot,
+            self.pass_slot,
+            self.pass_sum,
+        ) = slots
+        self.send, self.receive, self.local = sems
+        here = place
+        self.turned = self.turn_slot is not None
+        self.beside = remote(
+            self.sum_slot.at[here.m, 1 - here.k],
+            landed.at[here.k, 0],
+            self.send.at[LAYERS + 1],
+            self.receive.at[LAYERS + 1],
+            here.device(here.z, here.m, 1 - here.k),
+        )
+        local = self.local
+        self.keep = pltpu.make_async_copy(
+            self.sum_slot.at[here.m, here.k], landed.at[here.k, 0], local.at[0]
+        )
+        self.load_own = pltpu.make_async_copy(source.at[here.z], self.own_slot, local.at[1])
+        self.load_climbed = pltpu.make_async_copy(climbed, self.climb_slot, local.at[2])
+        self.load_land = pltpu.make_async_copy(landed, self.land_slot, local.at[3])
+        self.stores = [
+            pltpu.make_async_copy(piece(self.out_slot, self.turn_slot), target, local.at[5 + at])
+            for at, (piece, target) in enumerate(stores)
+        ]
+
+    def up(self, layer, block):
+        here = self.place
+        return remote(
+            block,
+            self.climbed_to.at[here.z],
+            self.send.at[layer],
+            self.receive.at[here.z],
+            here.device(layer, here.m, here.k),
+        )
+
+    def come(self, layer):
+        here = self.place
+        block = self.climbed_to.at[layer]
+        return remote(
+            block,
+            block,
+            self.send.at[layer],
+            self.receive.at[layer],
+            here.device(layer, here.m, here.k),
+        )
+
+    def far(self, layer, goal):
+        here = self.place
+        return remote(
+            self.source.at[layer],
+            self.passed,
+            self.send.at[LAYERS],
+            self.receive.at[LAYERS],
+            here.device(goal, here.m, here.k),
+        )
+
+    def across(self, step, core, wait):
+        here = self.place
+        at = LAYERS + 2 + (step - 1) * CORES
+        return remote(
+            self.sum_slot.at[here.mid(step), core],
+            self.landed.at[here.k, step],
+            self.send.at[at + core],
+            self.receive.at[at + (core if wait else here.k)],
+            here.device(here.z, here.mid(step), core),
+        )
+
+    def now(self, layer):
+        now = apart(self.place.z, layer)
+        if layer in (0, LAYERS - 1):
+            now = jnp.logical_and(now, self.place.z != (1 if layer == 0 else LAYERS - 2))
+        return now
+
+    def start(self):
+        for end, layer, goal in self.ends():
+
+            @pl.when(end)
+            def _():
+                self.far(layer, goal).start()
+
+        for layer in range(LAYERS):
+
+            @pl.when(self.now(layer))
+            def _():
+                self.up(layer, self.source.at[layer]).start()
+
+    def relay_up(self):
+        here = self.place
+        for _, layer, goal in self.ends():
+
+            @pl.when(here.z == goal)
+            def _():
+                self.far(layer, goal).wait_recv()
+                loads = (
+                    pltpu.make_async_copy(self.passed, self.pass_slot, self.local.at[4]),
+                    pltpu.make_async_copy(
+                        self.source.at[layer], self.pass_sum, self.local.at[11]
+                    ),
+                )
+                for copy in loads:
+                    copy.start()
+                for copy in loads:
+                    copy.wait()
+
+                @pl.loop(0, here.mids * CORES)
+                def _(at):
+                    mid, core = lax.div(at, CORES), lax.rem(at, CORES)
+                    total = self.pass_sum[mid, core].astype(jnp.float32)
+                    total += self.pass_slot[mid, core].astype(jnp.float32)
+                    self.pass_sum[mid, core] = total.astype(jnp.bfloat16)
+
+                self.up(layer, self.pass_sum).start()
+
+    def load(self):
+        self.load_own.start()
+        for layer in range(LAYERS):
+
+            @pl.when(apart(self.place.z, layer))
+            def _():
+                self.come(layer).wait_recv()
+
+        self.load_climbed.start()
+
+    def add(self):
+        here = self.place
+        self.load_own.wait()
+        self.load_climbed.wait()
+        present = [apart(here.z, layer) for layer in range(LAYERS)]
+
+        @pl.loop(0, here.mids * CORES)
+        def _(at):
+            mid, core = lax.div(at, CORES), lax.rem(at, CORES)
+            total = self.own_slot[mid, core].astype(jnp.float32)
+            for layer in range(LAYERS):
+                value = self.climb_slot[layer, mid, core].astype(jnp.float32)
+                total += jnp.where(present[layer], value, 0.0)
+            self.sum_slot[mid, core] = total.astype(jnp.bfloat16)
+
+        for step in range(1, here.mids):
+            for core in range(CORES):
+                self.across(step, core, False).start()
+        self.keep.start()
+        self.beside.start()
+
+    def relay(self):
+        pass
+
+    def release(self):
+        here = self.place
+        self.beside.wait_send()
+        for step in range(1, here.mids):
+            for core in range(CORES):
+                self.across(step, core, False).wait_send()
+        for layer in range(LAYERS):
+
+            @pl.when(apart(here.z, layer))
+            def _():
+                self.up(layer, self.source.at[layer]).wait_send()
+
+        for end, layer, goal in self.ends():
+
+            @pl.when(end)
+            def _():
+                self.far(layer, goal).wait_send()
+
+    def fetch(self):
+        self.keep.wait()
+        self.beside.wait_recv()
+        for step in range(1, self.place.mids):
+            for core in range(CORES):
+                here = self.place
+                at = LAYERS + 2 + (step - 1) * CORES + core
+                block = self.landed.at[core, step]
+                remote(
+                    block,
+                    block,
+                    self.send.at[at],
+                    self.receive.at[at],
+                    here.device(here.z, here.mid(step), core),
+                ).wait_recv()
+        self.load_land.start()
+
+    def total(self):
+        self.load_land.wait()
+
+        @pl.loop(0, CORES)
+        def _(core):
+            total = self.land_slot[core, 0].astype(jnp.float32)
+            for step in range(1, self.place.mids):
+                total += self.land_slot[core, step].astype(jnp.float32)
+            self.out_slot[core] = total
+            if self.turned:
+                self.turn_slot[core] = total[:, -LANES:].T
+
+        for store in self.stores:
+            store.start()
+
+    def finish(self):
+        pass
+
+
 def dots(left, right, left_axis, right_axis):
     return lax.dot_general(
         left, right, (((left_axis,), (right_axis,)), ((), ())), preferred_element_type=jnp.float32
@@ -513,45 +738,64 @@
 
 
 class Reducer:
-    def __init__(self, chunks):
-        self.chunks = chunks
-        self.ahead = BEHIND
-        self.produced = self.started = self.ticks = 0
+    def __init__(self, chunks, keys):
+        self.chunks, self.keys = chunks, keys
+        self.ahead, self.fetch = BEHIND, FETCH
+        self.ticks = self.landed = 0
+        self.produced, self.started, self.relayed = set(), set(), set()
 
     def launch(self):
-        while self.started < min(self.produced, self.ticks + self.ahead + 1):
-            self.chunks[self.started].start()
-            self.started += 1
-
-    def produce(self):
-        self.produced += 1
+        blocked = False
+        for at, chunk in enumerate(self.chunks):
+            if at in self.started:
+                continue
+            ready = at in self.produced
+            if chunk.sideways:
+                ready = ready and at <= self.ticks + EARLY
+            else:
+                blocked = blocked or not ready or at > self.ticks + self.ahead
+                ready = not blocked
+            if ready:
+                chunk.start()
+                self.started.add(at)
+
+    def relay_up(self, at):
+        if at in self.started and self.chunks[at].sideways and at not in self.relayed:
+            self.relayed.add(at)
+            self.chunks[at].relay_up()
+
+    def produce(self, key):
+        self.produced.add(self.keys.index(key))
         self.launch()
 
     def tick(self):
         at, chunks = self.ticks, self.chunks
-        count, passed, landed = len(chunks), at - 1, at - FETCH
+        count = len(chunks)
         if at < count:
-            assert at < self.started
+            assert at in self.started
+            self.relay_up(at)
             chunks[at].load()
         self.ticks += 1
         self.launch()
-        if 0 <= passed < count:
-            chunks[passed].relay()
-        if 0 <= landed:
-            chunks[landed].fetch()
+        for near in range(at + 1, min(at + 1 + NEAR, count)):
+            self.relay_up(near)
+        if 0 <= at - LAG < count:
+            chunks[at - LAG].relay()
         if at < count:
             if at >= SUMS:
                 chunks[at - SUMS].release()
             chunks[at].add()
-        if 0 <= landed:
-            if landed >= 2:
-                chunks[landed - 2].stored()
-            chunks[landed].total()
+        while self.landed <= min(at - self.fetch, count - 1):
+            chunks[self.landed].fetch()
+            if self.landed >= 2:
+                chunks[self.landed - 2].stored()
+            chunks[self.landed].total()
+            self.landed += 1
 
     def drain(self):
         count = len(self.chunks)
-        self.ahead = AHEAD
-        while self.ticks < count + FETCH:
+        self.ahead, self.fetch = AHEAD, LAG + 1
+        while self.landed < count:
             self.tick()
         for chunk in self.chunks[-2:]:
             chunk.stored()
@@ -630,7 +874,7 @@
         p_gain,
         *rest,
     ) = refs
-    crossed, landed, passed, rest = rest[:4], rest[4:8], rest[8:12], rest[12:]
+    crossed, landed, passed, side, rest = rest[:4], rest[4:8], rest[8:12], rest[12:15], rest[15:]
     (
         normed,
         upstream,
@@ -645,6 +889,12 @@
         turn_slot,
         pass_slot,
         gain_slot,
+        side_own,
+        side_climb,
+        side_sum,
+        side_land,
+        side_pass,
+        side_pass_sum,
         saved,
         values,
         weights,
@@ -696,7 +946,10 @@
             where = pl.ds((core * count + index) * LANES, LANES)
             yield (lambda out, turn, core=core: turn.at[core], target.at[where])
 
-    for index in range(units):
+    order = [index for index in range(units) if index not in CLIMBS]
+    for index, place in CLIMBS.items():
+        order.insert(place, index)
+    for index in order:
         stores = [
             *columns_of(out_left, index, units, 0),
             *columns_of(out_right, index, units, 1),
@@ -713,6 +966,28 @@
     lists.append((p_gain, 0, 3, [], False))
     for at, (source, index, kind, stores, turned) in enumerate(lists):
         wide = source.shape[-1]
+        if kind == 0 and index in CLIMBS:
+            nth = list(CLIMBS).index(index)
+            chunks.append(
+                Climb(
+                    here,
+                    source.at[index],
+                    *[buffer.at[nth] for buffer in side],
+                    stores,
+                    (
+                        side_own,
+                        side_climb,
+                        side_sum,
+                        side_land,
+                        out_slot.at[at % 2],
+                        turn_slot.at[at % 2],
+                        side_pass,
+                        side_pass_sum,
+                    ),
+                    (send.at[at], receive.at[at], local.at[at]),
+                )
+            )
+            continue
         slots = [
             slot.at[(at % slot.shape[0],) + (slice(None),) * (len(slot.shape) - 2) + (pl.ds(0, wide),)]
             for slot in (own_slot, cross_slot, sum_slot, land_slot, out_slot)
@@ -731,7 +1006,7 @@
                 (send.at[at], receive.at[at], local.at[at]),
             )
         )
-    reducer = Reducer(chunks)
+    reducer = Reducer(chunks, [(kind, index) for _, index, kind, _, _ in lists])
 
     def load(source, target, at):
         return pltpu.make_async_copy(source, target, load_sem.at[at])
@@ -745,14 +1020,10 @@
     acts = [load(act_hbm.at[at], act.at[at % 2], 4 + at % 2) for at in range(units)]
     head_loads = [
         (
-            load(saved_hbm.at[at], saved.at[at % 2], 6 + at % 2),
-            load(values_hbm.at[at], values.at[at % 2], 8 + at % 2),
-            load(weights_hbm.at[at], weights.at[at % 2, :, pl.ds(0, 3 * LANES)], 10 + at % 2),
-            load(
-                weights_go_hbm.at[at],
-                weights.at[at % 2, :, pl.ds(3 * LANES, 2 * LANES)],
-                13 + at % 2,
-            ),
+            load(saved_hbm.at[at], saved.at[0], 6),
+            load(values_hbm.at[at], values.at[0], 8),
+            load(weights_hbm.at[at], weights.at[0, :, pl.ds(0, 3 * LANES)], 10),
+            load(weights_go_hbm.at[at], weights.at[0, :, pl.ds(3 * LANES, 2 * LANES)], 13),
         )
         for at in range(heads)
     ]
@@ -777,6 +1048,84 @@
     beside = swap_beside(partial_hbm.at[pl.ds((1 - here.k) * half, half)], 0)
     beside.start()
 
+    per_block = 2 * LANES
+    group = per_block // (CORES * p_f.shape[4])
+    turns = mids // group
+
+    def store_block(slot, at, first, value):
+        layer, chip = lax.div(at, turns), lax.rem(at, turns) * group
+        shaped = value.astype(bf16).reshape(group, CORES, p_f.shape[4], value.shape[-1])
+        stage[slot, layer, pl.ds(chip, group), :, :, pl.ds(first, value.shape[-1])] = shaped
+
+    def stage_out(slot, target):
+        wide = target.shape[-1]
+        return pltpu.make_async_copy(
+            stage.at[slot, :, :, :, :, pl.ds(0, wide)], target, stage_sem.at[slot]
+        )
+
+    pending = [None, None]
+
+    def send_stage(slot, target, kind, index):
+        copy = stage_out(slot, target.at[index])
+        copy.start()
+        pending[slot] = (copy, (kind, index))
+
+    def flush(slot):
+        if pending[slot] is not None:
+            copy, key = pending[slot]
+            copy.wait()
+            pending[slot] = None
+            reducer.produce(key)
+
+    def unit_chunk(at):
+        slot = at % 2
+        if at + 1 < units:
+            acts[at + 1].start()
+        acts[at].wait()
+        flush(slot)
+
+        @pl.loop(0, width // per_block)
+        def _(block):
+            where = pl.ds(pl.multiple_of(block * per_block, per_block), per_block)
+            store_block(slot, block, 0, dots(normed[:, where], act[slot, :, : 2 * LANES], 0, 0))
+            store_block(
+                slot, block, 2 * LANES, dots(upstream[:, where], act[slot, :, 2 * LANES :], 0, 0)
+            )
+
+        flush(1 - slot)
+        send_stage(slot, p_f, 0, at)
+        if at < 2:
+            flush(slot)
+
+    step_rows = 16
+
+    def row_loop(count):
+        return pl.loop(0, count // step_rows)
+
+    def at_rows(base, index):
+        return pl.ds(pl.multiple_of(base + index * step_rows, step_rows), step_rows)
+
+    def reduce_beside(own):
+        def leave(batch):
+            @row_loop(part_rows)
+            def _(index):
+                base = batch * length + (1 - here.t) * part_rows
+                value = own(base, index) + part_in[at_rows(base, index), :].astype(f32)
+                across[at_rows(batch * part_rows, index), :] = value.astype(bf16)
+
+        def keep(batch):
+            @row_loop(part_rows)
+            def _(index):
+                base = batch * length + here.t * part_rows
+                value = own(base, index) + part_in[at_rows(base, index), :].astype(f32)
+                kept[at_rows(batch * part_rows, index), :] = value
+
+        return leave, keep
+
+    loads["normed_ffn"].wait()
+    loads["upstream"].wait()
+    unit_chunk(0)
+    unit_chunk(1)
     down = lax.broadcasted_iota(jnp.int32, (length, length), 0)
     right = lax.broadcasted_iota(jnp.int32, (length, length), 1)
     offset = (down - right).astype(f32)
@@ -787,77 +1136,6 @@
         marks = onehot[pl.ds(sequence * length, length), :]
         same[sequence] = dots(marks, marks, 1, 1)
 
-    per_block = 2 * LANES
-    group = per_block // (CORES * p_f.shape[4])
-    turns = mids // group
-
-    def store_block(slot, at, first, value):
-        layer, chip = lax.div(at, turns), lax.rem(at, turns) * group
-        shaped = value.astype(bf16).reshape(group, CORES, p_f.shape[4], value.shape[-1])
-        stage[slot, layer, pl.ds(chip, group), :, :, pl.ds(first, value.shape[-1])] = shaped
-
-    def stage_out(slot, target):
-        wide = target.shape[-1]
-        return pltpu.make_async_copy(
-            stage.at[slot, :, :, :, :, pl.ds(0, wide)], target, stage_sem.at[slot]
-        )
-
-    pending = [None, None]
-
-    def flush(slot):
-        if pending[slot] is not None:
-            pending[slot].wait()
-            pending[slot] = None
-            reducer.produce()
-
-    def unit_chunk(at):
-        slot = at % 2
-        if at + 1 < units:
-            acts[at + 1].start()
-        acts[at].wait()
-        flush(slot)
-
-        @pl.loop(0, width // per_block)
-        def _(block):
-            where = pl.ds(pl.multiple_of(block * per_block, per_block), per_block)
-            store_block(slot, block, 0, dots(normed[:, where], act[slot, :, : 2 * LANES], 0, 0))
-            store_block(
-                slot, block, 2 * LANES, dots(upstream[:, where], act[slot, :, 2 * LANES :], 0, 0)
-            )
-
-        flush(1 - slot)
-        pending[slot] = stage_out(slot, p_f.at[at])
-        pending[slot].start()
-
-    step_rows = 16
-
-    def row_loop(count):
-        return pl.loop(0, count // step_rows)
-
-    def at_rows(base, index):
-        return pl.ds(pl.multiple_of(base + index * step_rows, step_rows), step_rows)
-
-    def reduce_beside(own):
-        def leave(batch):
-            @row_loop(part_rows)
-            def _(index):
-                base = batch * length + (1 - here.t) * part_rows
-                value = own(base, index) + part_in[at_rows(base, index), :].astype(f32)
-                across[at_rows(batch * part_rows, index), :] = value.astype(bf16)
-
-        def keep(batch):
-            @row_loop(part_rows)
-            def _(index):
-                base = batch * length + here.t * part_rows
-                value = own(base, index) + part_in[at_rows(base, index), :].astype(f32)
-                kept[at_rows(batch * part_rows, index), :] = value
-
-        return leave, keep
-
-    loads["normed_ffn"].wait()
-    loads["upstream"].wait()
-    unit_chunk(0)
-    unit_chunk(1)
     loads["part"].wait()
     beside.wait_recv()
     leave, keep = reduce_beside(lambda base, index: part[at_rows(base, index), :].astype(f32))
@@ -923,22 +1201,18 @@
     load_part.start()
 
     for head in range(heads):
-        slot = head % 2
-        if head + 1 < heads:
-            for copy in head_loads[head + 1]:
-                copy.start()
         for copy in head_loads[head]:
             copy.wait()
 
         @pl.loop(0, rows // length)
         def _(sequence):
             where = pl.ds(pl.multiple_of(sequence * length, length), length)
-            query_pre = saved[slot, where, 0:LANES]
-            key_pre = saved[slot, where, LANES : 2 * LANES]
-            gate = saved[slot, where, 2 * LANES : 3 * LANES]
+            query_pre = saved[0, where, 0:LANES]
+            key_pre = saved[0, where, LANES : 2 * LANES]
+            gate = saved[0, where, 2 * LANES : 3 * LANES]
             scale = inverse[where, :]
-            unit = saved[slot, where, 3 * LANES : 4 * LANES] * scale
-            grad_branch = dots(grad_out[where, :], weights[slot, :, 4 * LANES :], 1, 0)
+            unit = saved[0, where, 3 * LANES : 4 * LANES] * scale
+            grad_branch = dots(grad_out[where, :], weights[0, :, 4 * LANES :], 1, 0)
             grad_unit = grad_branch * gate
             branch[where, :] = (unit * gate).astype(bf16)
             projected[where, 3 * LANES :] = (grad_branch * unit).astype(bf16)
@@ -950,7 +1224,7 @@
             masked = table[head] * same[sequence]
             mixing = (dots(queries, keys, 1, 1) * masked).astype(bf16)
             grad_scores = (
-                dots(grad_mixed, values[slot, where, :], 1, 1) * masked
+                dots(grad_mixed, values[0, where, :], 1, 1) * masked
             ).astype(bf16)
             grad_queries = dots(grad_scores, keys, 1, 0)
             grad_keys = dots(grad_scores, queries, 0, 0)
@@ -961,12 +1235,15 @@
                 grad_keys * (key_gate * (1.0 + key_pre * (1.0 - key_gate)))
             ).astype(bf16)
             projected[where, 2 * LANES : 3 * LANES] = dots(mixing, grad_mixed, 0, 0).astype(bf16)
-            product = dots(projected[where, :], weights[slot, :, : 4 * LANES], 1, 1)
+            product = dots(projected[where, :], weights[0, :, : 4 * LANES], 1, 1)
             if head == 0:
                 total[where, :] = product
             else:
                 total[where, :] += product
 
+        if head + 1 < heads:
+            for copy in head_loads[head + 1]:
+                copy.start()
         flush(0)
         flush(1)
         reducer.tick()
@@ -979,10 +1256,8 @@
             store_block(1, block, 0, product[:, 3 * LANES :])
             store_block(1, block, LANES, dots(grad_out[:, where], branch[...], 0, 0))
 
-        pending[0] = stage_out(0, p_qkv.at[head])
-        pending[1] = stage_out(1, p_go.at[head])
-        pending[0].start()
-        pending[1].start()
+        send_stage(0, p_qkv, 1, head)
+        send_stage(1, p_go, 2, head)
         if head == heads - 1:
             beside.wait_send()
 
@@ -1069,8 +1344,7 @@
         value += dots(columns[1, :, where].astype(bf16), second, 0, 0)
         store_block(0, block, 0, value)
 
-    pending[0] = stage_out(0, p_gain.at[0])
-    pending[0].start()
+    send_stage(0, p_gain, 3, 0)
     flush(0)
     reducer.drain()
     gain_sum = chunks[-1].out_slot[0] + chunks[-1].out_slot[1]
@@ -1116,12 +1390,18 @@
         shape((count, mids - 1, LAYERS, CORES, block_rows, wide), bf16) for count, wide in widths
     ]
     land = [shape((count, CORES, LAYERS, block_rows, wide), bf16) for count, wide in widths]
+    few = max(len(CLIMBS), 1)
+    side = [
+        shape((few, LAYERS, mids, CORES, block_rows, widest), bf16),
+        shape((few, CORES, mids, block_rows, widest), bf16),
+        shape((few, mids, CORES, block_rows, widest), bf16),
+    ]
     return pl.pallas_call(
         functools.partial(backward_kernel, mids),
         name="backward",
-        out_shape=(*outs, shape((own, width), f32), shape((own, width), bf16), *sums, *cross, *land, *passed),
+        out_shape=(*outs, shape((own, width), f32), shape((own, width), bf16), *sums, *cross, *land, *passed, *side),
         in_specs=[smem] + [vmem] * 6 + [anywhere] * 10,
-        out_specs=(anywhere,) * 8 + (vmem,) * 2 + (anywhere,) * 17,
+        out_specs=(anywhere,) * 8 + (vmem,) * 2 + (anywhere,) * 20,
         scratch_shapes=[
             pltpu.VMEM((rows, width), bf16),
             pltpu.VMEM((rows, width), bf16),
@@ -1136,9 +1416,15 @@
             pltpu.VMEM((2, CORES, LANES, block_rows), f32),
             pltpu.VMEM((CORES, block_rows, widest), bf16),
             pltpu.VMEM((2, block_rows, LANES), f32),
-            pltpu.VMEM((2, rows, 4 * LANES), f32),
-            pltpu.VMEM((2, rows, LANES), bf16),
-            pltpu.VMEM((2, width, 5 * LANES), bf16),
+            pltpu.VMEM((mids, CORES, block_rows, widest), bf16),
+            pltpu.VMEM((LAYERS, mids, CORES, block_rows, widest), bf16),
+            pltpu.VMEM((mids, CORES, block_rows, widest), bf16),
+            pltpu.VMEM((CORES, mids, block_rows, widest), bf16),
+            pltpu.VMEM((mids, CORES, block_rows, widest), bf16),
+            pltpu.VMEM((mids, CORES, block_rows, widest), bf16),
+            pltpu.VMEM((1, rows, 4 * LANES), f32),
+            pltpu.VMEM((1, rows, LANES), bf16),
+            pltpu.VMEM((1, width, 5 * LANES), bf16),
             pltpu.VMEM((rows, 4 * LANES), bf16),
             pltpu.VMEM((rows, LANES), bf16),
             pltpu.VMEM((rows, width), f32),
@@ -1154,7 +1440,7 @@
             pltpu.VMEM((2, 8, width), f32),
             pltpu.SemaphoreType.DMA((chunks, hops)),
             pltpu.SemaphoreType.DMA((chunks, hops)),
-            pltpu.SemaphoreType.DMA((chunks, 11)),
+            pltpu.SemaphoreType.DMA((chunks, 12)),
             pltpu.SemaphoreType.DMA((22,)),
             pltpu.SemaphoreType.DMA((22,)),
             pltpu.SemaphoreType.DMA((15,)),

time: 739 us -> 726 us (0.982)
  Pallas kernels: 706 us -> 693 us
    pallas_call x1, Pallas kernels: 365 us -> 353 us  [backward(): pl.pallas_call(functools.partial(backward_kernel, mids), name='backward',...]
    unnamed x45 -> x47, local copies, waits for them, and re-layouts: 16 us -> 15.7 us
where the time goes in v5:
time: 726 us; the launch traced here: 721 us
  Pallas kernels  693 us (95%)
  local copies, waits for them, and re-layouts  20.5 us (3%)
    pallas_call x1, Pallas kernels, backward(): pl.pallas_call(functools.partial(backward_kernel, mids), name='backward',...  353 us
    pallas_call x1, Pallas kernels, forward(): pl.pallas_call(functools.partial(forward_kernel, mids), name='forward', o...  341 us
    unnamed x47, local copies, waits for them, and re-layouts  15.7 us

profile of v5, /device:TPU:0, one launch (start us, length us, event | category | flops | bytes accessed | tf_op | source)
XLA Modules:
  0.0 720.6 jit_solution(13188499844481353517)
XLA Ops:
  0.6 0.0 copy-start.12
  0.7 1.3 dynamic_slice.3.refs_0_
  1.9 0.7 pad_maximum_fusion
  2.6 0.7 copy.59
  3.3 0.1 copy.44
  3.5 0.6 maximum_bitcast_fusion.3.refs_4_
  4.1 0.8 fusion.refs_1_
  4.9 1.1 copy.48
  6.0 0.0 copy-start.13
  6.0 0.2 copy.51
  6.2 1.1 copy.49
  7.3 0.0 copy-start.14
  7.3 0.2 copy.52
  7.5 0.0 copy-done.12
  7.5 0.2 copy.50
  7.7 0.2 copy.53
  7.9 0.0 copy-start.4
  7.9 1.0 maximum_bitcast_fusion.1.refs_6_
  8.9 0.0 copy-done.13
  8.9 0.2 copy.45
  9.1 0.2 copy.46
  9.3 0.0 copy-done.14
  9.3 0.0 copy-start.5
  9.3 0.2 copy.47
  9.5 0.9 maximum_bitcast_fusion.2.refs_5_
  10.3 0.0 copy-done.4
  10.3 0.3 copy.54
  10.7 0.0 copy-start.6
  10.7 0.4 copy.56
  11.1 0.0 copy-done.5
  11.1 0.3 copy.55
  11.4 0.4 copy.57
  11.8 0.0 copy-done.6
  11.8 0.4 copy.58
  12.2 1.7 maximum_bitcast_fusion.refs_7_
  13.9 340.6 %forward.1 = (bf16[1,4,2,2,128,128]{5,4,3,2,1,0:T(8,128)(2,1)}, bf16[4,4,2,2,128,256]{5,4,3,2,1,0:T(8,128)(2,1)}, bf16[4,4,2,2,128,384]{5,4,3,2,1,0:T(8,128)(2,1...) custom-call(f32[4]{0:T(128)} %dynamic_slice.3.refs_0_, ...), custom_call_target="tpu_custom_call" | custom-call | tf_op jit(solution)/shard_map/forward/pallas_call | solution.py:1876
  354.5 352.6 %backward.1 = (f32[128,1024]{1,0:T(8,128)}, f32[128,1024]{1,0:T(8,128)}, f32[128,1024]{1,0:T(8,128)}, f32[128,1024]{1,0:T(8,128)}, f32[1024,128]{1,0:T(8,128)}, ...) custom-call(f32[4]{0:T(128)} %dynamic_slice.3.refs_0_, ...), custom_call_target="tpu_custom_call" | custom-call | tf_op jit(solution)/shard_map/backward/pallas_call | solution.py:1399
  707.1 0.0 copy-start
  707.1 1.4 slice_bitcast_fusion
  708.5 2.3 copy.70
  710.8 0.0 copy-done
  710.8 0.0 copy-start.11
  710.8 0.0 copy-start.10
  710.8 0.0 copy-start.9
  710.8 1.3 copy.71
  712.1 0.0 copy-done.11
  712.1 0.0 copy-start.8
  712.1 0.0 copy-start.7
  712.1 0.8 copy.72
  712.9 0.0 copy-done.10
  712.9 0.0 copy-start.3
  712.9 0.8 copy.73
  713.7 0.0 copy-done.9
  713.7 0.8 copy.74
  714.5 0.0 copy-done.8
  714.5 0.8 copy.75
  715.3 0.0 copy-done.7
  715.3 0.8 copy.76
  716.1 0.0 copy-done.3
  716.1 1.1 copy.77
  717.2 0.0 copy-done.2
  717.2 1.1 copy.78
  718.3 0.8 copy-done.1
  719.1 1.1 copy.79
  (3 shorter events, 0.0 us)
Async XLA Ops:
  0.6 6.9 copy-start.12
  6.0 2.9 copy-start.13
  7.3 1.9 copy-start.14
  7.9 2.4 copy-start.4
  9.3 1.8 copy-start.5
  10.7 1.1 copy-start.6
  707.1 3.7 copy-start
  710.8 1.4 copy-start.11
  710.8 2.2 copy-start.10
  710.8 3.0 copy-start.9
  712.1 2.4 copy-start.8
  712.1 3.2 copy-start.7
  712.9 3.2 copy-start.3
  715.3 1.9 copy-start.2
  717.2 1.9 copy-start.1

commit v6 on v5

--- a/solution.py
+++ b/solution.py
@@ -928,7 +928,6 @@
     here = Place(mids)
     sibling = here.device(here.z, here.m, 1 - here.k)
     other = (here.device(here.z, here.m, here.k)[0], 1 - here.t)
-    greet(here.weight_peers() + [other])
 
     chunks = []
     lists = []
@@ -1031,6 +1030,7 @@
     acts[0].start()
     loads["upstream"].start()
     loads["part"].start()
+    greet(here.weight_peers() + [other])
 
     def swap_beside(source, at):
         return remote(source, part_in, row_send.at[12 + at], row_receive.at[12 + at], sibling)

time: 726 us -> 723 us (level)
  no operation moved by 1% of the time
where the time goes in v6:
time: 723 us; the launch traced here: 717 us
  Pallas kernels  690 us (95%)
  local copies, waits for them, and re-layouts  20.5 us (3%)
    pallas_call x1, Pallas kernels, backward(): pl.pallas_call(functools.partial(backward_kernel, mids), name='backward',...  349 us
    pallas_call x1, Pallas kernels, forward(): pl.pallas_call(functools.partial(forward_kernel, mids), name='forward', o...  341 us
    unnamed x47, local copies, waits for them, and re-layouts  15.7 us

profile of v6, /device:TPU:0, one launch (start us, length us, event | category | flops | bytes accessed | tf_op | source)
XLA Modules:
  0.0 717.4 jit_solution(17926669384050498823)
XLA Ops:
  0.6 0.0 copy-start.12
  0.7 1.3 dynamic_slice.3.refs_0_
  1.9 0.7 pad_maximum_fusion
  2.6 0.7 copy.59
  3.3 0.1 copy.44
  3.5 0.6 maximum_bitcast_fusion.3.refs_4_
  4.1 0.8 fusion.refs_1_
  4.9 1.1 copy.48
  6.0 0.0 copy-start.13
  6.0 0.2 copy.51
  6.2 1.1 copy.49
  7.3 0.0 copy-start.14
  7.3 0.2 copy.52
  7.5 0.0 copy-done.12
  7.5 0.2 copy.50
  7.7 0.2 copy.53
  7.9 0.0 copy-start.4
  7.9 1.0 maximum_bitcast_fusion.1.refs_6_
  8.9 0.0 copy-done.13
  8.9 0.2 copy.45
  9.1 0.2 copy.46
  9.3 0.0 copy-done.14
  9.3 0.0 copy-start.5
  9.3 0.2 copy.47
  9.5 0.9 maximum_bitcast_fusion.2.refs_5_
  10.3 0.0 copy-done.4
  10.3 0.3 copy.54
  10.7 0.0 copy-start.6
  10.7 0.4 copy.56
  11.1 0.0 copy-done.5
  11.1 0.3 copy.55
  11.4 0.4 copy.57
  11.8 0.0 copy-done.6
  11.8 0.4 copy.58
  12.2 1.7 maximum_bitcast_fusion.refs_7_
  13.9 340.6 %forward.1 = (bf16[1,4,2,2,128,128]{5,4,3,2,1,0:T(8,128)(2,1)}, bf16[4,4,2,2,128,256]{5,4,3,2,1,0:T(8,128)(2,1)}, bf16[4,4,2,2,128,384]{5,4,3,2,1,0:T(8,128)(2,1...) custom-call(f32[4]{0:T(128)} %dynamic_slice.3.refs_0_, ...), custom_call_target="tpu_custom_call" | custom-call | tf_op jit(solution)/shard_map/forward/pallas_call | solution.py:1876
  354.5 349.4 %backward.1 = (f32[128,1024]{1,0:T(8,128)}, f32[128,1024]{1,0:T(8,128)}, f32[128,1024]{1,0:T(8,128)}, f32[128,1024]{1,0:T(8,128)}, f32[1024,128]{1,0:T(8,128)}, ...) custom-call(f32[4]{0:T(128)} %dynamic_slice.3.refs_0_, ...), custom_call_target="tpu_custom_call" | custom-call | tf_op jit(solution)/shard_map/backward/pallas_call | solution.py:1399
  703.8 0.0 copy-start
  703.8 1.4 slice_bitcast_fusion
  705.2 2.3 copy.70
  707.5 0.0 copy-done
  707.5 0.0 copy-start.11
  707.5 0.0 copy-start.10
  707.5 0.0 copy-start.9
  707.5 1.3 copy.71
  708.8 0.0 copy-done.11
  708.9 0.0 copy-start.8
  708.9 0.0 copy-start.7
  708.9 0.8 copy.72
  709.7 0.0 copy-done.10
  709.7 0.0 copy-start.3
  709.7 0.8 copy.73
  710.5 0.0 copy-done.9
  710.5 0.8 copy.74
  711.3 0.0 copy-done.8
  711.3 0.8 copy.75
  712.1 0.0 copy-done.7
  712.1 0.8 copy.76
  712.9 0.0 copy-done.3
  712.9 1.1 copy.77
  714.0 0.0 copy-done.2
  714.0 1.1 copy.78
  715.1 0.8 copy-done.1
  715.9 1.1 copy.79
  (3 shorter events, 0.0 us)
Async XLA Ops:
  0.6 6.9 copy-start.12
  6.0 2.9 copy-start.13
  7.3 1.9 copy-start.14
  7.9 2.4 copy-start.4
  9.3 1.8 copy-start.5
  10.7 1.1 copy-start.6
  703.8 3.7 copy-start
  707.5 1.4 copy-start.11
  707.5 2.2 copy-start.10
  707.5 3.0 copy-start.9
  708.9 2.4 copy-start.8
  708.9 3.2 copy-start.7
  709.7 3.2 copy-start.3
  712.1 1.9 copy-start.2
  714.0 1.9 copy-start.1
